TPU v7x, 32 devices: a whole 2x2x4 slice. The times are simulated.
32 devices in a mesh: patch: 2 (over y), space: 4 (over z), tm: 2 (over x), row: 2 (over core).
Axes of the slice: x: 2, y: 2, z: 4, core: 2. Of those that a mesh axis runs over, the one named last changes fastest.
Arguments:
- doppler: float32 [32, 192, 256], P('tm', ('patch', 'space'), 'row'), parts along dimension 1, may hold values from -24 to 24
- cycle_masks: int32 [8, 33, 33], replicated, may hold values from 0 to 1, as said below
- lag_list: int32 [4], replicated, may hold values from 1 to 16, as said below
Outputs:
- correlations: float32 [2, 8, 4, 192, 256], P('tm', None, None, ('patch', 'space'), 'row'), parts along dimension 3
There are 2 independent parts, one for each index of `patch`. A program takes and returns all parts, laid end to end along the dimension named above; an argument that names none is the same for every part. Nothing has to cross between parts.
Inputs may be any that keep to these rules, and one draw needn't show every extreme that they name: Each cycle_masks[r] is 1 only at offsets whose distance from the centre lies within half a pixel of one radius of 1 to 16, distinct radii over r, and is 1 at the offsets of that radius along both pixel directions; one annulus has radius 16. `lag_list`: the lags are distinct and one of them is 16.
All inputs are finite; a program needn't handle non-finite values.
Results may differ from a plain program's by a relative error of at most 0.0033.
Values may be sent and summed in bfloat16 or wider, within the bound.
No kernel may reach another device: no remote copies, remote signals or barrier semaphores. Data moves between devices by JAX's collectives and lax.ppermute only.
A program may use at most 64 MiB of HBM per device.

v0:
```python
import jax
import jax.numpy as jnp
from jax import lax
from jax.experimental import pallas as pl
from jax.experimental.pallas import tpu as pltpu
from jax.sharding import PartitionSpec as P

RMAX = 16
MAXLAG = 16
TILE = 32

gaussian_taps = (0.05448868, 0.24420134, 0.40261995, 0.24420134, 0.05448868)
REACH = len(gaussian_taps) // 2
LANES = 128
VMEM = pltpu.VMEM


def pairs(count, first):
    partner = list(range(count))
    for low in range(first, count - 1, 2):
        partner[low], partner[low + 1] = low + 1, low
    return [(source, target) for source, target in enumerate(partner)]


def onward(count):
    return [(source, (source + 1) % count) for source in range(count)]


def vmem_call(body, out_shape, scratch=(), smem=0, inputs=1, cost=None):
    specs = [pl.BlockSpec(memory_space=pltpu.SMEM)] * smem + [pl.BlockSpec(memory_space=VMEM)] * inputs
    many = isinstance(out_shape, (list, tuple))
    out_specs = [pl.BlockSpec(memory_space=VMEM)] * len(out_shape) if many else pl.BlockSpec(memory_space=VMEM)
    return pl.pallas_call(
        body,
        out_shape=out_shape,
        in_specs=specs,
        out_specs=out_specs,
        scratch_shapes=list(scratch),
        compiler_params=pltpu.CompilerParams(vmem_limit_bytes=24 * 1024 * 1024),
        cost_estimate=cost,
    )


def blend(parts):
    a, b, c, _, _ = gaussian_taps
    return c * parts[2] + b * (parts[1] + parts[3]) + a * (parts[0] + parts[4])


def table_body(flat_ref, table_ref, inverse_ref):
    radii, width = flat_ref.shape
    for r in range(radii):
        row = flat_ref[r : r + 1, :]
        total = jnp.sum(row, axis=1, keepdims=True)
        inverse_ref[r : r + 1, :] = jnp.broadcast_to(1.0 / total, (1, LANES))
        for k in range(width // LANES):
            wide = jnp.broadcast_to(row[:, k * LANES : (k + 1) * LANES], (TILE, LANES))
            turned = pltpu.roll(wide, 0, 1, stride=1, stride_axis=0)
            table_ref[r * TILE : (r + 1) * TILE, k * LANES : (k + 1) * LANES] = turned.astype(jnp.bfloat16)


def columns_body(frames, cols, x_ref, a_ref, b_ref, out_ref):
    place, count = lax.axis_index("space"), lax.axis_size("space")
    even = lax.rem(place, 2) == 0
    lowest, highest = place > 0, place < count - 1
    halo = RMAX + REACH

    def raw(c):
        if 0 <= c < cols:
            return x_ref[pl.ds(c, frames, stride=cols), :]
        at = c + cols if c < 0 else c - cols
        rows = pl.ds(at, frames, stride=cols)
        first, second, there = (b_ref, a_ref, lowest) if c < 0 else (a_ref, b_ref, highest)
        value = jnp.where(even, first[rows, :], second[rows, :])
        return jnp.where(there, value, jnp.zeros_like(value))

    held = {}
    for c in range(-halo, cols + halo):
        held[c] = raw(c)
        done = c - REACH
        if done >= -RMAX:
            out_ref[done + RMAX] = blend([held[done + k] for k in range(-REACH, REACH + 1)])


def rows_body(frames, cols, own_ref, low_ref, high_ref, tiles_ref, smooth_ref, turn_ref):
    place, count = lax.axis_index("row"), lax.axis_size("row")
    column, columns = lax.axis_index("space"), lax.axis_size("space")
    wide = cols + 2 * RMAX
    lane = lax.broadcasted_iota(jnp.int32, (frames, LANES), 1)
    halo = RMAX + REACH
    left = jnp.logical_and(lane >= LANES - halo, place > 0)
    right = jnp.logical_and(lane < halo, place < count - 1)
    left_kept = jnp.logical_and(lane >= LANES - RMAX, place > 0)
    right_kept = jnp.logical_and(lane < RMAX, place < count - 1)

    def around(near, far, k):
        if k == 0:
            return near
        near, far = pltpu.roll(near, (-k) % LANES, 1), pltpu.roll(far, (-k) % LANES, 1)
        return jnp.where(lane >= LANES - k if k > 0 else lane < -k, far, near)

    def smooth_of(c):
        own = own_ref[c]
        side = jnp.where(left, low_ref[c], jnp.where(right, high_ref[c], 0.0))
        shifts = range(-REACH, REACH + 1)
        main = blend([around(own, side, k) for k in shifts])
        edge = blend([around(side, own, k) for k in shifts])
        edge = jnp.where(jnp.logical_or(left_kept, right_kept), edge, 0.0)
        if c < RMAX or c >= RMAX + cols:
            inside = column > 0 if c < RMAX else column < columns - 1
            main, edge = jnp.where(inside, main, 0.0), jnp.where(inside, edge, 0.0)
        return main, edge

    tile_count = LANES // TILE
    first_half = lane < 2 * TILE

    def windows(c):
        main, edge = smooth_of(c)
        if RMAX <= c < RMAX + cols:
            turn_ref[(c - RMAX) * frames : (c - RMAX + 1) * frames, :] = main
        out = []
        for j in range(tile_count):
            start = TILE * j - RMAX
            source = main
            if start < 0:
                source = jnp.where(lane >= LANES + start, edge, main)
            if start + 2 * TILE > LANES:
                source = jnp.where(lane < start + 2 * TILE - LANES, edge, source)
            out.append((pltpu.roll(source, (-start) % LANES, 1), pltpu.roll(source, (2 * TILE - start) % LANES, 1)))
        return out

    before = windows(0)
    for c in range(wide):
        after = windows(c + 1) if c + 1 < wide else [(jnp.zeros((frames, LANES), jnp.float32),) * 2] * tile_count
        for j in range(tile_count):
            tiles_ref[j, c] = jnp.where(first_half, before[j][0], after[j][1]).astype(jnp.bfloat16)
        before = after
    for t in range(frames):
        smooth_ref[t] = turn_ref[pl.ds(t, cols, stride=frames), :].astype(jnp.bfloat16)


def sums_body(frames, cols, table_ref, tiles_ref, out_ref):
    tile_count = tiles_ref.shape[0]
    offsets = 2 * RMAX + 1
    rows = cols * frames
    for j in range(tile_count):
        pieces = []
        for a in range(0, offsets, 2):
            pieces.append(tiles_ref[j, a : a + cols].reshape(rows, LANES))
        stacked = jnp.concatenate(pieces, axis=1)
        found = lax.dot_general(
            stacked, table_ref[...], (((1,), (1,)), ((), ())), preferred_element_type=jnp.float32
        )
        for g in range(out_ref.shape[1]):
            out_ref[j, g] = found[:, g * LANES : (g + 1) * LANES]


def correlate_body(frames, cols, radii, lag_ref, sums_ref, own_ref, earlier_ref, inverse_ref, out_ref, spread_ref):
    lag_count = lag_ref.shape[0]
    tile_count = LANES // TILE
    wide = tile_count * LANES
    here = lax.broadcasted_iota(jnp.int32, (LANES, wide), 0)
    there = lax.broadcasted_iota(jnp.int32, (LANES, wide), 1)
    wanted = (there // LANES) * TILE + there % TILE
    pick = jnp.where(here == wanted, 1.0, 0.0).astype(jnp.bfloat16)
    begun = lax.axis_index("tm") > 0
    for half, source in enumerate((earlier_ref, own_ref)):
        value = jnp.dot(source[...], pick, preferred_element_type=jnp.float32)
        if half == 0:
            value = jnp.where(begun, value, 0.0)
        spread_ref[half * frames * cols : (half + 1) * frames * cols, :] = value
    lane = lax.broadcasted_iota(jnp.int32, (8, LANES), 1)
    block = [jnp.logical_and(lane >= TILE * j, lane < TILE * (j + 1)) for j in range(tile_count)]
    groups = radii * TILE // LANES
    per = LANES // TILE
    for c in range(0, cols, 8):
        totals = {}
        for j in range(tile_count):
            for t in range(frames):
                parts = [
                    sums_ref[j, g, pl.ds(c * frames + t, 8, stride=frames), :]
                    for g in range(groups)
                ]
                for lag in range(lag_count):
                    row = (MAXLAG + t - lag_ref[lag]) * cols + c
                    old = spread_ref[pl.ds(pl.multiple_of(row, 8), 8), j * LANES : (j + 1) * LANES]
                    for g in range(groups):
                        term = parts[g] * old
                        key = (lag, g, j)
                        totals[key] = totals[key] + term if key in totals else term
        for lag in range(lag_count):
            for g in range(groups):
                for q in range(per):
                    joined = None
                    for j in range(tile_count):
                        piece = totals[(lag, g, j)]
                        shift = (TILE * (j - q)) % LANES
                        piece = pltpu.roll(piece, shift, 1) if shift else piece
                        joined = piece if joined is None else jnp.where(block[j], piece, joined)
                    r = g * per + q
                    out_ref[r, lag, c : c + 8, :] = joined * inverse_ref[r : r + 1, :]


def local(doppler, cycle_masks, lag_list):
    frames, cols, rows = doppler.shape
    radii = cycle_masks.shape[0]
    lag_count = lag_list.shape[0]
    wide = cols + 2 * RMAX
    offsets = 2 * RMAX + 1
    tile_count = rows // TILE
    f32, bf16 = jnp.float32, jnp.bfloat16
    shape = jax.ShapeDtypeStruct

    flat = doppler.reshape(frames * cols, rows)
    count = lax.axis_size("space")
    one = lax.ppermute(flat, "space", pairs(count, 0))
    two = lax.ppermute(flat, "space", pairs(count, 1))

    kept = offsets + 1
    masks = jnp.pad(cycle_masks.astype(f32), ((0, 0), (0, kept - offsets), (0, 2 * TILE - offsets)))
    masks = masks.reshape(radii, kept * 2 * TILE)
    table, inverse = vmem_call(
        table_body, [shape((radii * TILE, kept * 2 * TILE), bf16), shape((radii, LANES), f32)]
    )(masks)

    def columns(*refs):
        columns_body(frames, cols, *refs)

    blurred = vmem_call(columns, shape((wide, frames, rows), f32), inputs=3)(flat, one, two)

    row_count = lax.axis_size("row")
    ring = onward(row_count)
    low = lax.ppermute(blurred, "row", ring)
    high = low if row_count == 2 else lax.ppermute(blurred, "row", [(b, a) for a, b in ring])

    def along(*refs):
        rows_body(frames, cols, *refs)

    tiles, smooth = vmem_call(
        along,
        [shape((tile_count, wide, frames, LANES), bf16), shape((frames, cols, rows), bf16)],
        scratch=[VMEM((cols * frames, LANES), f32)],
        inputs=3,
    )(blurred, low, high)

    smooth = smooth.reshape(frames * cols, rows)
    earlier = lax.ppermute(smooth, "tm", onward(lax.axis_size("tm")))

    def products(*refs):
        sums_body(frames, cols, *refs)

    flops = 2 * tile_count * cols * frames * radii * TILE * kept * 2 * TILE
    sums = vmem_call(
        products,
        shape((tile_count, radii * TILE // LANES, cols * frames, LANES), f32),
        inputs=2,
        cost=pl.CostEstimate(flops=flops, bytes_accessed=1 << 20, transcendentals=0),
    )(table, tiles)

    def correlate(*refs):
        correlate_body(frames, cols, radii, *refs)

    out = vmem_call(
        correlate,
        shape((radii, lag_count, cols, rows), f32),
        scratch=[VMEM((2 * frames * cols, tile_count * LANES), f32)],
        smem=1,
        inputs=4,
    )(lag_list, sums, smooth, earlier, inverse)
    return out[None]


def solution(mesh):
    return jax.shard_map(
        local,
        mesh=mesh,
        in_specs=(P("tm", ("patch", "space"), "row"), P(), P()),
        out_specs=P("tm", None, None, ("patch", "space"), "row"),
        check_vma=False,
    )
```

profile of v0, /device:TPU:20, one launch (start us, length us, event | category | flops | bytes accessed | tf_op | source)
XLA Modules:
  0.0 26.0 jit_solution(3198710558833180342)
XLA Ops:
  0.0 1.6 %collective-permute-start = (f32[384,128]{1,0:T(8,128)}, f32[384,128]{1,0:T(8,128)S(1)}, u32[]{:S(2)}, u32[]{:S(2)}) collective-permute-start(f32[384,128]{1,0:T(8,128)} %bitcast.3), channel_id=1, source_target_pairs={{0,4},{4,0},{8,12},{12,8},{1,5},{5,1},{9,13},{13,9},{2,6},{6,2},{1... | collective-permute-start | bytes 589832 | tf_op jit(solution)/shard_map/ppermute | solution.py:215
  1.6 1.9 %collective-permute-start.1 = (f32[384,128]{1,0:T(8,128)}, f32[384,128]{1,0:T(8,128)S(1)}, u32[]{:S(2)}, u32[]{:S(2)}) collective-permute-start(f32[384,128]{1,0:T(8,128)} %bitcast.4), channel_id=1, source_target_pairs={{0,0},{4,8},{8,4},{12,12},{1,1},{5,9},{9,5},{13,13},{2,2},{6,10},{... | collective-permute-start | bytes 589832 | tf_op jit(solution)/shard_map/ppermute | solution.py:216
  3.5 3.4 %collective-permute-done.refs_1_ = f32[384,128]{1,0:T(8,128)S(1)} collective-permute-done((f32[384,128]{1,0:T(8,128)}, f32[384,128]{1,0:T(8,128)S(1)}, u32[]{:S(2)}, u32[]{:S(2)}) %collective-permute-start) | collective-permute-done | bytes 196640 | tf_op jit(solution)/shard_map/ppermute | solution.py:215
  6.9 3.2 %collective-permute-done.1.refs_2_ = f32[384,128]{1,0:T(8,128)S(1)} collective-permute-done((f32[384,128]{1,0:T(8,128)}, f32[384,128]{1,0:T(8,128)S(1)}, u32[]{:S(2)}, u32[]{:S(2)}) %collective-permute-start.1) | collective-permute-done | bytes 196640 | tf_op jit(solution)/shard_map/ppermute | solution.py:216
  10.0 0.0 copy-start
  10.0 0.9 %copy-done = f32[16,24,128]{2,1,0:T(8,128)S(1)} copy-done((f32[16,24,128]{2,1,0:T(8,128)S(1)}, f32[16,24,128]{2,1,0:T(8,128)}, u32[]{:S(2)}) %copy-start) | copy-done | bytes 196632
  11.0 0.2 shard_map.38.refs_0_
  11.2 0.1 collective-permute-start.2
  11.2 0.9 %convert_element_type.5 = f32[8,33,33]{2,0,1:T(8,128)S(1)} convert(s32[8,33,33]{2,0,1:T(8,128)} %param.4) | non-fusion elementwise | flops 8712 | bytes 69696 | tf_op jit(solution)/shard_map/convert_element_type | solution.py:219
  12.2 0.1 reshape.9.flat_ref
  12.3 0.5 %shard_map.37 = (bf16[256,2176]{1,0:T(8,128)(2,1)S(1)}, f32[8,128]{1,0:T(8,128)S(1)}) custom-call(f32[8,2176]{1,0:T(8,128)S(1)} %reshape.9.flat_ref), custom_call_target="tpu_custom_call" | custom-call | tf_op jit(solution)/shard_map/pallas_call | solution.py:221
  12.8 0.3 collective-permute-done.2.refs_1_.refs_2_
  13.0 5.3 %shard_map.39 = (bf16[4,56,16,128]{3,2,1,0:T(8,128)(2,1)S(1)}, bf16[16,24,128]{2,1,0:T(8,128)(2,1)S(1)}) custom-call(f32[56,16,128]{2,1,0:T(8,128)S(1)} %shard_map.38.refs_0_, f32[56,16,128]{2,1,0:T(8,128)S(1)} %collective-permute-done.2.refs_1_.refs_2_, f32[56,16,128]{2,1,0:T(8,128)S(1)} %collective-permute-done.2.refs_1_.refs_2_), custom_call_target="tpu_custom_call" | custom-call | tf_op jit(solution)/shard_map/pallas_call | solution.py:238
  18.3 1.6 %collective-permute-start.3 = (bf16[384,128]{1,0:T(8,128)(2,1)S(1)}, bf16[384,128]{1,0:T(8,128)(2,1)S(1)}, u32[]{:S(2)}, u32[]{:S(2)}) collective-permute-start(bf16[384,128]{1,0:T(8,128)(2,1)S(1)} %bitcast.6), channel_id=1, source_target_pairs={{0,2},{2,0},{1,3},{3,1},{4,6},{6,4},{5,7},{7,5},{8,10},{10,8},{9,1... | collective-permute-start | bytes 294920 | tf_op jit(solution)/shard_map/ppermute | solution.py:246
  19.9 0.0 copy-start.1
  19.9 2.0 %shard_map.40.refs_1_ = f32[4,2,384,128]{3,2,1,0:T(8,128)S(1)} custom-call(bf16[256,2176]{1,0:T(8,128)(2,1)S(1)} %get-tuple-element.9.refs_0_, bf16[4,56,16,128]{3,2,1,0:T(8,128)(2,1)S(1)} %get-tuple-element.10.refs_1_), custom_call_target="tpu_custom_call" | custom-call | flops 1711276032 | bytes 1048576 | tf_op jit(solution)/shard_map/pallas_call | solution.py:252
  21.9 1.4 %collective-permute-done.3.refs_3_ = bf16[384,128]{1,0:T(8,128)(2,1)S(1)} collective-permute-done((bf16[384,128]{1,0:T(8,128)(2,1)S(1)}, bf16[384,128]{1,0:T(8,128)(2,1)S(1)}, u32[]{:S(2)}, u32[]{:S(2)}) %collective-permute-start.3) | collective-permute-done | bytes 98336 | tf_op jit(solution)/shard_map/ppermute | solution.py:246
  23.3 0.0 copy-done.1
  23.3 2.7 %shard_map.41 = f32[8,4,24,128]{3,2,1,0:T(8,128)} custom-call(s32[4]{0:T(128)S(1)} %copy-done.1, f32[4,2,384,128]{3,2,1,0:T(8,128)S(1)} %shard_map.40.refs_1_, bf16[384,128]{1,0:T(8,128)(2,1)S(1)} %bitcast.7, bf16[384,128]{1,0:T(8,128)(2,1)S(1)} %collective-permute-done.3.refs_3_, f32[8,128]{1,0:T(8,128)S(1)} %get-tuple-element.12.refs_4_), custom_call_target="tpu_custom_call" | custom-call | tf_op jit(solution)/shard_map/pallas_call | solution.py:262
  (2 shorter events, 0.0 us)
Async XLA Ops:
  0.0 6.9 %collective-permute-start = (f32[384,128]{1,0:T(8,128)}, f32[384,128]{1,0:T(8,128)S(1)}, u32[]{:S(2)}, u32[]{:S(2)}) collective-permute-start(f32[384,128]{1,0:T(8,128)} %bitcast.3), channel_id=1, source_target_pairs={{0,4},{4,0},{8,12},{12,8},{1,5},{5,1},{9,13},{13,9},{2,6},{6,2},{1... | collective-permute-start | bytes 589832 | tf_op jit(solution)/shard_map/ppermute | solution.py:215
  1.6 8.5 %collective-permute-start.1 = (f32[384,128]{1,0:T(8,128)}, f32[384,128]{1,0:T(8,128)S(1)}, u32[]{:S(2)}, u32[]{:S(2)}) collective-permute-start(f32[384,128]{1,0:T(8,128)} %bitcast.4), channel_id=1, source_target_pairs={{0,0},{4,8},{8,4},{12,12},{1,1},{5,9},{9,5},{13,13},{2,2},{6,10},{... | collective-permute-start | bytes 589832 | tf_op jit(solution)/shard_map/ppermute | solution.py:216
  10.0 0.9 %copy-start = (f32[16,24,128]{2,1,0:T(8,128)S(1)}, f32[16,24,128]{2,1,0:T(8,128)}, u32[]{:S(2)}) copy-start(f32[16,24,128]{2,1,0:T(8,128)} %param.3) | copy-start | bytes 589828
  11.2 1.9 %collective-permute-start.2 = (f32[56,16,128]{2,1,0:T(8,128)S(1)}, f32[56,16,128]{2,1,0:T(8,128)S(1)}, u32[]{:S(2)}, u32[]{:S(2)}) collective-permute-start(f32[56,16,128]{2,1,0:T(8,128)S(1)} %shard_map.38.refs_0_), channel_id=1, source_target_pairs={{0,1},{1,0},{2,3},{3,2},{4,5},{5,4},{6,7},{7,6},{8,9},{9,8},{10,11... | collective-permute-start | bytes 1376264 | tf_op jit(solution)/shard_map/ppermute | solution.py:232
  18.3 5.0 %collective-permute-start.3 = (bf16[384,128]{1,0:T(8,128)(2,1)S(1)}, bf16[384,128]{1,0:T(8,128)(2,1)S(1)}, u32[]{:S(2)}, u32[]{:S(2)}) collective-permute-start(bf16[384,128]{1,0:T(8,128)(2,1)S(1)} %bitcast.6), channel_id=1, source_target_pairs={{0,2},{2,0},{1,3},{3,1},{4,6},{6,4},{5,7},{7,5},{8,10},{10,8},{9,1... | collective-permute-start | bytes 294920 | tf_op jit(solution)/shard_map/ppermute | solution.py:246
  19.9 3.5 %copy-start.1 = (s32[4]{0:T(128)S(1)}, s32[4]{0:T(128)}, u32[]{:S(2)}) copy-start(s32[4]{0:T(128)} %refs_0_.1) | copy-start | bytes 52
where the time goes:
time: 26.2 us; the launch traced here: 26 us
  Pallas kernels  10.7 us (41%)
  waiting for transfers between devices  8.22 us (31%)
  starting transfers between devices  5.11 us (20%)
  local copies, waits for them, and re-layouts  1.07 us (4%)
  other arithmetic  0.92 us (4%)
    pallas_call x1, Pallas kernels, local(): vmem_call(along, [shape((tile_count, wide, frames, LANES), bf16), shape((...  5.26 us
    ppermute x1, waiting for transfers between devices, local(): one = lax.ppermute(flat, 'space', pairs(count, 0))  3.36 us
    ppermute x1, waiting for transfers between devices, local(): two = lax.ppermute(flat, 'space', pairs(count, 1))  3.18 us
    pallas_call x1, Pallas kernels, local(): vmem_call(correlate, shape((radii, lag_count, cols, rows), f32), scratch=...  2.69 us
    pallas_call x1, Pallas kernels, local(): vmem_call(products, shape((tile_count, radii * TILE // LANES, cols * fram...  2.03 us
    ppermute x1, starting transfers between devices, local(): two = lax.ppermute(flat, 'space', pairs(count, 1))  1.91 us
    ppermute x1, starting transfers between devices, local(): one = lax.ppermute(flat, 'space', pairs(count, 0))  1.58 us
    ppermute x1, starting transfers between devices, local(): earlier = lax.ppermute(smooth, 'tm', onward(lax.axis_size('tm')))  1.56 us
  transfers between devices with their start and end apart: 4, of which 4 were waited for; matrix products, arithmetic and copies ran while one was open for 4% of the time, Pallas kernels for 10%

commit v1 on v0

v1 whole, which is shorter than its diff:
```python
import jax
import jax.numpy as jnp
from jax import lax
from jax.experimental import pallas as pl
from jax.experimental.pallas import tpu as pltpu
from jax.sharding import PartitionSpec as P

RMAX = 16
MAXLAG = 16
TILE = 32

gaussian_taps = (0.05448868, 0.24420134, 0.40261995, 0.24420134, 0.05448868)
REACH = len(gaussian_taps) // 2
LANES = 128
VMEM = pltpu.VMEM


def pairs(count, first, beside):
    partner = [None] * count
    for low in range(first, count - 1, 2):
        partner[low], partner[low + 1] = low + 1, low
    found = []
    for source, target in enumerate(partner):
        for other in range(beside):
            twin = other ^ 1 if (other ^ 1) < beside else other
            place = (source, twin) if target is None else (target, other)
            found.append((source * beside + other, place[0] * beside + place[1]))
    return found


def onward(count):
    return [(source, (source + 1) % count) for source in range(count)]


def vmem_call(body, out_shape, scratch=(), smem=0, inputs=1, cost=None):
    specs = [pl.BlockSpec(memory_space=pltpu.SMEM)] * smem + [pl.BlockSpec(memory_space=VMEM)] * inputs
    many = isinstance(out_shape, (list, tuple))
    out_specs = [pl.BlockSpec(memory_space=VMEM)] * len(out_shape) if many else pl.BlockSpec(memory_space=VMEM)
    return pl.pallas_call(
        body,
        out_shape=out_shape,
        in_specs=specs,
        out_specs=out_specs,
        scratch_shapes=list(scratch),
        compiler_params=pltpu.CompilerParams(vmem_limit_bytes=24 * 1024 * 1024),
        cost_estimate=cost,
    )


def blend(parts):
    a, b, c, _, _ = gaussian_taps
    return c * parts[2] + b * (parts[1] + parts[3]) + a * (parts[0] + parts[4])


def prepare_body(frames, cols, masks_ref, x_ref, table_ref, inverse_ref, blur_ref, turned_ref, wide_ref):
    offsets, radii, _ = masks_ref.shape
    span = 2 * TILE
    wide_ref[...] = jnp.zeros_like(wide_ref)
    wide_ref[0:offsets, :, 0:offsets] = masks_ref[...].astype(jnp.float32)
    total = jnp.zeros((radii, 1), jnp.float32)
    for k in range(wide_ref.shape[0] // 2):
        pair = wide_ref[2 * k] + pltpu.roll(wide_ref[2 * k + 1], span, 1)
        total = total + jnp.sum(pair, axis=1, keepdims=True)
        for r in range(radii):
            rows = jnp.broadcast_to(pair[r : r + 1, :], (TILE, LANES))
            turned = pltpu.roll(rows, 0, 1, stride=1, stride_axis=0)
            table_ref[r * TILE : (r + 1) * TILE, k * LANES : (k + 1) * LANES] = turned.astype(jnp.bfloat16)
    inverse_ref[...] = jnp.broadcast_to(1.0 / total, (radii, LANES))

    place, count = lax.axis_index("row"), lax.axis_size("row")
    source = lax.broadcasted_iota(jnp.int32, (LANES, LANES), 0)
    target = lax.broadcasted_iota(jnp.int32, (LANES, LANES), 1)
    outside = jnp.where(source < LANES // 2, source + LANES, source - LANES)

    def held(position):
        low = jnp.logical_or(position >= 0, place > 0)
        return jnp.logical_and(low, jnp.logical_or(position < LANES, place < count - 1))

    for n in range(blur_ref.shape[1] // LANES):
        if n < 2:
            landing = (target // span + 2 * n) * TILE - RMAX + target % span
        else:
            landing = target
        for half, origin in enumerate((source, outside)):
            apart = jnp.abs(origin - landing)
            weight = jnp.zeros((LANES, LANES), jnp.float32)
            for k in range(REACH + 1):
                weight = jnp.where(apart == k, gaussian_taps[REACH + k], weight)
            weight = jnp.where(jnp.logical_and(held(origin), held(landing)), weight, 0.0)
            blur_ref[half * LANES : (half + 1) * LANES, n * LANES : (n + 1) * LANES] = weight
    for c in range(cols):
        turned_ref[c] = x_ref[pl.ds(c, frames, stride=cols), :]


def columns_body(frames, cols, x_ref, a_ref, b_ref, out_ref):
    place, count = lax.axis_index("space"), lax.axis_size("space")
    even = lax.rem(place, 2) == 0
    lowest, highest = place > 0, place < count - 1
    halo = RMAX + REACH

    def raw(c):
        if 0 <= c < cols:
            return x_ref[c]
        at = c + cols if c < 0 else c - cols
        rows = pl.ds(at, frames, stride=cols)
        first, second, there = (b_ref, a_ref, lowest) if c < 0 else (a_ref, b_ref, highest)
        value = jnp.where(even, first[rows, :], second[rows, :])
        return jnp.where(there, value, jnp.zeros_like(value))

    held = {}
    for c in range(-halo, cols + halo):
        held[c] = raw(c)
        done = c - REACH
        if done >= -RMAX:
            value = blend([held[done + k] for k in range(-REACH, REACH + 1)])
            if done < 0 or done >= cols:
                value = jnp.where(lowest if done < 0 else highest, value, jnp.zeros_like(value))
            out_ref[(done + RMAX) * frames : (done + RMAX + 1) * frames, :] = value


def beside(low, high):
    if high is None:
        return low
    lane = lax.broadcasted_iota(jnp.int32, low.shape, 1)
    return jnp.where(lane < LANES // 2, high, low)


def exact_dot(x, y):
    return jnp.dot(x, y, precision=lax.Precision.HIGHEST, preferred_element_type=jnp.float32)


def own_body(frames, cols, own_ref, low_ref, high_ref, blur_ref, smooth_ref, turn_ref):
    rows = pl.ds(RMAX * frames, cols * frames)
    side = beside(low_ref[rows, :], None if high_ref is None else high_ref[rows, :])
    both = jnp.concatenate([own_ref[rows, :], side], axis=1)
    turn_ref[...] = exact_dot(both, blur_ref[:, 2 * LANES : 3 * LANES])
    for t in range(frames):
        smooth_ref[t * cols : (t + 1) * cols, :] = turn_ref[pl.ds(t, cols, stride=frames), :].astype(jnp.bfloat16)


def spread_of(smooth):
    wide = LANES // TILE * LANES
    here = lax.broadcasted_iota(jnp.int32, (LANES, wide), 0)
    there = lax.broadcasted_iota(jnp.int32, (LANES, wide), 1)
    wanted = (there // LANES) * TILE + there % TILE
    pick = jnp.where(here == wanted, 1.0, 0.0).astype(jnp.bfloat16)
    return jnp.dot(smooth, pick, preferred_element_type=jnp.float32)


def sums_body(frames, cols, own_ref, low_ref, high_ref, blur_ref, table_ref, smooth_ref, out_ref, spread_ref, tiles_ref, turn_ref):
    wide = cols + 2 * RMAX
    tile_count = LANES // TILE
    rows = cols * frames
    lane = lax.broadcasted_iota(jnp.int32, (frames, LANES), 1)
    first = lane < 2 * TILE
    chunk = 8
    before = None
    for start in range(0, wide + 1, chunk):
        if start < wide:
            part = pl.ds(start * frames, chunk * frames)
            side = beside(low_ref[part, :], None if high_ref is None else high_ref[part, :])
            both = jnp.concatenate([own_ref[part, :], side], axis=1)
            found = exact_dot(both, blur_ref[:, : 2 * LANES])
        for c in range(start, min(start + chunk, wide + 1)):
            now = []
            for n in range(tile_count // 2):
                if c < wide:
                    value = found[(c - start) * frames : (c - start + 1) * frames, n * LANES : (n + 1) * LANES]
                    now.append((value, pltpu.roll(value, 2 * TILE, 1)))
                else:
                    now.append((jnp.zeros((frames, LANES), jnp.float32),) * 2)
                if before is not None:
                    low = jnp.where(first, before[n][0], now[n][1])
                    high = jnp.where(first, before[n][1], now[n][0])
                    tiles_ref[2 * n, c - 1] = low.astype(jnp.bfloat16)
                    tiles_ref[2 * n + 1, c - 1] = high.astype(jnp.bfloat16)
            before = now
    spread_ref[...] = spread_of(smooth_ref[...])
    for j in range(tile_count):
        pieces = [tiles_ref[j, a : a + cols].reshape(rows, LANES) for a in range(0, 2 * RMAX + 1, 2)]
        found = lax.dot_general(
            jnp.concatenate(pieces, axis=1),
            table_ref[...],
            (((1,), (1,)), ((), ())),
            preferred_element_type=jnp.float32,
        )
        for g in range(out_ref.shape[1]):
            turn_ref[j, g] = found[:, g * LANES : (g + 1) * LANES]
            for t in range(frames):
                out_ref[j, g, t * cols : (t + 1) * cols, :] = turn_ref[j, g, pl.ds(t, cols, stride=frames), :]


def correlate_body(frames, cols, radii, lag_ref, sums_ref, own_ref, earlier_ref, inverse_ref, out_ref, spread_ref):
    lag_count = lag_ref.shape[0]
    tile_count = LANES // TILE
    begun = lax.axis_index("tm") > 0
    spread_ref[0 : frames * cols, :] = jnp.where(begun, spread_of(earlier_ref[...]), 0.0)
    spread_ref[frames * cols : 2 * frames * cols, :] = own_ref[...]
    lane = lax.broadcasted_iota(jnp.int32, (8, LANES), 1)
    block = [jnp.logical_and(lane >= TILE * j, lane < TILE * (j + 1)) for j in range(tile_count)]
    groups = radii * TILE // LANES
    per = LANES // TILE
    for c in range(0, cols, 8):
        totals = {}
        for j in range(tile_count):
            for t in range(frames):
                parts = [sums_ref[j, g, t * cols + c : t * cols + c + 8, :] for g in range(groups)]
                for lag in range(lag_count):
                    row = (MAXLAG + t - lag_ref[lag]) * cols + c
                    old = spread_ref[pl.ds(pl.multiple_of(row, 8), 8), j * LANES : (j + 1) * LANES]
                    for g in range(groups):
                        term = parts[g] * old
                        key = (lag, g, j)
                        totals[key] = totals[key] + term if key in totals else term
        for lag in range(lag_count):
            for g in range(groups):
                for q in range(per):
                    joined = None
                    for j in range(tile_count):
                        piece = totals[(lag, g, j)]
                        shift = (TILE * (j - q)) % LANES
                        piece = pltpu.roll(piece, shift, 1) if shift else piece
                        joined = piece if joined is None else jnp.where(block[j], piece, joined)
                    r = g * per + q
                    out_ref[r, lag, c : c + 8, :] = joined * inverse_ref[r : r + 1, :]


def local(doppler, cycle_masks, lag_list):
    frames, cols, rows = doppler.shape
    radii = cycle_masks.shape[0]
    lag_count = lag_list.shape[0]
    wide = cols + 2 * RMAX
    offsets = 2 * RMAX + 1
    tile_count = rows // TILE
    f32, bf16 = jnp.float32, jnp.bfloat16
    shape = jax.ShapeDtypeStruct

    flat = doppler.reshape(frames * cols, rows)
    count, row_count = lax.axis_size("space"), lax.axis_size("row")
    one = lax.ppermute(flat, ("space", "row"), pairs(count, 0, row_count))
    two = lax.ppermute(flat, ("space", "row"), pairs(count, 1, row_count))

    def prepare(*refs):
        prepare_body(frames, cols, *refs)

    depth = (offsets + 1) * 2 * TILE
    table, inverse, blur, turned = vmem_call(
        prepare,
        [
            shape((radii * TILE, depth), bf16),
            shape((radii, LANES), f32),
            shape((2 * LANES, 3 * LANES), f32),
            shape((cols, frames, LANES), f32),
        ],
        scratch=[VMEM((offsets + 1, radii, LANES), f32)],
        inputs=2,
    )(jnp.transpose(cycle_masks, (1, 0, 2)), flat)

    def columns(*refs):
        columns_body(frames, cols, *refs)

    blurred = vmem_call(columns, shape((wide * frames, rows), f32), inputs=3)(turned, one, two)

    ring = onward(row_count)
    low = lax.ppermute(blurred, "row", ring)
    sides = [low] if row_count == 2 else [low, lax.ppermute(blurred, "row", [(b, a) for a, b in ring])]

    def split(refs):
        return (refs[0], refs[1], refs[2] if len(sides) == 2 else None), refs[1 + len(sides) :]

    def own(*refs):
        lead, rest = split(refs)
        own_body(frames, cols, *lead, *rest)

    smooth = vmem_call(
        own, shape((frames * cols, rows), bf16), scratch=[VMEM((cols * frames, LANES), f32)], inputs=2 + len(sides)
    )(blurred, *sides, blur)
    earlier = lax.ppermute(smooth, "tm", onward(lax.axis_size("tm")))

    def products(*refs):
        lead, rest = split(refs)
        sums_body(frames, cols, *lead, *rest)

    groups = radii * TILE // LANES
    flops = 2 * tile_count * cols * frames * radii * TILE * depth
    sums, spread = vmem_call(
        products,
        [shape((tile_count, groups, frames * cols, LANES), f32), shape((frames * cols, tile_count * LANES), f32)],
        scratch=[
            VMEM((tile_count, wide, frames, LANES), bf16),
            VMEM((tile_count, groups, cols * frames, LANES), f32),
        ],
        inputs=4 + len(sides),
        cost=pl.CostEstimate(flops=flops, bytes_accessed=1 << 20, transcendentals=0),
    )(blurred, *sides, blur, table, smooth)

    def correlate(*refs):
        correlate_body(frames, cols, radii, *refs)

    out = vmem_call(
        correlate,
        shape((radii, lag_count, cols, rows), f32),
        scratch=[VMEM((2 * frames * cols, tile_count * LANES), f32)],
        smem=1,
        inputs=4,
    )(lag_list, sums, spread, earlier, inverse)
    return out[None]


def solution(mesh):
    return jax.shard_map(
        local,
        mesh=mesh,
        in_specs=(P("tm", ("patch", "space"), "row"), P(), P()),
        out_specs=P("tm", None, None, ("patch", "space"), "row"),
        check_vma=False,
    )
```

time: 26.2 us -> 19.4 us (0.74)
  the two profiles are of different devices: /device:TPU:20 before, /device:TPU:0 now
where the time goes in v1:
time: 19.4 us; the launch traced here: 19.3 us
  Pallas kernels  7.74 us (40%)
  starting transfers between devices  6.26 us (32%)
  waiting for transfers between devices  3.35 us (17%)
  local copies, waits for them, and re-layouts  1.87 us (10%)
    ppermute x1, starting transfers between devices, local(): one = lax.ppermute(flat, ('space', 'row'), pairs(count, 0, row_count))  4.14 us
    pallas_call x1, Pallas kernels, local(): vmem_call(products, [shape((tile_count, groups, frames * cols, LANES), f3...  3.27 us
    pallas_call x1, Pallas kernels, local(): vmem_call(correlate, shape((radii, lag_count, cols, rows), f32), scratch=...  2.27 us
    unnamed x6, local copies, waits for them, and re-layouts  1.87 us
    ppermute x1, waiting for transfers between devices, local(): low = lax.ppermute(blurred, 'row', ring)  1.8 us
    ppermute x1, starting transfers between devices, local(): earlier = lax.ppermute(smooth, 'tm', onward(lax.axis_size('tm')))  1.56 us
    pallas_call x1, Pallas kernels, local(): vmem_call(prepare, [shape((radii * TILE, depth), bf16), shape((radii, LAN...  1.5 us
    ppermute x1, waiting for transfers between devices, local(): one = lax.ppermute(flat, ('space', 'row'), pairs(count, 0, row_count))  1.47 us
  transfers between devices with their start and end apart: 4, of which 3 were waited for; matrix products, arithmetic and copies ran while one was open for 0% of the time, Pallas kernels for 25%

profile of v1, /device:TPU:0, one launch (start us, length us, event | category | flops | bytes accessed | tf_op | source)
XLA Modules:
  0.0 19.3 jit_solution(11745295628313860353)
XLA Ops:
  0.0 0.5 %collective-permute-start.1 = (f32[384,128]{1,0:T(8,128)}, f32[384,128]{1,0:T(8,128)S(1)}, u32[]{:S(2)}, u32[]{:S(2)}) collective-permute-start(f32[384,128]{1,0:T(8,128)} %bitcast.3), channel_id=1, source_target_pairs={{0,1},{1,0},{4,8},{5,9},{8,4},{9,5},{12,13},{13,12},{2,3},{3,2},{6... | collective-permute-start | bytes 589832 | tf_op jit(solution)/shard_map/ppermute | solution.py:241
  0.5 4.1 %collective-permute-start = (f32[384,128]{1,0:T(8,128)}, f32[384,128]{1,0:T(8,128)S(1)}, u32[]{:S(2)}, u32[]{:S(2)}) collective-permute-start(f32[384,128]{1,0:T(8,128)} %bitcast.4), channel_id=1, source_target_pairs={{0,4},{1,5},{4,0},{5,1},{8,12},{9,13},{12,8},{13,9},{2,6},{3,7},{6... | collective-permute-start | bytes 589832 | tf_op jit(solution)/shard_map/ppermute | solution.py:240
  4.6 0.0 copy-start
  4.6 1.0 %copy-done = f32[16,24,128]{2,1,0:T(8,128)S(1)} copy-done((f32[16,24,128]{2,1,0:T(8,128)S(1)}, f32[16,24,128]{2,1,0:T(8,128)}, u32[]{:S(2)}) %copy-start) | copy-done | bytes 196632
  5.6 0.0 copy-start.1
  5.6 0.9 %copy-done.1 = s32[8,33,33]{2,0,1:T(8,128)S(1)} copy-done((s32[8,33,33]{2,0,1:T(8,128)S(1)}, s32[8,33,33]{2,0,1:T(8,128)}, u32[]{:S(2)}) %copy-start.1) | copy-done | bytes 34872
  6.5 1.5 %shard_map.37 = (bf16[256,2176]{1,0:T(8,128)(2,1)S(1)}, f32[8,128]{1,0:T(8,128)S(1)}, f32[256,384]{1,0:T(8,128)S(1)}, f32[24,16,128]{2,1,0:T(8,128)S(1)}) custom-call(s32[33,8,33]{2,1,0:T(8,128)S(1)} %bitcast.6, f32[384,128]{1,0:T(8,128)S(1)} %bitcast.5), custom_call_target="tpu_custom_call" | custom-call | tf_op jit(solution)/shard_map/pallas_call | solution.py:247
  8.0 0.0 collective-permute-done.1.refs_2_
  8.0 1.5 %collective-permute-done.refs_1_ = f32[384,128]{1,0:T(8,128)S(1)} collective-permute-done((f32[384,128]{1,0:T(8,128)}, f32[384,128]{1,0:T(8,128)S(1)}, u32[]{:S(2)}, u32[]{:S(2)}) %collective-permute-start) | collective-permute-done | bytes 196640 | tf_op jit(solution)/shard_map/ppermute | solution.py:240
  9.5 0.2 %shard_map.38.refs_0_ = f32[896,128]{1,0:T(8,128)S(1)} custom-call(f32[24,16,128]{2,1,0:T(8,128)S(1)} %get-tuple-element.11.refs_0_, f32[384,128]{1,0:T(8,128)S(1)} %collective-permute-done.refs_1_, f32[384,128]{1,0:T(8,128)S(1)} %collective-permute-done.1.refs_2_), custom_call_target="tpu_custom_call" | custom-call | tf_op jit(solution)/shard_map/pallas_call | solution.py:262
  9.7 0.1 collective-permute-start.2
  9.8 1.8 %collective-permute-done.2.refs_1_ = f32[896,128]{1,0:T(8,128)S(1)} collective-permute-done((f32[896,128]{1,0:T(8,128)S(1)}, f32[896,128]{1,0:T(8,128)S(1)}, u32[]{:S(2)}, u32[]{:S(2)}) %collective-permute-start.2) | collective-permute-done | bytes 458784 | tf_op jit(solution)/shard_map/ppermute | solution.py:265
  11.6 0.5 %shard_map.39.refs_4_ = bf16[384,128]{1,0:T(8,128)(2,1)S(1)} custom-call(f32[896,128]{1,0:T(8,128)S(1)} %shard_map.38.refs_0_, f32[896,128]{1,0:T(8,128)S(1)} %collective-permute-done.2.refs_1_, f32[256,384]{1,0:T(8,128)S(1)} %get-tuple-element.12.refs_2_), custom_call_target="tpu_custom_call" | custom-call | tf_op jit(solution)/shard_map/pallas_call | solution.py:275
  12.1 1.6 %collective-permute-start.3 = (bf16[384,128]{1,0:T(8,128)(2,1)S(1)}, bf16[384,128]{1,0:T(8,128)(2,1)S(1)}, u32[]{:S(2)}, u32[]{:S(2)}) collective-permute-start(bf16[384,128]{1,0:T(8,128)(2,1)S(1)} %shard_map.39.refs_4_), channel_id=1, source_target_pairs={{0,2},{2,0},{1,3},{3,1},{4,6},{6,4},{5,7},{7,5},{8,10},{10,8},{9,1... | collective-permute-start | bytes 294920 | tf_op jit(solution)/shard_map/ppermute | solution.py:278
  13.6 0.0 copy-start.2
  13.6 3.3 %shard_map.40 = (f32[4,2,384,128]{3,2,1,0:T(8,128)S(1)}, f32[384,512]{1,0:T(8,128)S(1)}) custom-call(f32[896,128]{1,0:T(8,128)S(1)} %shard_map.38.refs_0_, f32[896,128]{1,0:T(8,128)S(1)} %collective-permute-done.2.refs_1_, f32[256,384]{1,0:T(8,128)S(1)} %get-tuple-element.12.refs_2_, bf16[256,2176]{1,0:T(8,128)(2,1)S(1)} %get-tuple-element.13.refs_3_, ...), custom_call_target="tpu_custom_call" | custom-call | flops 1711276032 | bytes 1048576 | tf_op jit(solution)/shard_map/pallas_call | solution.py:286
  16.9 0.1 collective-permute-done.3.refs_3_
  17.0 0.0 copy-done.2
  17.0 2.3 %shard_map.41 = f32[8,4,24,128]{3,2,1,0:T(8,128)} custom-call(s32[4]{0:T(128)S(1)} %copy-done.2, f32[4,2,384,128]{3,2,1,0:T(8,128)S(1)} %get-tuple-element.14.refs_1_, f32[384,512]{1,0:T(8,128)S(1)} %get-tuple-element.15.refs_2_, bf16[384,128]{1,0:T(8,128)(2,1)S(1)} %collective-permute-done.3.refs_3_, f32[8,128]{1,0:T(8,128)S(1)} %get-tuple-element.16.refs_4_), custom_call_target="tpu_custom_call" | custom-call | tf_op jit(solution)/shard_map/pallas_call | solution.py:300
Async XLA Ops:
  0.0 8.0 %collective-permute-start.1 = (f32[384,128]{1,0:T(8,128)}, f32[384,128]{1,0:T(8,128)S(1)}, u32[]{:S(2)}, u32[]{:S(2)}) collective-permute-start(f32[384,128]{1,0:T(8,128)} %bitcast.3), channel_id=1, source_target_pairs={{0,1},{1,0},{4,8},{5,9},{8,4},{9,5},{12,13},{13,12},{2,3},{3,2},{6... | collective-permute-start | bytes 589832 | tf_op jit(solution)/shard_map/ppermute | solution.py:241
  0.5 9.0 %collective-permute-start = (f32[384,128]{1,0:T(8,128)}, f32[384,128]{1,0:T(8,128)S(1)}, u32[]{:S(2)}, u32[]{:S(2)}) collective-permute-start(f32[384,128]{1,0:T(8,128)} %bitcast.4), channel_id=1, source_target_pairs={{0,4},{1,5},{4,0},{5,1},{8,12},{9,13},{12,8},{13,9},{2,6},{3,7},{6... | collective-permute-start | bytes 589832 | tf_op jit(solution)/shard_map/ppermute | solution.py:240
  4.6 1.0 %copy-start = (f32[16,24,128]{2,1,0:T(8,128)S(1)}, f32[16,24,128]{2,1,0:T(8,128)}, u32[]{:S(2)}) copy-start(f32[16,24,128]{2,1,0:T(8,128)} %param.3) | copy-start | bytes 589828
  5.6 0.9 %copy-start.1 = (s32[8,33,33]{2,0,1:T(8,128)S(1)}, s32[8,33,33]{2,0,1:T(8,128)}, u32[]{:S(2)}) copy-start(s32[8,33,33]{2,0,1:T(8,128)} %param.4) | copy-start | bytes 104548
  9.7 1.9 %collective-permute-start.2 = (f32[896,128]{1,0:T(8,128)S(1)}, f32[896,128]{1,0:T(8,128)S(1)}, u32[]{:S(2)}, u32[]{:S(2)}) collective-permute-start(f32[896,128]{1,0:T(8,128)S(1)} %shard_map.38.refs_0_), channel_id=1, source_target_pairs={{0,1},{1,0},{2,3},{3,2},{4,5},{5,4},{6,7},{7,6},{8,9},{9,8},{10,11... | collective-permute-start | bytes 1376264 | tf_op jit(solution)/shard_map/ppermute | solution.py:265
  12.1 4.9 %collective-permute-start.3 = (bf16[384,128]{1,0:T(8,128)(2,1)S(1)}, bf16[384,128]{1,0:T(8,128)(2,1)S(1)}, u32[]{:S(2)}, u32[]{:S(2)}) collective-permute-start(bf16[384,128]{1,0:T(8,128)(2,1)S(1)} %shard_map.39.refs_4_), channel_id=1, source_target_pairs={{0,2},{2,0},{1,3},{3,1},{4,6},{6,4},{5,7},{7,5},{8,10},{10,8},{9,1... | collective-permute-start | bytes 294920 | tf_op jit(solution)/shard_map/ppermute | solution.py:278
  13.6 3.3 %copy-start.2 = (s32[4]{0:T(128)S(1)}, s32[4]{0:T(128)}, u32[]{:S(2)}) copy-start(s32[4]{0:T(128)} %refs_0_.1) | copy-start | bytes 52

commit v2 on v1

--- a/solution.py
+++ b/solution.py
@@ -4,6 +4,7 @@
 from jax.experimental import pallas as pl
 from jax.experimental.pallas import tpu as pltpu
 from jax.sharding import PartitionSpec as P
+
 
 RMAX = 16
 MAXLAG = 16
@@ -32,10 +33,11 @@
     return [(source, (source + 1) % count) for source in range(count)]
 
 
-def vmem_call(body, out_shape, scratch=(), smem=0, inputs=1, cost=None):
+def vmem_call(body, out_shape, scratch=(), smem=0, inputs=1, cost=None, out_space=VMEM):
     specs = [pl.BlockSpec(memory_space=pltpu.SMEM)] * smem + [pl.BlockSpec(memory_space=VMEM)] * inputs
     many = isinstance(out_shape, (list, tuple))
-    out_specs = [pl.BlockSpec(memory_space=VMEM)] * len(out_shape) if many else pl.BlockSpec(memory_space=VMEM)
+    out_specs = pl.BlockSpec(memory_space=out_space)
+    out_specs = [out_specs] * len(out_shape) if many else out_specs
     return pl.pallas_call(
         body,
         out_shape=out_shape,
@@ -190,8 +192,9 @@
                 out_ref[j, g, t * cols : (t + 1) * cols, :] = turn_ref[j, g, pl.ds(t, cols, stride=frames), :]
 
 
-def correlate_body(frames, cols, radii, lag_ref, sums_ref, own_ref, earlier_ref, inverse_ref, out_ref, spread_ref):
-    lag_count = lag_ref.shape[0]
+def correlate_body(frames, cols, radii, lag_ref, sums_ref, own_ref, earlier_ref, inverse_ref, out_ref, spread_ref, held_ref, sem):
+    lag_count = lag_ref.shape[1]
+    lags = [lag_ref[0, lag] for lag in range(lag_count)]
     tile_count = LANES // TILE
     begun = lax.axis_index("tm") > 0
     spread_ref[0 : frames * cols, :] = jnp.where(begun, spread_of(earlier_ref[...]), 0.0)
@@ -200,13 +203,14 @@
     block = [jnp.logical_and(lane >= TILE * j, lane < TILE * (j + 1)) for j in range(tile_count)]
     groups = radii * TILE // LANES
     per = LANES // TILE
+    copies = []
     for c in range(0, cols, 8):
         totals = {}
         for j in range(tile_count):
             for t in range(frames):
                 parts = [sums_ref[j, g, t * cols + c : t * cols + c + 8, :] for g in range(groups)]
                 for lag in range(lag_count):
-                    row = (MAXLAG + t - lag_ref[lag]) * cols + c
+                    row = (MAXLAG + t - lags[lag]) * cols + c
                     old = spread_ref[pl.ds(pl.multiple_of(row, 8), 8), j * LANES : (j + 1) * LANES]
                     for g in range(groups):
                         term = parts[g] * old
@@ -222,7 +226,11 @@
                         piece = pltpu.roll(piece, shift, 1) if shift else piece
                         joined = piece if joined is None else jnp.where(block[j], piece, joined)
                     r = g * per + q
-                    out_ref[r, lag, c : c + 8, :] = joined * inverse_ref[r : r + 1, :]
+                    held_ref[c // 8, r, lag] = joined * inverse_ref[r : r + 1, :]
+        copies.append(pltpu.make_async_copy(held_ref.at[c // 8], out_ref.at[:, :, pl.ds(c, 8), :], sem.at[c // 8]))
+        copies[-1].start()
+    for copy in copies:
+        copy.wait()
 
 
 def local(doppler, cycle_masks, lag_list):
@@ -300,10 +308,14 @@
     out = vmem_call(
         correlate,
         shape((radii, lag_count, cols, rows), f32),
-        scratch=[VMEM((2 * frames * cols, tile_count * LANES), f32)],
-        smem=1,
-        inputs=4,
-    )(lag_list, sums, spread, earlier, inverse)
+        scratch=[
+            VMEM((2 * frames * cols, tile_count * LANES), f32),
+            VMEM((cols // 8, radii, lag_count, 8, LANES), f32),
+            pltpu.SemaphoreType.DMA((cols // 8,)),
+        ],
+        inputs=5,
+        out_space=pl.ANY,
+    )(lag_list.reshape(1, lag_count), sums, spread, earlier, inverse)
     return out[None]
 
 

time: 19.4 us -> 18.8 us (0.969)
  Pallas kernels: 7.74 us -> 7.16 us
    pallas_call x1, Pallas kernels: 2.27 us -> 1.69 us  [local(): vmem_call(correlate, shape((radii, lag_count, cols, rows), f32), scratch=...]
  transfers between devices with their start and end apart: 4 -> 4, of which waited for: 3 -> 3; matrix products, arithmetic and copies ran while one was open for 0% -> 0% of each run, Pallas kernels for 25% -> 26%
where the time goes in v2:
time: 18.8 us; the launch traced here: 18.7 us
  Pallas kernels  7.16 us (38%)
  starting transfers between devices  6.26 us (33%)
  waiting for transfers between devices  3.35 us (18%)
  local copies, waits for them, and re-layouts  1.87 us (10%)
    ppermute x1, starting transfers between devices, local(): one = lax.ppermute(flat, ('space', 'row'), pairs(count, 0, row_count))  4.14 us
    pallas_call x1, Pallas kernels, local(): vmem_call(products, [shape((tile_count, groups, frames * cols, LANES), f3...  3.27 us
    unnamed x6, local copies, waits for them, and re-layouts  1.87 us
    ppermute x1, waiting for transfers between devices, local(): low = lax.ppermute(blurred, 'row', ring)  1.8 us
    pallas_call x1, Pallas kernels, local(): vmem_call(correlate, shape((radii, lag_count, cols, rows), f32), scratch=...  1.69 us
    ppermute x1, starting transfers between devices, local(): earlier = lax.ppermute(smooth, 'tm', onward(lax.axis_size('tm')))  1.56 us
    pallas_call x1, Pallas kernels, local(): vmem_call(prepare, [shape((radii * TILE, depth), bf16), shape((radii, LAN...  1.5 us
    ppermute x1, waiting for transfers between devices, local(): one = lax.ppermute(flat, ('space', 'row'), pairs(count, 0, row_count))  1.47 us
  transfers between devices with their start and end apart: 4, of which 3 were waited for; matrix products, arithmetic and copies ran while one was open for 0% of the time, Pallas kernels for 26%

profile of v2, /device:TPU:0, one launch (start us, length us, event | category | flops | bytes accessed | tf_op | source)
XLA Modules:
  0.0 18.7 jit_solution(10550792830615766021)
XLA Ops:
  0.0 0.5 %collective-permute-start.1 = (f32[384,128]{1,0:T(8,128)}, f32[384,128]{1,0:T(8,128)S(1)}, u32[]{:S(2)}, u32[]{:S(2)}) collective-permute-start(f32[384,128]{1,0:T(8,128)} %bitcast.4), channel_id=1, source_target_pairs={{0,1},{1,0},{4,8},{5,9},{8,4},{9,5},{12,13},{13,12},{2,3},{3,2},{6... | collective-permute-start | bytes 589832 | tf_op jit(solution)/shard_map/ppermute | solution.py:249
  0.5 4.1 %collective-permute-start = (f32[384,128]{1,0:T(8,128)}, f32[384,128]{1,0:T(8,128)S(1)}, u32[]{:S(2)}, u32[]{:S(2)}) collective-permute-start(f32[384,128]{1,0:T(8,128)} %bitcast.5), channel_id=1, source_target_pairs={{0,4},{1,5},{4,0},{5,1},{8,12},{9,13},{12,8},{13,9},{2,6},{3,7},{6... | collective-permute-start | bytes 589832 | tf_op jit(solution)/shard_map/ppermute | solution.py:248
  4.6 0.0 copy-start
  4.6 1.0 %copy-done = f32[16,24,128]{2,1,0:T(8,128)S(1)} copy-done((f32[16,24,128]{2,1,0:T(8,128)S(1)}, f32[16,24,128]{2,1,0:T(8,128)}, u32[]{:S(2)}) %copy-start) | copy-done | bytes 196632
  5.6 0.0 copy-start.1
  5.6 0.9 %copy-done.1 = s32[8,33,33]{2,0,1:T(8,128)S(1)} copy-done((s32[8,33,33]{2,0,1:T(8,128)S(1)}, s32[8,33,33]{2,0,1:T(8,128)}, u32[]{:S(2)}) %copy-start.1) | copy-done | bytes 34872
  6.5 1.5 %shard_map.37 = (bf16[256,2176]{1,0:T(8,128)(2,1)S(1)}, f32[8,128]{1,0:T(8,128)S(1)}, f32[256,384]{1,0:T(8,128)S(1)}, f32[24,16,128]{2,1,0:T(8,128)S(1)}) custom-call(s32[33,8,33]{2,1,0:T(8,128)S(1)} %bitcast.7, f32[384,128]{1,0:T(8,128)S(1)} %bitcast.6), custom_call_target="tpu_custom_call" | custom-call | tf_op jit(solution)/shard_map/pallas_call | solution.py:255
  8.0 0.0 collective-permute-done.1.refs_2_
  8.0 1.5 %collective-permute-done.refs_1_ = f32[384,128]{1,0:T(8,128)S(1)} collective-permute-done((f32[384,128]{1,0:T(8,128)}, f32[384,128]{1,0:T(8,128)S(1)}, u32[]{:S(2)}, u32[]{:S(2)}) %collective-permute-start) | collective-permute-done | bytes 196640 | tf_op jit(solution)/shard_map/ppermute | solution.py:248
  9.5 0.2 %shard_map.38.refs_0_ = f32[896,128]{1,0:T(8,128)S(1)} custom-call(f32[24,16,128]{2,1,0:T(8,128)S(1)} %get-tuple-element.11.refs_0_, f32[384,128]{1,0:T(8,128)S(1)} %collective-permute-done.refs_1_, f32[384,128]{1,0:T(8,128)S(1)} %collective-permute-done.1.refs_2_), custom_call_target="tpu_custom_call" | custom-call | tf_op jit(solution)/shard_map/pallas_call | solution.py:270
  9.7 0.1 collective-permute-start.2
  9.8 1.8 %collective-permute-done.2.refs_1_ = f32[896,128]{1,0:T(8,128)S(1)} collective-permute-done((f32[896,128]{1,0:T(8,128)S(1)}, f32[896,128]{1,0:T(8,128)S(1)}, u32[]{:S(2)}, u32[]{:S(2)}) %collective-permute-start.2) | collective-permute-done | bytes 458784 | tf_op jit(solution)/shard_map/ppermute | solution.py:273
  11.6 0.5 %shard_map.39.refs_4_ = bf16[384,128]{1,0:T(8,128)(2,1)S(1)} custom-call(f32[896,128]{1,0:T(8,128)S(1)} %shard_map.38.refs_0_, f32[896,128]{1,0:T(8,128)S(1)} %collective-permute-done.2.refs_1_, f32[256,384]{1,0:T(8,128)S(1)} %get-tuple-element.12.refs_2_), custom_call_target="tpu_custom_call" | custom-call | tf_op jit(solution)/shard_map/pallas_call | solution.py:283
  12.1 1.6 %collective-permute-start.3 = (bf16[384,128]{1,0:T(8,128)(2,1)S(1)}, bf16[384,128]{1,0:T(8,128)(2,1)S(1)}, u32[]{:S(2)}, u32[]{:S(2)}) collective-permute-start(bf16[384,128]{1,0:T(8,128)(2,1)S(1)} %shard_map.39.refs_4_), channel_id=1, source_target_pairs={{0,2},{2,0},{1,3},{3,1},{4,6},{6,4},{5,7},{7,5},{8,10},{10,8},{9,1... | collective-permute-start | bytes 294920 | tf_op jit(solution)/shard_map/ppermute | solution.py:286
  13.6 0.0 copy-start.2
  13.6 3.3 %shard_map.40 = (f32[4,2,384,128]{3,2,1,0:T(8,128)S(1)}, f32[384,512]{1,0:T(8,128)S(1)}) custom-call(f32[896,128]{1,0:T(8,128)S(1)} %shard_map.38.refs_0_, f32[896,128]{1,0:T(8,128)S(1)} %collective-permute-done.2.refs_1_, f32[256,384]{1,0:T(8,128)S(1)} %get-tuple-element.12.refs_2_, bf16[256,2176]{1,0:T(8,128)(2,1)S(1)} %get-tuple-element.13.refs_3_, ...), custom_call_target="tpu_custom_call" | custom-call | flops 1711276032 | bytes 1048576 | tf_op jit(solution)/shard_map/pallas_call | solution.py:294
  16.9 0.1 collective-permute-done.3.refs_3_
  17.0 0.0 copy-done.2
  17.0 1.7 %shard_map.41 = f32[8,4,24,128]{3,2,1,0:T(8,128)} custom-call(s32[1,4]{1,0:T(1,128)S(1)} %bitcast.8, f32[4,2,384,128]{3,2,1,0:T(8,128)S(1)} %get-tuple-element.14.refs_1_, f32[384,512]{1,0:T(8,128)S(1)} %get-tuple-element.15.refs_2_, bf16[384,128]{1,0:T(8,128)(2,1)S(1)} %collective-permute-done.3.refs_3_, f32[8,128]{1,0:T(8,128)S(1)} %get-tuple-element.16.refs_4_), custom_call_target="tpu_custom_call" | custom-call | tf_op jit(solution)/shard_map/pallas_call | solution.py:308
Async XLA Ops:
  0.0 8.0 %collective-permute-start.1 = (f32[384,128]{1,0:T(8,128)}, f32[384,128]{1,0:T(8,128)S(1)}, u32[]{:S(2)}, u32[]{:S(2)}) collective-permute-start(f32[384,128]{1,0:T(8,128)} %bitcast.4), channel_id=1, source_target_pairs={{0,1},{1,0},{4,8},{5,9},{8,4},{9,5},{12,13},{13,12},{2,3},{3,2},{6... | collective-permute-start | bytes 589832 | tf_op jit(solution)/shard_map/ppermute | solution.py:249
  0.5 9.0 %collective-permute-start = (f32[384,128]{1,0:T(8,128)}, f32[384,128]{1,0:T(8,128)S(1)}, u32[]{:S(2)}, u32[]{:S(2)}) collective-permute-start(f32[384,128]{1,0:T(8,128)} %bitcast.5), channel_id=1, source_target_pairs={{0,4},{1,5},{4,0},{5,1},{8,12},{9,13},{12,8},{13,9},{2,6},{3,7},{6... | collective-permute-start | bytes 589832 | tf_op jit(solution)/shard_map/ppermute | solution.py:248
  4.6 1.0 %copy-start = (f32[16,24,128]{2,1,0:T(8,128)S(1)}, f32[16,24,128]{2,1,0:T(8,128)}, u32[]{:S(2)}) copy-start(f32[16,24,128]{2,1,0:T(8,128)} %param.3) | copy-start | bytes 589828
  5.6 0.9 %copy-start.1 = (s32[8,33,33]{2,0,1:T(8,128)S(1)}, s32[8,33,33]{2,0,1:T(8,128)}, u32[]{:S(2)}) copy-start(s32[8,33,33]{2,0,1:T(8,128)} %param.4) | copy-start | bytes 104548
  9.7 1.9 %collective-permute-start.2 = (f32[896,128]{1,0:T(8,128)S(1)}, f32[896,128]{1,0:T(8,128)S(1)}, u32[]{:S(2)}, u32[]{:S(2)}) collective-permute-start(f32[896,128]{1,0:T(8,128)S(1)} %shard_map.38.refs_0_), channel_id=1, source_target_pairs={{0,1},{1,0},{2,3},{3,2},{4,5},{5,4},{6,7},{7,6},{8,9},{9,8},{10,11... | collective-permute-start | bytes 1376264 | tf_op jit(solution)/shard_map/ppermute | solution.py:273
  12.1 4.9 %collective-permute-start.3 = (bf16[384,128]{1,0:T(8,128)(2,1)S(1)}, bf16[384,128]{1,0:T(8,128)(2,1)S(1)}, u32[]{:S(2)}, u32[]{:S(2)}) collective-permute-start(bf16[384,128]{1,0:T(8,128)(2,1)S(1)} %shard_map.39.refs_4_), channel_id=1, source_target_pairs={{0,2},{2,0},{1,3},{3,1},{4,6},{6,4},{5,7},{7,5},{8,10},{10,8},{9,1... | collective-permute-start | bytes 294920 | tf_op jit(solution)/shard_map/ppermute | solution.py:286
  13.6 3.3 %copy-start.2 = (s32[4]{0:T(128)S(1)}, s32[4]{0:T(128)}, u32[]{:S(2)}) copy-start(s32[4]{0:T(128)} %param.5) | copy-start | bytes 52

commit v3 on v2

v3 whole, which is shorter than its diff:
```python
import jax
import jax.numpy as jnp
from jax import lax
from jax.experimental import pallas as pl
from jax.experimental.pallas import tpu as pltpu
from jax.sharding import PartitionSpec as P


RMAX = 16
MAXLAG = 16
TILE = 32

gaussian_taps = (0.05448868, 0.24420134, 0.40261995, 0.24420134, 0.05448868)
REACH = len(gaussian_taps) // 2
LANES = 128
VMEM = pltpu.VMEM


def pairs(count, first, beside):
    partner = [None] * count
    for low in range(first, count - 1, 2):
        partner[low], partner[low + 1] = low + 1, low
    found = []
    for source, target in enumerate(partner):
        for other in range(beside):
            twin = other ^ 1 if (other ^ 1) < beside else other
            place = (source, twin) if target is None else (target, other)
            found.append((source * beside + other, place[0] * beside + place[1]))
    return found


def onward(count):
    return [(source, (source + 1) % count) for source in range(count)]


def vmem_call(body, out_shape, scratch=(), smem=0, inputs=1, cost=None, in_space=VMEM, out_space=VMEM, aliases=None):
    specs = [pl.BlockSpec(memory_space=pltpu.SMEM)] * smem + [pl.BlockSpec(memory_space=in_space)] * inputs
    many = isinstance(out_shape, (list, tuple))
    spaces = out_space if isinstance(out_space, list) else [out_space] * (len(out_shape) if many else 1)
    out_specs = [pl.BlockSpec(memory_space=space) for space in spaces]
    out_specs = out_specs if many else out_specs[0]
    return pl.pallas_call(
        body,
        out_shape=out_shape,
        in_specs=specs,
        out_specs=out_specs,
        scratch_shapes=list(scratch),
        compiler_params=pltpu.CompilerParams(vmem_limit_bytes=24 * 1024 * 1024),
        cost_estimate=cost,
        input_output_aliases=aliases or {},
    )


def blend(parts):
    a, b, c, _, _ = gaussian_taps
    return c * parts[2] + b * (parts[1] + parts[3]) + a * (parts[0] + parts[4])


def prepare_body(masks_hbm, x_hbm, table_ref, inverse_ref, blur_ref, x_ref, wide_ref, masks_ref, sem):
    masks_in = pltpu.make_async_copy(masks_hbm, masks_ref, sem.at[0])
    masks_in.start()
    x_in = pltpu.make_async_copy(x_hbm, x_ref, sem.at[1])
    x_in.start()
    offsets, radii, _ = masks_ref.shape
    span = 2 * TILE

    place, count = lax.axis_index("row"), lax.axis_size("row")
    source = lax.broadcasted_iota(jnp.int32, (LANES, LANES), 0)
    target = lax.broadcasted_iota(jnp.int32, (LANES, LANES), 1)
    outside = jnp.where(source < LANES // 2, source + LANES, source - LANES)

    def held(position):
        low = jnp.logical_or(position >= 0, place > 0)
        return jnp.logical_and(low, jnp.logical_or(position < LANES, place < count - 1))

    for n in range(blur_ref.shape[1] // LANES):
        landing = (target // span + 2 * n) * TILE - RMAX + target % span
        for half, origin in enumerate((source, outside)):
            apart = jnp.abs(origin - landing)
            weight = jnp.zeros((LANES, LANES), jnp.float32)
            for k in range(REACH + 1):
                weight = jnp.where(apart == k, gaussian_taps[REACH + k], weight)
            weight = jnp.where(jnp.logical_and(held(origin), held(landing)), weight, 0.0)
            blur_ref[half * LANES : (half + 1) * LANES, n * LANES : (n + 1) * LANES] = weight

    wide_ref[...] = jnp.zeros_like(wide_ref)
    masks_in.wait()
    wide_ref[0:offsets, :, 0:offsets] = masks_ref[...].astype(jnp.float32)
    total = jnp.zeros((radii, LANES), jnp.float32)
    for k in range(wide_ref.shape[0] // 2):
        pair = wide_ref[2 * k] + pltpu.roll(wide_ref[2 * k + 1], span, 1)
        total = total + pair
        for r in range(radii):
            rows = jnp.broadcast_to(pair[r : r + 1, :], (TILE, LANES))
            turned = pltpu.roll(rows, 0, 1, stride=1, stride_axis=0)
            table_ref[r * TILE : (r + 1) * TILE, k * LANES : (k + 1) * LANES] = turned.astype(jnp.bfloat16)
    inverse_ref[...] = jnp.broadcast_to(1.0 / jnp.sum(total, axis=1, keepdims=True), (radii, LANES))
    x_in.wait()


def beside(low, high):
    if high is None:
        return low
    lane = lax.broadcasted_iota(jnp.int32, low.shape, 1)
    return jnp.where(lane < LANES // 2, high, low)


def exact_dot(x, y):
    return jnp.dot(x, y, precision=lax.Precision.HIGHEST, preferred_element_type=jnp.float32)


def own_lanes(first, second):
    lane = lax.broadcasted_iota(jnp.int32, first.shape, 1)
    found = pltpu.roll(first, LANES - RMAX, 1)
    found = jnp.where(lane < TILE, found, pltpu.roll(first, LANES - RMAX - TILE, 1))
    found = jnp.where(lane < 2 * TILE, found, pltpu.roll(second, RMAX + TILE, 1))
    return jnp.where(lane < 3 * TILE, found, pltpu.roll(second, RMAX, 1))


def own_body(frames, cols, x_ref, low_ref, high_ref, blur_ref, smooth_ref, pairs_ref, rim_ref, both_ref, found_ref, turn_ref):
    inner = cols - 2 * REACH

    def raw(c):
        rows = pl.ds(c, frames, stride=cols)
        return x_ref[rows, :], beside(low_ref[rows, :], None if high_ref is None else high_ref[rows, :])

    held = {}
    for c in range(cols):
        held[c] = raw(c)
        done = c - REACH
        if done >= REACH:
            for n in range(2):
                both_ref[(done - REACH) * frames : (done - REACH + 1) * frames, n * LANES : (n + 1) * LANES] = blend(
                    [held[done + k][n] for k in range(-REACH, REACH + 1)]
                )
    found_ref[...] = exact_dot(both_ref[...], blur_ref[...])
    turn_ref[...] = jnp.zeros_like(turn_ref)
    lane = lax.broadcasted_iota(jnp.int32, (frames, LANES), 1)
    first = lane < 2 * TILE
    before = None
    for c in range(inner):
        rows = slice(c * frames, (c + 1) * frames)
        value = [found_ref[rows, n * LANES : (n + 1) * LANES] for n in range(2)]
        turn_ref[(c + REACH) * frames : (c + REACH + 1) * frames, :] = own_lanes(*value)
        now = [(v, pltpu.roll(v, 2 * TILE, 1)) for v in value]
        if c == 0 or c == inner - 1:
            for n in range(2):
                rim_ref[0 if c == 0 else 1, n] = value[n]
        if before is not None:
            for n in range(2):
                pairs_ref[2 * n, c - 1] = jnp.where(first, before[n][0], now[n][1]).astype(jnp.bfloat16)
                pairs_ref[2 * n + 1, c - 1] = jnp.where(first, before[n][1], now[n][0]).astype(jnp.bfloat16)
        before = now
    for t in range(frames):
        smooth_ref[t * cols : (t + 1) * cols, :] = turn_ref[pl.ds(t, cols, stride=frames), :].astype(jnp.bfloat16)


def columns_body(frames, cols, x_ref, a_ref, b_ref, out_ref, edge_ref):
    place, count = lax.axis_index("space"), lax.axis_size("space")
    even = lax.rem(place, 2) == 0
    lowest, highest = place > 0, place < count - 1
    halo = RMAX + REACH

    def raw(c):
        if 0 <= c < cols:
            return x_ref[pl.ds(c, frames, stride=cols), :]
        at = c + cols if c < 0 else c - cols
        rows = pl.ds(at, frames, stride=cols)
        first, second, there = (b_ref, a_ref, lowest) if c < 0 else (a_ref, b_ref, highest)
        value = jnp.where(even, first[rows, :], second[rows, :])
        return jnp.where(there, value, jnp.zeros_like(value))

    order = 0
    for low in (-halo, cols - 2 * REACH):
        held = {}
        for c in range(low, low + halo + 2 * REACH):
            held[c] = raw(c)
            done = c - REACH
            if done >= low + REACH:
                value = blend([held[done + k] for k in range(-REACH, REACH + 1)])
                if done < 0 or done >= cols:
                    value = jnp.where(lowest if done < 0 else highest, value, jnp.zeros_like(value))
                else:
                    slot = done if done < REACH else done - cols + 2 * REACH
                    edge_ref[slot * frames : (slot + 1) * frames, :] = value
                out_ref[order * frames : (order + 1) * frames, :] = value
                order += 1


def placed(frames, cols, edges):
    slots = 2 * REACH
    row = lax.broadcasted_iota(jnp.int32, (frames * cols, slots * frames), 0)
    from_row = lax.broadcasted_iota(jnp.int32, (frames * cols, slots * frames), 1)
    slot, frame = from_row // frames, from_row % frames
    column = jnp.where(slot < REACH, slot, slot + cols - slots)
    pick = jnp.where(row == frame * cols + column, 1.0, 0.0).astype(jnp.bfloat16)
    return jnp.dot(pick, edges, preferred_element_type=jnp.float32).astype(jnp.bfloat16)


def spread_of(smooth):
    wide = LANES // TILE * LANES
    here = lax.broadcasted_iota(jnp.int32, (LANES, wide), 0)
    there = lax.broadcasted_iota(jnp.int32, (LANES, wide), 1)
    wanted = (there // LANES) * TILE + there % TILE
    pick = jnp.where(here == wanted, 1.0, 0.0).astype(jnp.bfloat16)
    return jnp.dot(smooth, pick, preferred_element_type=jnp.float32)


def windows_body(frames, cols, own_ref, low_ref, high_ref, blur_ref, smooth_ref, pairs_ref, rim_ref, tiles_ref, whole_ref, found_ref):
    wide = cols + 2 * RMAX
    edge = RMAX + REACH
    lane = lax.broadcasted_iota(jnp.int32, (frames, LANES), 1)
    first = lane < 2 * TILE
    side = beside(low_ref[...], None if high_ref is None else high_ref[...])
    found_ref[...] = exact_dot(jnp.concatenate([own_ref[...], side], axis=1), blur_ref[...])

    def window(c, n):
        if c == wide:
            return jnp.zeros((frames, LANES), jnp.float32)
        if c == edge or c == wide - edge - 1:
            return rim_ref[0 if c == edge else 1, n]
        at = c if c < edge else c - wide + 2 * edge
        return found_ref[at * frames : (at + 1) * frames, n * LANES : (n + 1) * LANES]

    for begin, end in ((0, edge), (wide - edge - 1, wide)):
        before = None
        for c in range(begin, end + 1):
            now = []
            for n in range(2):
                value = window(c, n)
                now.append((value, pltpu.roll(value, 2 * TILE, 1)))
                if before is not None:
                    low = jnp.where(first, before[n][0], now[n][1])
                    high = jnp.where(first, before[n][1], now[n][0])
                    tiles_ref[2 * n, c - 1] = low.astype(jnp.bfloat16)
                    tiles_ref[2 * n + 1, c - 1] = high.astype(jnp.bfloat16)
            before = now
    for j in range(pairs_ref.shape[0]):
        tiles_ref[j, edge : wide - edge - 1] = pairs_ref[j]
    rows = slice(RMAX * frames, (RMAX + 2 * REACH) * frames)
    edges = own_lanes(found_ref[rows, 0:LANES], found_ref[rows, LANES : 2 * LANES]).astype(jnp.bfloat16)
    whole_ref[...] = smooth_ref[...] + placed(frames, cols, edges)


def sums_body(frames, cols, first, table_ref, tiles_ref, out_ref, turn_ref):
    rows = cols * frames
    for j in range(out_ref.shape[0]):
        pieces = [tiles_ref[first + j, a : a + cols].reshape(rows, LANES) for a in range(0, 2 * RMAX + 1, 2)]
        found = lax.dot_general(
            jnp.concatenate(pieces, axis=1),
            table_ref[...],
            (((1,), (1,)), ((), ())),
            preferred_element_type=jnp.float32,
        )
        for g in range(out_ref.shape[1]):
            turn_ref[j, g] = found[:, g * LANES : (g + 1) * LANES]
            for t in range(frames):
                out_ref[j, g, t * cols : (t + 1) * cols, :] = turn_ref[j, g, pl.ds(t, cols, stride=frames), :]


def later_body(frames, cols, first, table_ref, tiles_ref, whole_ref, earlier_ref, out_ref, spread_ref, turn_ref):
    begun = lax.axis_index("tm") > 0
    rows = frames * cols
    for half, source in enumerate((earlier_ref, whole_ref)):
        value = spread_of(source[...])
        if half == 0:
            value = jnp.where(begun, value, 0.0)
        for j in range(LANES // TILE):
            spread_ref[j, half * rows : (half + 1) * rows, :] = value[:, j * LANES : (j + 1) * LANES]
    sums_body(frames, cols, first, table_ref, tiles_ref, out_ref, turn_ref)


def correlate_body(
    frames, cols, radii, edge_ref, low_ref, high_ref, lag_ref, one_ref, two_ref, blur_ref, inverse_ref, given_ref,
    out_ref, spread_ref, held_ref, sem,
):
    lag_count = lag_ref.shape[1]
    lags = [lag_ref[0, lag] for lag in range(lag_count)]
    tile_count = LANES // TILE
    begun = lax.axis_index("tm") > 0
    del given_ref
    side = beside(low_ref[...], None if high_ref is None else high_ref[...])
    found = exact_dot(jnp.concatenate([edge_ref[...], side], axis=1), blur_ref[...])
    edges = own_lanes(found[:, :LANES], found[:, LANES : 2 * LANES]).astype(jnp.bfloat16)
    rims = jnp.where(begun, spread_of(edges), 0.0)
    for slot in range(2 * REACH):
        column = slot if slot < REACH else slot + cols - 2 * REACH
        for j in range(tile_count):
            value = rims[slot * frames : (slot + 1) * frames, j * LANES : (j + 1) * LANES]
            spread_ref[j, pl.ds(column, frames, stride=cols), :] = value
    lane = lax.broadcasted_iota(jnp.int32, (8, LANES), 1)
    block = [jnp.logical_and(lane >= TILE * j, lane < TILE * (j + 1)) for j in range(tile_count)]
    groups = radii * TILE // LANES
    per = LANES // TILE
    copies = []
    for c in range(0, cols, 8):
        totals = {}
        for j in range(tile_count):
            for t in range(frames):
                found_ref, at = (one_ref, j) if j < one_ref.shape[0] else (two_ref, j - one_ref.shape[0])
                parts = [found_ref[at, g, t * cols + c : t * cols + c + 8, :] for g in range(groups)]
                for lag in range(lag_count):
                    row = (MAXLAG + t - lags[lag]) * cols + c
                    old = spread_ref[j, pl.ds(pl.multiple_of(row, 8), 8), :]
                    for g in range(groups):
                        term = parts[g] * old
                        key = (lag, g, j)
                        totals[key] = totals[key] + term if key in totals else term
        for lag in range(lag_count):
            for g in range(groups):
                for q in range(per):
                    joined = None
                    for j in range(tile_count):
                        piece = totals[(lag, g, j)]
                        shift = (TILE * (j - q)) % LANES
                        piece = pltpu.roll(piece, shift, 1) if shift else piece
                        joined = piece if joined is None else jnp.where(block[j], piece, joined)
                    r = g * per + q
                    held_ref[c // 8, r, lag] = joined * inverse_ref[r : r + 1, :]
        copies.append(pltpu.make_async_copy(held_ref.at[c // 8], out_ref.at[:, :, pl.ds(c, 8), :], sem.at[c // 8]))
        copies[-1].start()
    for copy in copies:
        copy.wait()


def local(doppler, cycle_masks, lag_list):
    frames, cols, rows = doppler.shape
    radii = cycle_masks.shape[0]
    lag_count = lag_list.shape[0]
    wide = cols + 2 * RMAX
    edge = RMAX + REACH
    inner = cols - 2 * REACH
    offsets = 2 * RMAX + 1
    tile_count = rows // TILE
    groups = radii * TILE // LANES
    f32, bf16 = jnp.float32, jnp.bfloat16
    shape = jax.ShapeDtypeStruct

    flat = doppler.reshape(frames * cols, rows)
    count, row_count = lax.axis_size("space"), lax.axis_size("row")
    ring = onward(row_count)

    def across(value):
        low = lax.ppermute(value, "row", ring)
        return [low] if row_count == 2 else [low, lax.ppermute(value, "row", [(b, a) for a, b in ring])]

    def split(refs, lead=1):
        both = 1 if row_count == 2 else 2
        sides = (refs[lead], refs[lead + 1] if both == 2 else None)
        return refs[:lead] + sides + refs[lead + both :]

    one = lax.ppermute(flat, ("space", "row"), pairs(count, 0, row_count))
    two = lax.ppermute(flat, ("space", "row"), pairs(count, 1, row_count))
    near = across(flat)

    def prepare(*refs):
        prepare_body(*refs)

    depth = (offsets + 1) * 2 * TILE
    table, inverse, blur, held = vmem_call(
        prepare,
        [
            shape((radii * TILE, depth), bf16),
            shape((radii, LANES), f32),
            shape((2 * LANES, 2 * LANES), f32),
            shape((frames * cols, rows), f32),
        ],
        scratch=[
            VMEM((offsets + 1, radii, LANES), f32),
            VMEM((offsets, radii, offsets), jnp.int32),
            pltpu.SemaphoreType.DMA((2,)),
        ],
        inputs=2,
        in_space=pltpu.HBM,
    )(*[pltpu.with_memory_space_constraint(a, pltpu.HBM) for a in (jnp.transpose(cycle_masks, (1, 0, 2)), flat)])

    def own(*refs):
        own_body(frames, cols, *split(refs))

    smooth, inner_pairs, rim = vmem_call(
        own,
        [
            shape((frames * cols, rows), bf16),
            shape((tile_count, inner - 1, frames, LANES), bf16),
            shape((2, 2, frames, LANES), f32),
        ],
        scratch=[
            VMEM((inner * frames, 2 * LANES), f32),
            VMEM((inner * frames, 2 * LANES), f32),
            VMEM((cols * frames, LANES), f32),
        ],
        inputs=2 + len(near),
    )(held, *near, blur)
    later = onward(lax.axis_size("tm"))
    earlier = lax.ppermute(smooth, "tm", later)

    def columns(*refs):
        columns_body(frames, cols, *refs)

    blurred, edges = vmem_call(
        columns, [shape((2 * edge * frames, rows), f32), shape((2 * REACH * frames, rows), f32)], inputs=3
    )(held, one, two)

    sides = across(blurred)
    edges = lax.ppermute(edges, "tm", later)

    def windows(*refs):
        windows_body(frames, cols, *split(refs))

    tiles, whole = vmem_call(
        windows,
        [shape((tile_count, wide, frames, LANES), bf16), shape((frames * cols, rows), bf16)],
        scratch=[VMEM((2 * edge * frames, 2 * LANES), f32)],
        inputs=5 + len(sides),
    )(blurred, *sides, blur, smooth, inner_pairs, rim)

    half = tile_count // 2
    sums = shape((half, groups, frames * cols, LANES), f32)
    turn = VMEM((half, groups, cols * frames, LANES), f32)
    flops = tile_count * cols * frames * radii * TILE * depth
    cost = pl.CostEstimate(flops=flops, bytes_accessed=1 << 20, transcendentals=0)

    def products(*refs):
        sums_body(frames, cols, 0, *refs)

    first = vmem_call(products, sums, scratch=[turn], inputs=2, cost=cost)(table, tiles)

    far = across(edges)

    def others(*refs):
        later_body(frames, cols, half, *refs)

    second, spread = vmem_call(
        others,
        [sums, shape((tile_count, 2 * frames * cols, LANES), f32)],
        scratch=[turn],
        inputs=4,
        cost=cost,
    )(table, tiles, whole, earlier)

    def correlate(*refs):
        correlate_body(frames, cols, radii, *split(refs))

    out, _ = vmem_call(
        correlate,
        [shape((radii, lag_count, cols, rows), f32), shape(spread.shape, f32)],
        scratch=[
            VMEM((cols // 8, radii, lag_count, 8, LANES), f32),
            pltpu.SemaphoreType.DMA((cols // 8,)),
        ],
        inputs=7 + len(far),
        out_space=[pl.ANY, VMEM],
        aliases={6 + len(far): 1},
    )(edges, *far, lag_list.reshape(1, lag_count), first, second, blur, inverse, spread)
    return out[None]


def solution(mesh):
    return jax.shard_map(
        local,
        mesh=mesh,
        in_specs=(P("tm", ("patch", "space"), "row"), P(), P()),
        out_specs=P("tm", None, None, ("patch", "space"), "row"),
        check_vma=False,
    )
```

time: 18.8 us -> 19.8 us (1.053)
  the two profiles are of different devices: /device:TPU:0 before, /device:TPU:20 now
where the time goes in v3:
time: 19.8 us; the launch traced here: 19.6 us
  Pallas kernels  8.74 us (44%)
  waiting for transfers between devices  5.77 us (29%)
  starting transfers between devices  5.05 us (26%)
    ppermute x1, waiting for transfers between devices, local(): one = lax.ppermute(flat, ('space', 'row'), pairs(count, 0, row_count))  3.12 us
    pallas_call x1, Pallas kernels, local(): vmem_call(prepare, [shape((radii * TILE, depth), bf16), shape((radii, LAN...  2.15 us
    pallas_call x1, Pallas kernels, local(): vmem_call(correlate, [shape((radii, lag_count, cols, rows), f32), shape(s...  2.11 us
    ppermute x1, starting transfers between devices, local(): one = lax.ppermute(flat, ('space', 'row'), pairs(count, 0, row_count))  1.58 us
    ppermute x1, starting transfers between devices, local(): edges = lax.ppermute(edges, 'tm', later)  1.49 us
    pallas_call x1, Pallas kernels, local(): vmem_call(others, [sums, shape((tile_count, 2 * frames * cols, LANES), f3...  1.48 us
    ppermute x1, starting transfers between devices, local(): earlier = lax.ppermute(smooth, 'tm', later)  1.41 us
    pallas_call x1, Pallas kernels, local(): vmem_call(products, sums, scratch=[turn], inputs=2, cost=cost)(table, tiles)  1.3 us
  transfers between devices with their start and end apart: 7, of which 4 were waited for; matrix products, arithmetic and copies ran while one was open for 0% of the time, Pallas kernels for 33%

profile of v3, /device:TPU:20, one launch (start us, length us, event | category | flops | bytes accessed | tf_op | source)
XLA Modules:
  0.0 19.6 jit_solution(12951964954881503512)
XLA Ops:
  0.0 1.6 %collective-permute-start = (f32[384,128]{1,0:T(8,128)}, f32[384,128]{1,0:T(8,128)S(1)}, u32[]{:S(2)}, u32[]{:S(2)}) collective-permute-start(f32[384,128]{1,0:T(8,128)} %bitcast.5), channel_id=1, source_target_pairs={{0,4},{1,5},{4,0},{5,1},{8,12},{9,13},{12,8},{13,9},{2,6},{3,7},{6... | collective-permute-start | bytes 589832 | tf_op jit(solution)/shard_map/ppermute | solution.py:352
  1.6 0.0 collective-permute-start.1
  1.6 2.1 %shard_map.37 = (bf16[256,2176]{1,0:T(8,128)(2,1)S(1)}, f32[8,128]{1,0:T(8,128)S(1)}, f32[256,256]{1,0:T(8,128)S(1)}, f32[384,128]{1,0:T(8,128)S(1)}) custom-call(s32[33,8,33]{2,1,0:T(8,128)} %bitcast.9, f32[384,128]{1,0:T(8,128)} %bitcast.7), custom_call_target="tpu_custom_call" | custom-call | tf_op jit(solution)/shard_map/pallas_call | solution.py:360
  3.7 3.1 %collective-permute-done.refs_1_ = f32[384,128]{1,0:T(8,128)S(1)} collective-permute-done((f32[384,128]{1,0:T(8,128)}, f32[384,128]{1,0:T(8,128)S(1)}, u32[]{:S(2)}, u32[]{:S(2)}) %collective-permute-start) | collective-permute-done | bytes 196640 | tf_op jit(solution)/shard_map/ppermute | solution.py:352
  6.9 1.3 %collective-permute-done.1.refs_2_ = f32[384,128]{1,0:T(8,128)S(1)} collective-permute-done((f32[384,128]{1,0:T(8,128)}, f32[384,128]{1,0:T(8,128)S(1)}, u32[]{:S(2)}, u32[]{:S(2)}) %collective-permute-start.1) | collective-permute-done | bytes 196640 | tf_op jit(solution)/shard_map/ppermute | solution.py:353
  8.2 0.2 shard_map.38
  8.3 0.1 collective-permute-start.4
  8.4 0.5 %collective-permute-start.5 = (f32[384,128]{1,0:T(8,128)}, f32[384,128]{1,0:T(8,128)S(1)}, u32[]{:S(2)}, u32[]{:S(2)}) collective-permute-start(f32[384,128]{1,0:T(8,128)} %bitcast.8), channel_id=1, source_target_pairs={{0,1},{1,0},{2,3},{3,2},{4,5},{5,4},{6,7},{7,6},{8,9},{9,8},{10,11... | collective-permute-start | bytes 589832 | tf_op jit(solution)/shard_map/ppermute | solution.py:344
  8.9 1.5 %collective-permute-start.2 = (f32[64,128]{1,0:T(8,128)S(1)}, f32[64,128]{1,0:T(8,128)S(1)}, u32[]{:S(2)}, u32[]{:S(2)}) collective-permute-start(f32[64,128]{1,0:T(8,128)S(1)} %get-tuple-element.20), channel_id=1, source_target_pairs={{0,2},{2,0},{1,3},{3,1},{4,6},{6,4},{5,7},{7,5},{8,10},{10,8},{9,1... | collective-permute-start | bytes 98312 | tf_op jit(solution)/shard_map/ppermute | solution.py:405
  10.4 0.0 collective-permute-done.5.refs_1_
  10.4 0.7 %shard_map.39 = (bf16[384,128]{1,0:T(8,128)(2,1)S(1)}, bf16[4,19,16,128]{3,2,1,0:T(8,128)(2,1)S(1)}, f32[2,2,16,128]{3,2,1,0:T(8,128)S(1)}) custom-call(f32[384,128]{1,0:T(8,128)S(1)} %get-tuple-element.19.refs_0_, f32[384,128]{1,0:T(8,128)S(1)} %collective-permute-done.5.refs_1_, f32[256,256]{1,0:T(8,128)S(1)} %get-tuple-element.23.refs_2_.refs_5_), custom_call_target="tpu_custom_call" | custom-call | tf_op jit(solution)/shard_map/pallas_call | solution.py:380
  11.1 1.4 %collective-permute-start.6 = (bf16[384,128]{1,0:T(8,128)(2,1)S(1)}, bf16[384,128]{1,0:T(8,128)(2,1)S(1)}, u32[]{:S(2)}, u32[]{:S(2)}) collective-permute-start(bf16[384,128]{1,0:T(8,128)(2,1)S(1)} %get-tuple-element.24.refs_3_), channel_id=1, source_target_pairs={{0,2},{2,0},{1,3},{3,1},{4,6},{6,4},{5,7},{7,5},{8,10},{10,8},{9,1... | collective-permute-start | bytes 294920 | tf_op jit(solution)/shard_map/ppermute | solution.py:395
  12.5 0.3 %collective-permute-done.2.refs_0_ = f32[64,128]{1,0:T(8,128)S(1)} collective-permute-done((f32[64,128]{1,0:T(8,128)S(1)}, f32[64,128]{1,0:T(8,128)S(1)}, u32[]{:S(2)}, u32[]{:S(2)}) %collective-permute-start.2) | collective-permute-done | bytes 32800 | tf_op jit(solution)/shard_map/ppermute | solution.py:405
  12.8 0.0 collective-permute-start.3
  12.8 0.0 collective-permute-done.4.refs_1_
  12.8 0.8 %shard_map.40 = (bf16[4,56,16,128]{3,2,1,0:T(8,128)(2,1)S(1)}, bf16[384,128]{1,0:T(8,128)(2,1)S(1)}) custom-call(f32[576,128]{1,0:T(8,128)S(1)} %get-tuple-element.22.refs_0_, f32[576,128]{1,0:T(8,128)S(1)} %collective-permute-done.4.refs_1_, f32[256,256]{1,0:T(8,128)S(1)} %get-tuple-element.23.refs_2_.refs_5_, ...), custom_call_target="tpu_custom_call" | custom-call | tf_op jit(solution)/shard_map/pallas_call | solution.py:410
  13.7 1.3 %shard_map.41.refs_3_ = f32[2,2,384,128]{3,2,1,0:T(8,128)S(1)} custom-call(bf16[256,2176]{1,0:T(8,128)(2,1)S(1)} %get-tuple-element.21.refs_0_, bf16[4,56,16,128]{3,2,1,0:T(8,128)(2,1)S(1)} %get-tuple-element.27.refs_1_), custom_call_target="tpu_custom_call" | custom-call | flops 855638016 | bytes 1048576 | tf_op jit(solution)/shard_map/pallas_call | solution.py:426
  15.0 1.1 %collective-permute-done.6.refs_3_ = bf16[384,128]{1,0:T(8,128)(2,1)S(1)} collective-permute-done((bf16[384,128]{1,0:T(8,128)(2,1)S(1)}, bf16[384,128]{1,0:T(8,128)(2,1)S(1)}, u32[]{:S(2)}, u32[]{:S(2)}) %collective-permute-start.6) | collective-permute-done | bytes 98336 | tf_op jit(solution)/shard_map/ppermute | solution.py:395
  16.0 0.0 copy-start
  16.0 1.5 %shard_map.42 = (f32[2,2,384,128]{3,2,1,0:T(8,128)S(1)}, f32[4,768,128]{2,1,0:T(8,128)S(1)}) custom-call(bf16[256,2176]{1,0:T(8,128)(2,1)S(1)} %get-tuple-element.21.refs_0_, bf16[4,56,16,128]{3,2,1,0:T(8,128)(2,1)S(1)} %get-tuple-element.27.refs_1_, bf16[384,128]{1,0:T(8,128)(2,1)S(1)} %get-tuple-element.28.refs_2_, ...), custom_call_target="tpu_custom_call" | custom-call | flops 855638016 | bytes 1048576 | tf_op jit(solution)/shard_map/pallas_call | solution.py:433
  17.5 0.0 collective-permute-done.3.refs_1_
  17.5 0.0 copy-done
  17.5 2.1 %shard_map.43 = (f32[8,4,24,128]{3,2,1,0:T(8,128)}, f32[4,768,128]{2,1,0:T(8,128)S(1)}) custom-call(f32[64,128]{1,0:T(8,128)S(1)} %collective-permute-done.2.refs_0_, f32[64,128]{1,0:T(8,128)S(1)} %collective-permute-done.3.refs_1_, s32[1,4]{1,0:T(1,128)S(1)} %bitcast.4, f32[2,2,384,128]{3,2,1,0:T(8,128)S(1)} %shard_map.41.refs_3_, ...), custom_call_target="tpu_custom_call", output_to_operand_aliasing={{1}: (7, {})} | custom-call | tf_op jit(solution)/shard_map/pallas_call | solution.py:444
Async XLA Ops:
  0.0 6.9 %collective-permute-start = (f32[384,128]{1,0:T(8,128)}, f32[384,128]{1,0:T(8,128)S(1)}, u32[]{:S(2)}, u32[]{:S(2)}) collective-permute-start(f32[384,128]{1,0:T(8,128)} %bitcast.5), channel_id=1, source_target_pairs={{0,4},{1,5},{4,0},{5,1},{8,12},{9,13},{12,8},{13,9},{2,6},{3,7},{6... | collective-permute-start | bytes 589832 | tf_op jit(solution)/shard_map/ppermute | solution.py:352
  1.6 6.6 %collective-permute-start.1 = (f32[384,128]{1,0:T(8,128)}, f32[384,128]{1,0:T(8,128)S(1)}, u32[]{:S(2)}, u32[]{:S(2)}) collective-permute-start(f32[384,128]{1,0:T(8,128)} %bitcast.6), channel_id=1, source_target_pairs={{0,1},{1,0},{4,8},{5,9},{8,4},{9,5},{12,13},{13,12},{2,3},{3,2},{6... | collective-permute-start | bytes 589832 | tf_op jit(solution)/shard_map/ppermute | solution.py:353
  8.3 4.5 %collective-permute-start.4 = (f32[576,128]{1,0:T(8,128)S(1)}, f32[576,128]{1,0:T(8,128)S(1)}, u32[]{:S(2)}, u32[]{:S(2)}) collective-permute-start(f32[576,128]{1,0:T(8,128)S(1)} %get-tuple-element.22.refs_0_), channel_id=1, source_target_pairs={{0,1},{1,0},{2,3},{3,2},{4,5},{5,4},{6,7},{7,6},{8,9},{9,8},{10,11... | collective-permute-start | bytes 884744 | tf_op jit(solution)/shard_map/ppermute | solution.py:344
  8.4 2.0 %collective-permute-start.5 = (f32[384,128]{1,0:T(8,128)}, f32[384,128]{1,0:T(8,128)S(1)}, u32[]{:S(2)}, u32[]{:S(2)}) collective-permute-start(f32[384,128]{1,0:T(8,128)} %bitcast.8), channel_id=1, source_target_pairs={{0,1},{1,0},{2,3},{3,2},{4,5},{5,4},{6,7},{7,6},{8,9},{9,8},{10,11... | collective-permute-start | bytes 589832 | tf_op jit(solution)/shard_map/ppermute | solution.py:344
  8.9 3.9 %collective-permute-start.2 = (f32[64,128]{1,0:T(8,128)S(1)}, f32[64,128]{1,0:T(8,128)S(1)}, u32[]{:S(2)}, u32[]{:S(2)}) collective-permute-start(f32[64,128]{1,0:T(8,128)S(1)} %get-tuple-element.20), channel_id=1, source_target_pairs={{0,2},{2,0},{1,3},{3,1},{4,6},{6,4},{5,7},{7,5},{8,10},{10,8},{9,1... | collective-permute-start | bytes 98312 | tf_op jit(solution)/shard_map/ppermute | solution.py:405
  11.1 4.9 %collective-permute-start.6 = (bf16[384,128]{1,0:T(8,128)(2,1)S(1)}, bf16[384,128]{1,0:T(8,128)(2,1)S(1)}, u32[]{:S(2)}, u32[]{:S(2)}) collective-permute-start(bf16[384,128]{1,0:T(8,128)(2,1)S(1)} %get-tuple-element.24.refs_3_), channel_id=1, source_target_pairs={{0,2},{2,0},{1,3},{3,1},{4,6},{6,4},{5,7},{7,5},{8,10},{10,8},{9,1... | collective-permute-start | bytes 294920 | tf_op jit(solution)/shard_map/ppermute | solution.py:395
  12.8 4.7 %collective-permute-start.3 = (f32[64,128]{1,0:T(8,128)S(1)}, f32[64,128]{1,0:T(8,128)S(1)}, u32[]{:S(2)}, u32[]{:S(2)}) collective-permute-start(f32[64,128]{1,0:T(8,128)S(1)} %collective-permute-done.2.refs_0_), channel_id=1, source_target_pairs={{0,1},{1,0},{2,3},{3,2},{4,5},{5,4},{6,7},{7,6},{8,9},{9,8},{10,11... | collective-permute-start | bytes 98312 | tf_op jit(solution)/shard_map/ppermute | solution.py:344
  16.0 1.5 %copy-start = (s32[4]{0:T(128)S(1)}, s32[4]{0:T(128)}, u32[]{:S(2)}) copy-start(s32[4]{0:T(128)} %param.5) | copy-start | bytes 52

commit v4 on v3

--- a/solution.py
+++ b/solution.py
@@ -56,14 +56,14 @@
     return c * parts[2] + b * (parts[1] + parts[3]) + a * (parts[0] + parts[4])
 
 
-def prepare_body(masks_hbm, x_hbm, table_ref, inverse_ref, blur_ref, x_ref, wide_ref, masks_ref, sem):
-    masks_in = pltpu.make_async_copy(masks_hbm, masks_ref, sem.at[0])
-    masks_in.start()
-    x_in = pltpu.make_async_copy(x_hbm, x_ref, sem.at[1])
-    x_in.start()
-    offsets, radii, _ = masks_ref.shape
+def prepare_body(masks_hbm, x_hbm, blur_ref, x_ref, masks_ref, sem):
+    copies = [
+        pltpu.make_async_copy(x_hbm, x_ref, sem.at[0]),
+        pltpu.make_async_copy(masks_hbm, masks_ref, sem.at[1]),
+    ]
+    for copy in copies:
+        copy.start()
     span = 2 * TILE
-
     place, count = lax.axis_index("row"), lax.axis_size("row")
     source = lax.broadcasted_iota(jnp.int32, (LANES, LANES), 0)
     target = lax.broadcasted_iota(jnp.int32, (LANES, LANES), 1)
@@ -82,20 +82,23 @@
                 weight = jnp.where(apart == k, gaussian_taps[REACH + k], weight)
             weight = jnp.where(jnp.logical_and(held(origin), held(landing)), weight, 0.0)
             blur_ref[half * LANES : (half + 1) * LANES, n * LANES : (n + 1) * LANES] = weight
-
+    for copy in copies:
+        copy.wait()
+
+
+def table_body(masks_ref, table_ref, inverse_ref, wide_ref):
+    offsets, radii, _ = masks_ref.shape
     wide_ref[...] = jnp.zeros_like(wide_ref)
-    masks_in.wait()
     wide_ref[0:offsets, :, 0:offsets] = masks_ref[...].astype(jnp.float32)
     total = jnp.zeros((radii, LANES), jnp.float32)
     for k in range(wide_ref.shape[0] // 2):
-        pair = wide_ref[2 * k] + pltpu.roll(wide_ref[2 * k + 1], span, 1)
+        pair = wide_ref[2 * k] + pltpu.roll(wide_ref[2 * k + 1], 2 * TILE, 1)
         total = total + pair
         for r in range(radii):
             rows = jnp.broadcast_to(pair[r : r + 1, :], (TILE, LANES))
             turned = pltpu.roll(rows, 0, 1, stride=1, stride_axis=0)
             table_ref[r * TILE : (r + 1) * TILE, k * LANES : (k + 1) * LANES] = turned.astype(jnp.bfloat16)
     inverse_ref[...] = jnp.broadcast_to(1.0 / jnp.sum(total, axis=1, keepdims=True), (radii, LANES))
-    x_in.wait()
 
 
 def beside(low, high):
@@ -242,8 +245,8 @@
     whole_ref[...] = smooth_ref[...] + placed(frames, cols, edges)
 
 
-def sums_body(frames, cols, first, table_ref, tiles_ref, out_ref, turn_ref):
-    rows = cols * frames
+def sums_body(frames, cols, first, table_ref, tiles_ref, out_ref):
+    rows, pitch = cols * frames, frames + 8
     for j in range(out_ref.shape[0]):
         pieces = [tiles_ref[first + j, a : a + cols].reshape(rows, LANES) for a in range(0, 2 * RMAX + 1, 2)]
         found = lax.dot_general(
@@ -253,74 +256,117 @@
             preferred_element_type=jnp.float32,
         )
         for g in range(out_ref.shape[1]):
-            turn_ref[j, g] = found[:, g * LANES : (g + 1) * LANES]
-            for t in range(frames):
-                out_ref[j, g, t * cols : (t + 1) * cols, :] = turn_ref[j, g, pl.ds(t, cols, stride=frames), :]
-
-
-def later_body(frames, cols, first, table_ref, tiles_ref, whole_ref, earlier_ref, out_ref, spread_ref, turn_ref):
+            for c in range(cols):
+                value = found[c * frames : (c + 1) * frames, g * LANES : (g + 1) * LANES]
+                out_ref[j, g, c * pitch : c * pitch + frames, :] = value
+
+
+def correlate_block(frames, cols, n, lags, sources, spread_ref, inverse_ref, total_ref, held):
+    groups, pitch, per = total_ref.shape[2], frames + 8, LANES // TILE
+    tile_count = len(sources)
+    lane = lax.broadcasted_iota(jnp.int32, (8, LANES), 1)
+    block = [jnp.logical_and(lane >= TILE * j, lane < TILE * (j + 1)) for j in range(tile_count)]
+    c = n * 8
+    for j, (found_ref, at) in enumerate(sources):
+        totals = {}
+        for t in range(frames):
+            parts = [found_ref[at, g, pl.ds(c * pitch + t, 8, stride=pitch), :] for g in range(groups)]
+            for lag in range(len(lags)):
+                row = (MAXLAG - lags[lag]) * cols + c + t * cols
+                old = spread_ref[j, pl.ds(pl.multiple_of(row, 8), 8), :]
+                for g in range(groups):
+                    term = parts[g] * old
+                    key = (lag, g)
+                    totals[key] = totals[key] + term if key in totals else term
+        for lag in range(len(lags)):
+            for g in range(groups):
+                total_ref[j, lag, g] = totals[(lag, g)]
+    for lag in range(len(lags)):
+        for g in range(groups):
+            pieces = [total_ref[j, lag, g] for j in range(tile_count)]
+            for q in range(per):
+                joined = None
+                for j in range(tile_count):
+                    shift = (TILE * (j - q)) % LANES
+                    piece = pltpu.roll(pieces[j], shift, 1) if shift else pieces[j]
+                    joined = piece if joined is None else jnp.where(block[j], piece, joined)
+                r = g * per + q
+                held[r, lag] = joined * inverse_ref[r : r + 1, :]
+
+
+def read_lags(lag_ref):
+    return [lag_ref[0, lag] for lag in range(lag_ref.shape[1])]
+
+
+def later_body(
+    frames, cols, table_ref, tiles_ref, whole_ref, earlier_ref, lag_ref, inverse_ref, early_ref,
+    out_ref, spread_ref, held_ref, total_ref,
+):
     begun = lax.axis_index("tm") > 0
-    rows = frames * cols
+    rows, done = frames * cols, early_ref.shape[0]
     for half, source in enumerate((earlier_ref, whole_ref)):
         value = spread_of(source[...])
         if half == 0:
             value = jnp.where(begun, value, 0.0)
         for j in range(LANES // TILE):
             spread_ref[j, half * rows : (half + 1) * rows, :] = value[:, j * LANES : (j + 1) * LANES]
-    sums_body(frames, cols, first, table_ref, tiles_ref, out_ref, turn_ref)
+    sums_body(frames, cols, done, table_ref, tiles_ref, out_ref)
+    sources = [(early_ref, j) for j in range(done)] + [(out_ref, j) for j in range(out_ref.shape[0])]
+    lags = read_lags(lag_ref)
+    for n in range(held_ref.shape[0]):
+        correlate_block(frames, cols, n + 1, lags, sources, spread_ref, inverse_ref, total_ref, held_ref.at[n])
 
 
 def correlate_body(
-    frames, cols, radii, edge_ref, low_ref, high_ref, lag_ref, one_ref, two_ref, blur_ref, inverse_ref, given_ref,
-    out_ref, spread_ref, held_ref, sem,
+    frames, cols, edge_ref, low_ref, high_ref, lag_ref, early_ref, late_ref, middle_ref, inverse_ref, given_ref,
+    out_ref, spread_ref, held_ref, total_ref, sem,
 ):
-    lag_count = lag_ref.shape[1]
-    lags = [lag_ref[0, lag] for lag in range(lag_count)]
+    del given_ref
+    blocks = cols // 8
+
+    def send(source, n):
+        rows = pl.ds(pl.multiple_of(n * 8, 8), 8)
+        return pltpu.make_async_copy(source, out_ref.at[:, :, rows, :], sem.at[n])
+
+    for n in range(blocks - 2):
+        send(middle_ref.at[n], n + 1).start()
     tile_count = LANES // TILE
     begun = lax.axis_index("tm") > 0
-    del given_ref
     side = beside(low_ref[...], None if high_ref is None else high_ref[...])
-    found = exact_dot(jnp.concatenate([edge_ref[...], side], axis=1), blur_ref[...])
-    edges = own_lanes(found[:, :LANES], found[:, LANES : 2 * LANES]).astype(jnp.bfloat16)
-    rims = jnp.where(begun, spread_of(edges), 0.0)
-    for slot in range(2 * REACH):
-        column = slot if slot < REACH else slot + cols - 2 * REACH
-        for j in range(tile_count):
-            value = rims[slot * frames : (slot + 1) * frames, j * LANES : (j + 1) * LANES]
-            spread_ref[j, pl.ds(column, frames, stride=cols), :] = value
-    lane = lax.broadcasted_iota(jnp.int32, (8, LANES), 1)
-    block = [jnp.logical_and(lane >= TILE * j, lane < TILE * (j + 1)) for j in range(tile_count)]
-    groups = radii * TILE // LANES
-    per = LANES // TILE
-    copies = []
-    for c in range(0, cols, 8):
-        totals = {}
-        for j in range(tile_count):
-            for t in range(frames):
-                found_ref, at = (one_ref, j) if j < one_ref.shape[0] else (two_ref, j - one_ref.shape[0])
-                parts = [found_ref[at, g, t * cols + c : t * cols + c + 8, :] for g in range(groups)]
-                for lag in range(lag_count):
-                    row = (MAXLAG + t - lags[lag]) * cols + c
-                    old = spread_ref[j, pl.ds(pl.multiple_of(row, 8), 8), :]
-                    for g in range(groups):
-                        term = parts[g] * old
-                        key = (lag, g, j)
-                        totals[key] = totals[key] + term if key in totals else term
-        for lag in range(lag_count):
-            for g in range(groups):
-                for q in range(per):
-                    joined = None
-                    for j in range(tile_count):
-                        piece = totals[(lag, g, j)]
-                        shift = (TILE * (j - q)) % LANES
-                        piece = pltpu.roll(piece, shift, 1) if shift else piece
-                        joined = piece if joined is None else jnp.where(block[j], piece, joined)
-                    r = g * per + q
-                    held_ref[c // 8, r, lag] = joined * inverse_ref[r : r + 1, :]
-        copies.append(pltpu.make_async_copy(held_ref.at[c // 8], out_ref.at[:, :, pl.ds(c, 8), :], sem.at[c // 8]))
-        copies[-1].start()
-    for copy in copies:
-        copy.wait()
+    place, count = lax.axis_index("row"), lax.axis_size("row")
+    spot = lax.broadcasted_iota(jnp.int32, side.shape, 1)
+    halo = spot < LANES // 2
+    there = jnp.logical_or(jnp.logical_and(halo, place < count - 1), jnp.logical_and(jnp.logical_not(halo), place > 0))
+    side = jnp.where(there, side, 0.0)
+    shifted = []
+    for k in range(-REACH, REACH + 1):
+        near, far = edge_ref[...], side
+        if k:
+            near, far = pltpu.roll(near, (-k) % LANES, 1), pltpu.roll(far, (-k) % LANES, 1)
+            near = jnp.where(spot >= LANES - k if k > 0 else spot < -k, far, near)
+        shifted.append(near)
+    rims = jnp.where(begun, blend(shifted).astype(jnp.bfloat16).astype(jnp.float32), 0.0)
+    for j in range(tile_count):
+        tile = jnp.where(jnp.logical_and(spot >= TILE * j, spot < TILE * (j + 1)), rims, 0.0)
+        shift = TILE
+        while shift < LANES:
+            tile = tile + pltpu.roll(tile, shift, 1)
+            shift *= 2
+        for slot in range(2 * REACH):
+            column = slot if slot < REACH else slot + cols - 2 * REACH
+            spread_ref[j, pl.ds(column, frames, stride=cols), :] = tile[slot * frames : (slot + 1) * frames, :]
+    sources = [(early_ref, j) for j in range(early_ref.shape[0])] + [(late_ref, j) for j in range(late_ref.shape[0])]
+    lags = read_lags(lag_ref)
+
+    def one_end(end, carry):
+        n = end * (blocks - 1)
+        correlate_block(frames, cols, n, lags, sources, spread_ref, inverse_ref, total_ref, held_ref.at[end])
+        send(held_ref.at[end], n).start()
+        return carry
+
+    lax.fori_loop(0, 2, one_end, 0)
+    for n in range(blocks):
+        send(held_ref.at[0], n).wait()
 
 
 def local(doppler, cycle_masks, lag_list):
@@ -353,26 +399,19 @@
     two = lax.ppermute(flat, ("space", "row"), pairs(count, 1, row_count))
     near = across(flat)
 
-    def prepare(*refs):
-        prepare_body(*refs)
-
     depth = (offsets + 1) * 2 * TILE
-    table, inverse, blur, held = vmem_call(
-        prepare,
+    masks = jnp.transpose(cycle_masks, (1, 0, 2))
+    blur, held, masks = vmem_call(
+        prepare_body,
         [
-            shape((radii * TILE, depth), bf16),
-            shape((radii, LANES), f32),
             shape((2 * LANES, 2 * LANES), f32),
             shape((frames * cols, rows), f32),
+            shape((offsets, radii, offsets), jnp.int32),
         ],
-        scratch=[
-            VMEM((offsets + 1, radii, LANES), f32),
-            VMEM((offsets, radii, offsets), jnp.int32),
-            pltpu.SemaphoreType.DMA((2,)),
-        ],
+        scratch=[pltpu.SemaphoreType.DMA((2,))],
         inputs=2,
         in_space=pltpu.HBM,
-    )(*[pltpu.with_memory_space_constraint(a, pltpu.HBM) for a in (jnp.transpose(cycle_masks, (1, 0, 2)), flat)])
+    )(*[pltpu.with_memory_space_constraint(value, pltpu.HBM) for value in (masks, flat)])
 
     def own(*refs):
         own_body(frames, cols, *split(refs))
@@ -394,6 +433,12 @@
     later = onward(lax.axis_size("tm"))
     earlier = lax.ppermute(smooth, "tm", later)
 
+    table, inverse = vmem_call(
+        table_body,
+        [shape((radii * TILE, depth), bf16), shape((radii, LANES), f32)],
+        scratch=[VMEM((offsets + 1, radii, LANES), f32)],
+    )(masks)
+
     def columns(*refs):
         columns_body(frames, cols, *refs)
 
@@ -414,44 +459,54 @@
         inputs=5 + len(sides),
     )(blurred, *sides, blur, smooth, inner_pairs, rim)
 
-    half = tile_count // 2
-    sums = shape((half, groups, frames * cols, LANES), f32)
-    turn = VMEM((half, groups, cols * frames, LANES), f32)
-    flops = tile_count * cols * frames * radii * TILE * depth
-    cost = pl.CostEstimate(flops=flops, bytes_accessed=1 << 20, transcendentals=0)
+    blocks = cols // 8
+    total = VMEM((tile_count, lag_count, groups, 8, LANES), f32)
+    lags = lag_list.reshape(1, lag_count)
+
+    def sums_of(count):
+        flops = 2 * count * cols * frames * radii * TILE * depth
+        cost = pl.CostEstimate(flops=flops, bytes_accessed=1 << 20, transcendentals=0)
+        return shape((count, groups, cols * (frames + 8), LANES), f32), cost
 
     def products(*refs):
         sums_body(frames, cols, 0, *refs)
 
-    first = vmem_call(products, sums, scratch=[turn], inputs=2, cost=cost)(table, tiles)
+    sums, cost = sums_of(tile_count - 1)
+    early = vmem_call(products, sums, inputs=2, cost=cost)(table, tiles)
 
     far = across(edges)
 
     def others(*refs):
-        later_body(frames, cols, half, *refs)
-
-    second, spread = vmem_call(
+        later_body(frames, cols, *refs)
+
+    sums, cost = sums_of(1)
+    late, spread, middle = vmem_call(
         others,
-        [sums, shape((tile_count, 2 * frames * cols, LANES), f32)],
-        scratch=[turn],
-        inputs=4,
+        [
+            sums,
+            shape((tile_count, 2 * frames * cols, LANES), f32),
+            shape((blocks - 2, radii, lag_count, 8, LANES), f32),
+        ],
+        scratch=[total],
+        inputs=7,
         cost=cost,
-    )(table, tiles, whole, earlier)
+    )(table, tiles, whole, earlier, lags, inverse, early)
 
     def correlate(*refs):
-        correlate_body(frames, cols, radii, *split(refs))
+        correlate_body(frames, cols, *split(refs))
 
     out, _ = vmem_call(
         correlate,
         [shape((radii, lag_count, cols, rows), f32), shape(spread.shape, f32)],
         scratch=[
-            VMEM((cols // 8, radii, lag_count, 8, LANES), f32),
-            pltpu.SemaphoreType.DMA((cols // 8,)),
+            VMEM((2, radii, lag_count, 8, LANES), f32),
+            total,
+            pltpu.SemaphoreType.DMA((blocks,)),
         ],
         inputs=7 + len(far),
         out_space=[pl.ANY, VMEM],
         aliases={6 + len(far): 1},
-    )(edges, *far, lag_list.reshape(1, lag_count), first, second, blur, inverse, spread)
+    )(edges, *far, lags, early, late, middle, inverse, spread)
     return out[None]
 
 

time: 19.8 us -> 20.1 us (1.015)
  waiting for transfers between devices: 5.77 us -> 7.19 us
  starting transfers between devices: 5.05 us -> 4.24 us
  Pallas kernels: 8.74 us -> 8.27 us
    ppermute x1, waiting for transfers between devices: 3.12 us -> 4.25 us  [local(): one = lax.ppermute(flat, ('space', 'row'), pairs(count, 0, row_count))]
    ppermute x1, starting transfers between devices: 1.41 us -> 0.6 us  [local(): earlier = lax.ppermute(smooth, 'tm', later)]
    ppermute x1, waiting for transfers between devices: 1.06 us -> 1.63 us  [local(): earlier = lax.ppermute(smooth, 'tm', later)]
    pallas_call x1, Pallas kernels: 2.11 us -> 1.67 us  [local(): vmem_call(correlate, [shape((radii, lag_count, cols, rows), f32), shape(s...]
    pallas_call x1, Pallas kernels: 1.48 us -> 1.07 us  [local(): vmem_call(others, [sums, shape((tile_count, 2 * frames * cols, LANES), f3...]
    pallas_call x2 -> x3, Pallas kernels: 3.45 us -> 3.82 us  [the longest x1 1.57 us: local(): early = vmem_call(products, sums, inputs=2, cost=cost)(table, tiles)]
    ppermute x1, waiting for transfers between devices: 0.29 us -> 0.01 us  [local(): edges = lax.ppermute(edges, 'tm', later)]
  transfers between devices with their start and end apart: 7 -> 7, of which waited for: 4 -> 3; matrix products, arithmetic and copies ran while one was open for 0% -> 0% of each run, Pallas kernels for 33% -> 33%
where the time goes in v4:
time: 20.1 us; the launch traced here: 19.8 us
  Pallas kernels  8.27 us (41%)
  waiting for transfers between devices  7.19 us (36%)
  starting transfers between devices  4.24 us (21%)
    ppermute x1, waiting for transfers between devices, local(): one = lax.ppermute(flat, ('space', 'row'), pairs(count, 0, row_count))  4.25 us
    pallas_call x1, Pallas kernels, local(): vmem_call(correlate, [shape((radii, lag_count, cols, rows), f32), shape(s...  1.67 us
    ppermute x1, waiting for transfers between devices, local(): earlier = lax.ppermute(smooth, 'tm', later)  1.63 us
    ppermute x1, starting transfers between devices, local(): one = lax.ppermute(flat, ('space', 'row'), pairs(count, 0, row_count))  1.58 us
    pallas_call x1, Pallas kernels, local(): early = vmem_call(products, sums, inputs=2, cost=cost)(table, tiles)  1.57 us
    ppermute x1, starting transfers between devices, local(): edges = lax.ppermute(edges, 'tm', later)  1.49 us
    ppermute x1, waiting for transfers between devices, local(): two = lax.ppermute(flat, ('space', 'row'), pairs(count, 1, row_count))  1.3 us
    pallas_call x1, Pallas kernels, local(): vmem_call(table_body, [shape((radii * TILE, depth), bf16), shape((radii,...  1.23 us
  transfers between devices with their start and end apart: 7, of which 3 were waited for; matrix products, arithmetic and copies ran while one was open for 0% of the time, Pallas kernels for 33%

profile of v4, /device:TPU:20, one launch (start us, length us, event | category | flops | bytes accessed | tf_op | source)
XLA Modules:
  0.0 19.8 jit_solution(14042386282119471079)
XLA Ops:
  0.0 1.6 %collective-permute-start = (f32[384,128]{1,0:T(8,128)}, f32[384,128]{1,0:T(8,128)S(1)}, u32[]{:S(2)}, u32[]{:S(2)}) collective-permute-start(f32[384,128]{1,0:T(8,128)} %bitcast.6), channel_id=1, source_target_pairs={{0,4},{1,5},{4,0},{5,1},{8,12},{9,13},{12,8},{13,9},{2,6},{3,7},{6... | collective-permute-start | bytes 589832 | tf_op jit(solution)/shard_map/ppermute | solution.py:398
  1.6 0.0 collective-permute-start.1
  1.6 1.0 %shard_map.37 = (f32[256,256]{1,0:T(8,128)S(1)}, f32[384,128]{1,0:T(8,128)S(1)}, s32[33,8,33]{2,1,0:T(8,128)S(1)}) custom-call(s32[33,8,33]{2,1,0:T(8,128)} %bitcast.10, f32[384,128]{1,0:T(8,128)} %bitcast.8), custom_call_target="tpu_custom_call" | custom-call | tf_op jit(solution)/shard_map/pallas_call | solution.py:404
  2.6 4.2 %collective-permute-done.refs_1_ = f32[384,128]{1,0:T(8,128)S(1)} collective-permute-done((f32[384,128]{1,0:T(8,128)}, f32[384,128]{1,0:T(8,128)S(1)}, u32[]{:S(2)}, u32[]{:S(2)}) %collective-permute-start) | collective-permute-done | bytes 196640 | tf_op jit(solution)/shard_map/ppermute | solution.py:398
  6.9 1.3 %collective-permute-done.1.refs_2_ = f32[384,128]{1,0:T(8,128)S(1)} collective-permute-done((f32[384,128]{1,0:T(8,128)}, f32[384,128]{1,0:T(8,128)S(1)}, u32[]{:S(2)}, u32[]{:S(2)}) %collective-permute-start.1) | collective-permute-done | bytes 196640 | tf_op jit(solution)/shard_map/ppermute | solution.py:399
  8.2 0.2 shard_map.38
  8.3 0.1 collective-permute-start.4
  8.4 0.5 %collective-permute-start.5 = (f32[384,128]{1,0:T(8,128)}, f32[384,128]{1,0:T(8,128)S(1)}, u32[]{:S(2)}, u32[]{:S(2)}) collective-permute-start(f32[384,128]{1,0:T(8,128)} %bitcast.9), channel_id=1, source_target_pairs={{0,1},{1,0},{2,3},{3,2},{4,5},{5,4},{6,7},{7,6},{8,9},{9,8},{10,11... | collective-permute-start | bytes 589832 | tf_op jit(solution)/shard_map/ppermute | solution.py:390
  8.9 1.5 %collective-permute-start.2 = (f32[64,128]{1,0:T(8,128)S(1)}, f32[64,128]{1,0:T(8,128)S(1)}, u32[]{:S(2)}, u32[]{:S(2)}) collective-permute-start(f32[64,128]{1,0:T(8,128)S(1)} %get-tuple-element.22), channel_id=1, source_target_pairs={{0,2},{2,0},{1,3},{3,1},{4,6},{6,4},{5,7},{7,5},{8,10},{10,8},{9,1... | collective-permute-start | bytes 98312 | tf_op jit(solution)/shard_map/ppermute | solution.py:450
  10.4 1.2 %shard_map.39 = (bf16[256,2176]{1,0:T(8,128)(2,1)S(1)}, f32[8,128]{1,0:T(8,128)S(1)}) custom-call(s32[33,8,33]{2,1,0:T(8,128)S(1)} %get-tuple-element.23.masks_ref), custom_call_target="tpu_custom_call" | custom-call | tf_op jit(solution)/shard_map/pallas_call | solution.py:436
  11.6 0.0 collective-permute-done.5.refs_1_
  11.6 0.7 %shard_map.40 = (bf16[384,128]{1,0:T(8,128)(2,1)S(1)}, bf16[4,19,16,128]{3,2,1,0:T(8,128)(2,1)S(1)}, f32[2,2,16,128]{3,2,1,0:T(8,128)S(1)}) custom-call(f32[384,128]{1,0:T(8,128)S(1)} %get-tuple-element.21.refs_0_, f32[384,128]{1,0:T(8,128)S(1)} %collective-permute-done.5.refs_1_, f32[256,256]{1,0:T(8,128)S(1)} %get-tuple-element.26.refs_2_), custom_call_target="tpu_custom_call" | custom-call | tf_op jit(solution)/shard_map/pallas_call | solution.py:419
  12.4 0.6 %collective-permute-start.6 = (bf16[384,128]{1,0:T(8,128)(2,1)S(1)}, bf16[384,128]{1,0:T(8,128)(2,1)S(1)}, u32[]{:S(2)}, u32[]{:S(2)}) collective-permute-start(bf16[384,128]{1,0:T(8,128)(2,1)S(1)} %get-tuple-element.27.refs_3_), channel_id=1, source_target_pairs={{0,2},{2,0},{1,3},{3,1},{4,6},{6,4},{5,7},{7,5},{8,10},{10,8},{9,1... | collective-permute-start | bytes 294920 | tf_op jit(solution)/shard_map/ppermute | solution.py:434
  13.0 0.0 collective-permute-done.2.refs_0_
  13.0 0.0 collective-permute-start.3
  13.0 0.0 collective-permute-done.4.refs_1_
  13.0 0.8 %shard_map.41 = (bf16[4,56,16,128]{3,2,1,0:T(8,128)(2,1)S(1)}, bf16[384,128]{1,0:T(8,128)(2,1)S(1)}) custom-call(f32[576,128]{1,0:T(8,128)S(1)} %get-tuple-element.25.refs_0_, f32[576,128]{1,0:T(8,128)S(1)} %collective-permute-done.4.refs_1_, f32[256,256]{1,0:T(8,128)S(1)} %get-tuple-element.26.refs_2_, bf16[384,128]{1,0:T(8,128)(2,1)S(1)} %get-tuple-element.27.refs_3_, ...), custom_call_target="tpu_custom_call" | custom-call | tf_op jit(solution)/shard_map/pallas_call | solution.py:455
  13.8 0.0 copy-start
  13.8 1.6 %shard_map.42.refs_6_.refs_3_ = f32[3,2,576,128]{3,2,1,0:T(8,128)S(1)} custom-call(bf16[256,2176]{1,0:T(8,128)(2,1)S(1)} %get-tuple-element.24.refs_0_, bf16[4,56,16,128]{3,2,1,0:T(8,128)(2,1)S(1)} %get-tuple-element.30.refs_1_), custom_call_target="tpu_custom_call" | custom-call | flops 1283457024 | bytes 1048576 | tf_op jit(solution)/shard_map/pallas_call | solution.py:475
  15.4 1.6 %collective-permute-done.6.refs_3_ = bf16[384,128]{1,0:T(8,128)(2,1)S(1)} collective-permute-done((bf16[384,128]{1,0:T(8,128)(2,1)S(1)}, bf16[384,128]{1,0:T(8,128)(2,1)S(1)}, u32[]{:S(2)}, u32[]{:S(2)}) %collective-permute-start.6) | collective-permute-done | bytes 98336 | tf_op jit(solution)/shard_map/ppermute | solution.py:434
  17.0 0.0 copy-done
  17.0 1.1 %shard_map.43 = (f32[1,2,576,128]{3,2,1,0:T(8,128)S(1)}, f32[4,768,128]{2,1,0:T(8,128)S(1)}, f32[1,8,4,8,128]{4,3,2,1,0:T(8,128)S(1)}) custom-call(bf16[256,2176]{1,0:T(8,128)(2,1)S(1)} %get-tuple-element.24.refs_0_, bf16[4,56,16,128]{3,2,1,0:T(8,128)(2,1)S(1)} %get-tuple-element.30.refs_1_, bf16[384,128]{1,0:T(8,128)(2,1)S(1)} %get-tuple-element.31.refs_2_, ...), custom_call_target="tpu_custom_call" | custom-call | flops 427819008 | bytes 1048576 | tf_op jit(solution)/shard_map/pallas_call | solution.py:483
  18.1 0.0 collective-permute-done.3.refs_1_
  18.1 1.7 %shard_map.44 = (f32[8,4,24,128]{3,2,1,0:T(8,128)}, f32[4,768,128]{2,1,0:T(8,128)S(1)}) custom-call(f32[64,128]{1,0:T(8,128)S(1)} %collective-permute-done.2.refs_0_, f32[64,128]{1,0:T(8,128)S(1)} %collective-permute-done.3.refs_1_, s32[1,4]{1,0:T(1,128)S(1)} %bitcast.5, ...), custom_call_target="tpu_custom_call", output_to_operand_aliasing={{1}: (7, {})} | custom-call | tf_op jit(solution)/shard_map/pallas_call | solution.py:498
Async XLA Ops:
  0.0 6.9 %collective-permute-start = (f32[384,128]{1,0:T(8,128)}, f32[384,128]{1,0:T(8,128)S(1)}, u32[]{:S(2)}, u32[]{:S(2)}) collective-permute-start(f32[384,128]{1,0:T(8,128)} %bitcast.6), channel_id=1, source_target_pairs={{0,4},{1,5},{4,0},{5,1},{8,12},{9,13},{12,8},{13,9},{2,6},{3,7},{6... | collective-permute-start | bytes 589832 | tf_op jit(solution)/shard_map/ppermute | solution.py:398
  1.6 6.6 %collective-permute-start.1 = (f32[384,128]{1,0:T(8,128)}, f32[384,128]{1,0:T(8,128)S(1)}, u32[]{:S(2)}, u32[]{:S(2)}) collective-permute-start(f32[384,128]{1,0:T(8,128)} %bitcast.7), channel_id=1, source_target_pairs={{0,1},{1,0},{4,8},{5,9},{8,4},{9,5},{12,13},{13,12},{2,3},{3,2},{6... | collective-permute-start | bytes 589832 | tf_op jit(solution)/shard_map/ppermute | solution.py:399
  8.3 4.6 %collective-permute-start.4 = (f32[576,128]{1,0:T(8,128)S(1)}, f32[576,128]{1,0:T(8,128)S(1)}, u32[]{:S(2)}, u32[]{:S(2)}) collective-permute-start(f32[576,128]{1,0:T(8,128)S(1)} %get-tuple-element.25.refs_0_), channel_id=1, source_target_pairs={{0,1},{1,0},{2,3},{3,2},{4,5},{5,4},{6,7},{7,6},{8,9},{9,8},{10,11... | collective-permute-start | bytes 884744 | tf_op jit(solution)/shard_map/ppermute | solution.py:390
  8.4 3.2 %collective-permute-start.5 = (f32[384,128]{1,0:T(8,128)}, f32[384,128]{1,0:T(8,128)S(1)}, u32[]{:S(2)}, u32[]{:S(2)}) collective-permute-start(f32[384,128]{1,0:T(8,128)} %bitcast.9), channel_id=1, source_target_pairs={{0,1},{1,0},{2,3},{3,2},{4,5},{5,4},{6,7},{7,6},{8,9},{9,8},{10,11... | collective-permute-start | bytes 589832 | tf_op jit(solution)/shard_map/ppermute | solution.py:390
  8.9 4.1 %collective-permute-start.2 = (f32[64,128]{1,0:T(8,128)S(1)}, f32[64,128]{1,0:T(8,128)S(1)}, u32[]{:S(2)}, u32[]{:S(2)}) collective-permute-start(f32[64,128]{1,0:T(8,128)S(1)} %get-tuple-element.22), channel_id=1, source_target_pairs={{0,2},{2,0},{1,3},{3,1},{4,6},{6,4},{5,7},{7,5},{8,10},{10,8},{9,1... | collective-permute-start | bytes 98312 | tf_op jit(solution)/shard_map/ppermute | solution.py:450
  12.4 4.7 %collective-permute-start.6 = (bf16[384,128]{1,0:T(8,128)(2,1)S(1)}, bf16[384,128]{1,0:T(8,128)(2,1)S(1)}, u32[]{:S(2)}, u32[]{:S(2)}) collective-permute-start(bf16[384,128]{1,0:T(8,128)(2,1)S(1)} %get-tuple-element.27.refs_3_), channel_id=1, source_target_pairs={{0,2},{2,0},{1,3},{3,1},{4,6},{6,4},{5,7},{7,5},{8,10},{10,8},{9,1... | collective-permute-start | bytes 294920 | tf_op jit(solution)/shard_map/ppermute | solution.py:434
  13.0 5.2 %collective-permute-start.3 = (f32[64,128]{1,0:T(8,128)S(1)}, f32[64,128]{1,0:T(8,128)S(1)}, u32[]{:S(2)}, u32[]{:S(2)}) collective-permute-start(f32[64,128]{1,0:T(8,128)S(1)} %collective-permute-done.2.refs_0_), channel_id=1, source_target_pairs={{0,1},{1,0},{2,3},{3,2},{4,5},{5,4},{6,7},{7,6},{8,9},{9,8},{10,11... | collective-permute-start | bytes 98312 | tf_op jit(solution)/shard_map/ppermute | solution.py:390
  13.8 3.2 %copy-start = (s32[4]{0:T(128)S(1)}, s32[4]{0:T(128)}, u32[]{:S(2)}) copy-start(s32[4]{0:T(128)} %param.5) | copy-start | bytes 52

commit v5 on v4

--- a/solution.py
+++ b/solution.py
@@ -14,11 +14,12 @@
 REACH = len(gaussian_taps) // 2
 LANES = 128
 VMEM = pltpu.VMEM
+PHASES = 3
 
 
 def pairs(count, first, beside):
     partner = [None] * count
-    for low in range(first, count - 1, 2):
+    for low in range(first, count - 1, PHASES):
         partner[low], partner[low + 1] = low + 1, low
     found = []
     for source, target in enumerate(partner):
@@ -86,16 +87,19 @@
         copy.wait()
 
 
-def table_body(masks_ref, table_ref, inverse_ref, wide_ref):
+def table_body(masks_ref, table_ref, inverse_ref, wide_ref, pair_ref):
     offsets, radii, _ = masks_ref.shape
     wide_ref[...] = jnp.zeros_like(wide_ref)
     wide_ref[0:offsets, :, 0:offsets] = masks_ref[...].astype(jnp.float32)
     total = jnp.zeros((radii, LANES), jnp.float32)
-    for k in range(wide_ref.shape[0] // 2):
+    count = wide_ref.shape[0] // 2
+    for k in range(count):
         pair = wide_ref[2 * k] + pltpu.roll(wide_ref[2 * k + 1], 2 * TILE, 1)
         total = total + pair
+        pair_ref[k * radii : (k + 1) * radii, :] = pair
+    for k in range(count):
         for r in range(radii):
-            rows = jnp.broadcast_to(pair[r : r + 1, :], (TILE, LANES))
+            rows = pair_ref[pl.ds(k * radii + r, TILE, stride=0), :]
             turned = pltpu.roll(rows, 0, 1, stride=1, stride_axis=0)
             table_ref[r * TILE : (r + 1) * TILE, k * LANES : (k + 1) * LANES] = turned.astype(jnp.bfloat16)
     inverse_ref[...] = jnp.broadcast_to(1.0 / jnp.sum(total, axis=1, keepdims=True), (radii, LANES))
@@ -158,9 +162,9 @@
         smooth_ref[t * cols : (t + 1) * cols, :] = turn_ref[pl.ds(t, cols, stride=frames), :].astype(jnp.bfloat16)
 
 
-def columns_body(frames, cols, x_ref, a_ref, b_ref, out_ref, edge_ref):
+def columns_body(frames, cols, x_ref, a_ref, b_ref, c_ref, out_ref, edge_ref):
     place, count = lax.axis_index("space"), lax.axis_size("space")
-    even = lax.rem(place, 2) == 0
+    phase = lax.rem(place, PHASES)
     lowest, highest = place > 0, place < count - 1
     halo = RMAX + REACH
 
@@ -169,8 +173,8 @@
             return x_ref[pl.ds(c, frames, stride=cols), :]
         at = c + cols if c < 0 else c - cols
         rows = pl.ds(at, frames, stride=cols)
-        first, second, there = (b_ref, a_ref, lowest) if c < 0 else (a_ref, b_ref, highest)
-        value = jnp.where(even, first[rows, :], second[rows, :])
+        refs, there = ((c_ref, a_ref, b_ref), lowest) if c < 0 else ((a_ref, b_ref, c_ref), highest)
+        value = jnp.where(phase == 0, refs[0][rows, :], jnp.where(phase == 1, refs[1][rows, :], refs[2][rows, :]))
         return jnp.where(there, value, jnp.zeros_like(value))
 
     order = 0
@@ -397,6 +401,7 @@
 
     one = lax.ppermute(flat, ("space", "row"), pairs(count, 0, row_count))
     two = lax.ppermute(flat, ("space", "row"), pairs(count, 1, row_count))
+    three = lax.ppermute(flat, ("space", "row"), pairs(count, 2, row_count))
     near = across(flat)
 
     depth = (offsets + 1) * 2 * TILE
@@ -436,15 +441,15 @@
     table, inverse = vmem_call(
         table_body,
         [shape((radii * TILE, depth), bf16), shape((radii, LANES), f32)],
-        scratch=[VMEM((offsets + 1, radii, LANES), f32)],
+        scratch=[VMEM((offsets + 1, radii, LANES), f32), VMEM(((offsets + 1) // 2 * radii, LANES), f32)],
     )(masks)
 
     def columns(*refs):
         columns_body(frames, cols, *refs)
 
     blurred, edges = vmem_call(
-        columns, [shape((2 * edge * frames, rows), f32), shape((2 * REACH * frames, rows), f32)], inputs=3
-    )(held, one, two)
+        columns, [shape((2 * edge * frames, rows), f32), shape((2 * REACH * frames, rows), f32)], inputs=4
+    )(held, one, two, three)
 
     sides = across(blurred)
     edges = lax.ppermute(edges, "tm", later)

time: 20.1 us -> 19.4 us (0.965)
  the two profiles are of different devices: /device:TPU:20 before, /device:TPU:0 now
where the time goes in v5:
time: 19.4 us; the launch traced here: 19.2 us
  Pallas kernels  7.54 us (39%)
  starting transfers between devices  6.73 us (35%)
  waiting for transfers between devices  4.87 us (25%)
    ppermute x1, waiting for transfers between devices, local(): one = lax.ppermute(flat, ('space', 'row'), pairs(count, 0, row_count))  3.57 us
    ppermute x1, starting transfers between devices, local(): one = lax.ppermute(flat, ('space', 'row'), pairs(count, 0, row_count))  3.05 us
    pallas_call x1, Pallas kernels, local(): vmem_call(correlate, [shape((radii, lag_count, cols, rows), f32), shape(s...  1.67 us
    ppermute x1, starting transfers between devices, local(): edges = lax.ppermute(edges, 'tm', later)  1.66 us
    pallas_call x1, Pallas kernels, local(): early = vmem_call(products, sums, inputs=2, cost=cost)(table, tiles)  1.58 us
    ppermute x1, waiting for transfers between devices, local(): earlier = lax.ppermute(smooth, 'tm', later)  1.17 us
    pallas_call x1, Pallas kernels, local(): vmem_call(others, [sums, shape((tile_count, 2 * frames * cols, LANES), f3...  1.07 us
    pallas_call x1, Pallas kernels, local(): vmem_call(prepare_body, [shape((2 * LANES, 2 * LANES), f32), shape((frame...  1.02 us
  transfers between devices with their start and end apart: 8, of which 3 were waited for; matrix products, arithmetic and copies ran while one was open for 0% of the time, Pallas kernels for 30%

profile of v5, /device:TPU:0, one launch (start us, length us, event | category | flops | bytes accessed | tf_op | source)
XLA Modules:
  0.0 19.2 jit_solution(2019267180206735198)
XLA Ops:
  0.0 3.1 %collective-permute-start = (f32[384,128]{1,0:T(8,128)}, f32[384,128]{1,0:T(8,128)S(1)}, u32[]{:S(2)}, u32[]{:S(2)}) collective-permute-start(f32[384,128]{1,0:T(8,128)} %bitcast.6), channel_id=1, source_target_pairs={{0,4},{1,5},{4,0},{5,1},{8,9},{9,8},{12,13},{13,12},{2,6},{3,7},{6... | collective-permute-start | bytes 589832 | tf_op jit(solution)/shard_map/ppermute | solution.py:402
  3.1 0.0 collective-permute-start.1
  3.1 0.5 %collective-permute-start.2 = (f32[384,128]{1,0:T(8,128)}, f32[384,128]{1,0:T(8,128)S(1)}, u32[]{:S(2)}, u32[]{:S(2)}) collective-permute-start(f32[384,128]{1,0:T(8,128)} %bitcast.8), channel_id=1, source_target_pairs={{0,1},{1,0},{4,5},{5,4},{8,12},{9,13},{12,8},{13,9},{2,3},{3,2},{6... | collective-permute-start | bytes 589832 | tf_op jit(solution)/shard_map/ppermute | solution.py:404
  3.6 1.0 %shard_map.37 = (f32[256,256]{1,0:T(8,128)S(1)}, f32[384,128]{1,0:T(8,128)S(1)}, s32[33,8,33]{2,1,0:T(8,128)S(1)}) custom-call(s32[33,8,33]{2,1,0:T(8,128)} %bitcast.11, f32[384,128]{1,0:T(8,128)} %bitcast.9), custom_call_target="tpu_custom_call" | custom-call | tf_op jit(solution)/shard_map/pallas_call | solution.py:409
  4.6 3.6 %collective-permute-done.refs_1_ = f32[384,128]{1,0:T(8,128)S(1)} collective-permute-done((f32[384,128]{1,0:T(8,128)}, f32[384,128]{1,0:T(8,128)S(1)}, u32[]{:S(2)}, u32[]{:S(2)}) %collective-permute-start) | collective-permute-done | bytes 196640 | tf_op jit(solution)/shard_map/ppermute | solution.py:402
  8.2 0.0 collective-permute-done.1.refs_2_
  8.2 0.0 collective-permute-done.2.refs_3_
  8.2 0.2 %shard_map.38 = (f32[576,128]{1,0:T(8,128)S(1)}, f32[64,128]{1,0:T(8,128)S(1)}) custom-call(f32[384,128]{1,0:T(8,128)S(1)} %get-tuple-element.21.refs_0_, f32[384,128]{1,0:T(8,128)S(1)} %collective-permute-done.refs_1_, f32[384,128]{1,0:T(8,128)S(1)} %collective-permute-done.1.refs_2_, f32[384,128]{1,0:T(8,128)S(1)} %collective-permute-done.2.refs_3_), custom_call_target="tpu_custom_call" | custom-call | tf_op jit(solution)/shard_map/pallas_call | solution.py:450
  8.4 0.1 collective-permute-start.5
  8.5 0.5 %collective-permute-start.6 = (f32[384,128]{1,0:T(8,128)}, f32[384,128]{1,0:T(8,128)S(1)}, u32[]{:S(2)}, u32[]{:S(2)}) collective-permute-start(f32[384,128]{1,0:T(8,128)} %bitcast.10), channel_id=1, source_target_pairs={{0,1},{1,0},{2,3},{3,2},{4,5},{5,4},{6,7},{7,6},{8,9},{9,8},{10,11... | collective-permute-start | bytes 589832 | tf_op jit(solution)/shard_map/ppermute | solution.py:394
  9.0 1.7 %collective-permute-start.3 = (f32[64,128]{1,0:T(8,128)S(1)}, f32[64,128]{1,0:T(8,128)S(1)}, u32[]{:S(2)}, u32[]{:S(2)}) collective-permute-start(f32[64,128]{1,0:T(8,128)S(1)} %get-tuple-element.22), channel_id=1, source_target_pairs={{0,2},{2,0},{1,3},{3,1},{4,6},{6,4},{5,7},{7,5},{8,10},{10,8},{9,1... | collective-permute-start | bytes 98312 | tf_op jit(solution)/shard_map/ppermute | solution.py:455
  10.6 0.5 %shard_map.39 = (bf16[256,2176]{1,0:T(8,128)(2,1)S(1)}, f32[8,128]{1,0:T(8,128)S(1)}) custom-call(s32[33,8,33]{2,1,0:T(8,128)S(1)} %get-tuple-element.23.masks_ref), custom_call_target="tpu_custom_call" | custom-call | tf_op jit(solution)/shard_map/pallas_call | solution.py:441
  11.1 0.0 collective-permute-done.6.refs_1_
  11.1 0.7 %shard_map.40 = (bf16[384,128]{1,0:T(8,128)(2,1)S(1)}, bf16[4,19,16,128]{3,2,1,0:T(8,128)(2,1)S(1)}, f32[2,2,16,128]{3,2,1,0:T(8,128)S(1)}) custom-call(f32[384,128]{1,0:T(8,128)S(1)} %get-tuple-element.21.refs_0_, f32[384,128]{1,0:T(8,128)S(1)} %collective-permute-done.6.refs_1_, f32[256,256]{1,0:T(8,128)S(1)} %get-tuple-element.26.refs_2_), custom_call_target="tpu_custom_call" | custom-call | tf_op jit(solution)/shard_map/pallas_call | solution.py:424
  11.8 0.9 %collective-permute-start.7 = (bf16[384,128]{1,0:T(8,128)(2,1)S(1)}, bf16[384,128]{1,0:T(8,128)(2,1)S(1)}, u32[]{:S(2)}, u32[]{:S(2)}) collective-permute-start(bf16[384,128]{1,0:T(8,128)(2,1)S(1)} %get-tuple-element.27.refs_3_), channel_id=1, source_target_pairs={{0,2},{2,0},{1,3},{3,1},{4,6},{6,4},{5,7},{7,5},{8,10},{10,8},{9,1... | collective-permute-start | bytes 294920 | tf_op jit(solution)/shard_map/ppermute | solution.py:439
  12.8 0.1 collective-permute-done.3.refs_0_
  12.9 0.0 collective-permute-start.4
  12.9 0.0 collective-permute-done.5.refs_1_
  12.9 0.8 %shard_map.41 = (bf16[4,56,16,128]{3,2,1,0:T(8,128)(2,1)S(1)}, bf16[384,128]{1,0:T(8,128)(2,1)S(1)}) custom-call(f32[576,128]{1,0:T(8,128)S(1)} %get-tuple-element.25.refs_0_, f32[576,128]{1,0:T(8,128)S(1)} %collective-permute-done.5.refs_1_, f32[256,256]{1,0:T(8,128)S(1)} %get-tuple-element.26.refs_2_, bf16[384,128]{1,0:T(8,128)(2,1)S(1)} %get-tuple-element.27.refs_3_, ...), custom_call_target="tpu_custom_call" | custom-call | tf_op jit(solution)/shard_map/pallas_call | solution.py:460
  13.7 0.0 copy-start
  13.7 1.6 %shard_map.42.refs_6_.refs_3_ = f32[3,2,576,128]{3,2,1,0:T(8,128)S(1)} custom-call(bf16[256,2176]{1,0:T(8,128)(2,1)S(1)} %get-tuple-element.24.refs_0_, bf16[4,56,16,128]{3,2,1,0:T(8,128)(2,1)S(1)} %get-tuple-element.30.refs_1_), custom_call_target="tpu_custom_call" | custom-call | flops 1283457024 | bytes 1048576 | tf_op jit(solution)/shard_map/pallas_call | solution.py:480
  15.3 1.2 %collective-permute-done.7.refs_3_ = bf16[384,128]{1,0:T(8,128)(2,1)S(1)} collective-permute-done((bf16[384,128]{1,0:T(8,128)(2,1)S(1)}, bf16[384,128]{1,0:T(8,128)(2,1)S(1)}, u32[]{:S(2)}, u32[]{:S(2)}) %collective-permute-start.7) | collective-permute-done | bytes 98336 | tf_op jit(solution)/shard_map/ppermute | solution.py:439
  16.5 1.1 %shard_map.43 = (f32[1,2,576,128]{3,2,1,0:T(8,128)S(1)}, f32[4,768,128]{2,1,0:T(8,128)S(1)}, f32[1,8,4,8,128]{4,3,2,1,0:T(8,128)S(1)}) custom-call(bf16[256,2176]{1,0:T(8,128)(2,1)S(1)} %get-tuple-element.24.refs_0_, bf16[4,56,16,128]{3,2,1,0:T(8,128)(2,1)S(1)} %get-tuple-element.30.refs_1_, bf16[384,128]{1,0:T(8,128)(2,1)S(1)} %get-tuple-element.31.refs_2_, ...), custom_call_target="tpu_custom_call" | custom-call | flops 427819008 | bytes 1048576 | tf_op jit(solution)/shard_map/pallas_call | solution.py:488
  17.6 1.7 %shard_map.44 = (f32[8,4,24,128]{3,2,1,0:T(8,128)}, f32[4,768,128]{2,1,0:T(8,128)S(1)}) custom-call(f32[64,128]{1,0:T(8,128)S(1)} %collective-permute-done.3.refs_0_, f32[64,128]{1,0:T(8,128)S(1)} %collective-permute-done.4.refs_1_, s32[1,4]{1,0:T(1,128)S(1)} %bitcast.5, ...), custom_call_target="tpu_custom_call", output_to_operand_aliasing={{1}: (7, {})} | custom-call | tf_op jit(solution)/shard_map/pallas_call | solution.py:503
  (2 shorter events, 0.0 us)
Async XLA Ops:
  0.0 8.2 %collective-permute-start = (f32[384,128]{1,0:T(8,128)}, f32[384,128]{1,0:T(8,128)S(1)}, u32[]{:S(2)}, u32[]{:S(2)}) collective-permute-start(f32[384,128]{1,0:T(8,128)} %bitcast.6), channel_id=1, source_target_pairs={{0,4},{1,5},{4,0},{5,1},{8,9},{9,8},{12,13},{13,12},{2,6},{3,7},{6... | collective-permute-start | bytes 589832 | tf_op jit(solution)/shard_map/ppermute | solution.py:402
  3.1 5.1 %collective-permute-start.1 = (f32[384,128]{1,0:T(8,128)}, f32[384,128]{1,0:T(8,128)S(1)}, u32[]{:S(2)}, u32[]{:S(2)}) collective-permute-start(f32[384,128]{1,0:T(8,128)} %bitcast.7), channel_id=1, source_target_pairs={{0,1},{1,0},{4,8},{5,9},{8,4},{9,5},{12,13},{13,12},{2,3},{3,2},{6... | collective-permute-start | bytes 589832 | tf_op jit(solution)/shard_map/ppermute | solution.py:403
  3.1 5.1 %collective-permute-start.2 = (f32[384,128]{1,0:T(8,128)}, f32[384,128]{1,0:T(8,128)S(1)}, u32[]{:S(2)}, u32[]{:S(2)}) collective-permute-start(f32[384,128]{1,0:T(8,128)} %bitcast.8), channel_id=1, source_target_pairs={{0,1},{1,0},{4,5},{5,4},{8,12},{9,13},{12,8},{13,9},{2,3},{3,2},{6... | collective-permute-start | bytes 589832 | tf_op jit(solution)/shard_map/ppermute | solution.py:404
  8.4 4.5 %collective-permute-start.5 = (f32[576,128]{1,0:T(8,128)S(1)}, f32[576,128]{1,0:T(8,128)S(1)}, u32[]{:S(2)}, u32[]{:S(2)}) collective-permute-start(f32[576,128]{1,0:T(8,128)S(1)} %get-tuple-element.25.refs_0_), channel_id=1, source_target_pairs={{0,1},{1,0},{2,3},{3,2},{4,5},{5,4},{6,7},{7,6},{8,9},{9,8},{10,11... | collective-permute-start | bytes 884744 | tf_op jit(solution)/shard_map/ppermute | solution.py:394
  8.5 2.6 %collective-permute-start.6 = (f32[384,128]{1,0:T(8,128)}, f32[384,128]{1,0:T(8,128)S(1)}, u32[]{:S(2)}, u32[]{:S(2)}) collective-permute-start(f32[384,128]{1,0:T(8,128)} %bitcast.10), channel_id=1, source_target_pairs={{0,1},{1,0},{2,3},{3,2},{4,5},{5,4},{6,7},{7,6},{8,9},{9,8},{10,11... | collective-permute-start | bytes 589832 | tf_op jit(solution)/shard_map/ppermute | solution.py:394
  9.0 3.9 %collective-permute-start.3 = (f32[64,128]{1,0:T(8,128)S(1)}, f32[64,128]{1,0:T(8,128)S(1)}, u32[]{:S(2)}, u32[]{:S(2)}) collective-permute-start(f32[64,128]{1,0:T(8,128)S(1)} %get-tuple-element.22), channel_id=1, source_target_pairs={{0,2},{2,0},{1,3},{3,1},{4,6},{6,4},{5,7},{7,5},{8,10},{10,8},{9,1... | collective-permute-start | bytes 98312 | tf_op jit(solution)/shard_map/ppermute | solution.py:455
  11.8 4.7 %collective-permute-start.7 = (bf16[384,128]{1,0:T(8,128)(2,1)S(1)}, bf16[384,128]{1,0:T(8,128)(2,1)S(1)}, u32[]{:S(2)}, u32[]{:S(2)}) collective-permute-start(bf16[384,128]{1,0:T(8,128)(2,1)S(1)} %get-tuple-element.27.refs_3_), channel_id=1, source_target_pairs={{0,2},{2,0},{1,3},{3,1},{4,6},{6,4},{5,7},{7,5},{8,10},{10,8},{9,1... | collective-permute-start | bytes 294920 | tf_op jit(solution)/shard_map/ppermute | solution.py:439
  12.9 4.7 %collective-permute-start.4 = (f32[64,128]{1,0:T(8,128)S(1)}, f32[64,128]{1,0:T(8,128)S(1)}, u32[]{:S(2)}, u32[]{:S(2)}) collective-permute-start(f32[64,128]{1,0:T(8,128)S(1)} %collective-permute-done.3.refs_0_), channel_id=1, source_target_pairs={{0,1},{1,0},{2,3},{3,2},{4,5},{5,4},{6,7},{7,6},{8,9},{9,8},{10,11... | collective-permute-start | bytes 98312 | tf_op jit(solution)/shard_map/ppermute | solution.py:394
  13.7 2.8 %copy-start = (s32[4]{0:T(128)S(1)}, s32[4]{0:T(128)}, u32[]{:S(2)}) copy-start(s32[4]{0:T(128)} %param.5) | copy-start | bytes 52

commit v6 on v5

--- a/solution.py
+++ b/solution.py
@@ -249,20 +249,51 @@
     whole_ref[...] = smooth_ref[...] + placed(frames, cols, edges)
 
 
-def sums_body(frames, cols, first, table_ref, tiles_ref, out_ref):
-    rows, pitch = cols * frames, frames + 8
-    for j in range(out_ref.shape[0]):
-        pieces = [tiles_ref[first + j, a : a + cols].reshape(rows, LANES) for a in range(0, 2 * RMAX + 1, 2)]
-        found = lax.dot_general(
-            jnp.concatenate(pieces, axis=1),
-            table_ref[...],
-            (((1,), (1,)), ((), ())),
-            preferred_element_type=jnp.float32,
-        )
-        for g in range(out_ref.shape[1]):
-            for c in range(cols):
-                value = found[c * frames : (c + 1) * frames, g * LANES : (g + 1) * LANES]
-                out_ref[j, g, c * pitch : c * pitch + frames, :] = value
+def inner_span(cols, block):
+    edge, last = RMAX + REACH, cols + RMAX - REACH - 2
+    return max(0, -(-(edge - 8 * block) // 2)), min(RMAX, (last - 8 * block - 7) // 2) + 1
+
+
+def times(pieces, weights):
+    return lax.dot_general(
+        jnp.concatenate(pieces, axis=1), weights, (((1,), (1,)), ((), ())), preferred_element_type=jnp.float32
+    )
+
+
+def inner_body(frames, cols, table_ref, pairs_ref, out_ref):
+    tile_count, groups, pitch = out_ref.shape[0], out_ref.shape[1], frames + 8
+    for block in range(cols // 8):
+        begin, end = inner_span(cols, block)
+        start = 8 * block - RMAX - REACH
+        pieces = [
+            pairs_ref[:, start + 2 * p : start + 2 * p + 8].reshape(tile_count * 8 * frames, LANES)
+            for p in range(begin, end)
+        ]
+        found = times(pieces, table_ref[:, begin * LANES : end * LANES])
+        for j in range(tile_count):
+            for c in range(8):
+                for g in range(groups):
+                    row, at = (j * 8 + c) * frames, (8 * block + c) * pitch
+                    out_ref[j, g, at : at + frames, :] = found[row : row + frames, g * LANES : (g + 1) * LANES]
+
+
+def sums_body(frames, cols, table_ref, tiles_ref, inner_ref, out_ref):
+    tile_count, groups, pitch = out_ref.shape[0], out_ref.shape[1], frames + 8
+    for block in range(cols // 8):
+        begin, end = inner_span(cols, block)
+        chosen = [p for p in range(RMAX + 1) if not begin <= p < end]
+        start = 8 * block
+        pieces = [
+            tiles_ref[:, start + 2 * p : start + 2 * p + 8].reshape(tile_count * 8 * frames, LANES) for p in chosen
+        ]
+        weights = [table_ref[:, p * LANES : (p + 1) * LANES] for p in chosen]
+        found = times(pieces, jnp.concatenate(weights, axis=1))
+        for j in range(tile_count):
+            for c in range(8):
+                for g in range(groups):
+                    row, at = (j * 8 + c) * frames, (8 * block + c) * pitch
+                    value = found[row : row + frames, g * LANES : (g + 1) * LANES]
+                    out_ref[j, g, at : at + frames, :] = value + inner_ref[j, g, at : at + frames, :]
 
 
 def correlate_block(frames, cols, n, lags, sources, spread_ref, inverse_ref, total_ref, held):
@@ -302,27 +333,27 @@
     return [lag_ref[0, lag] for lag in range(lag_ref.shape[1])]
 
 
-def later_body(
-    frames, cols, table_ref, tiles_ref, whole_ref, earlier_ref, lag_ref, inverse_ref, early_ref,
+def products_body(
+    frames, cols, table_ref, tiles_ref, inner_ref, whole_ref, earlier_ref, lag_ref, inverse_ref,
     out_ref, spread_ref, held_ref, total_ref,
 ):
     begun = lax.axis_index("tm") > 0
-    rows, done = frames * cols, early_ref.shape[0]
+    rows = frames * cols
     for half, source in enumerate((earlier_ref, whole_ref)):
         value = spread_of(source[...])
         if half == 0:
             value = jnp.where(begun, value, 0.0)
         for j in range(LANES // TILE):
             spread_ref[j, half * rows : (half + 1) * rows, :] = value[:, j * LANES : (j + 1) * LANES]
-    sums_body(frames, cols, done, table_ref, tiles_ref, out_ref)
-    sources = [(early_ref, j) for j in range(done)] + [(out_ref, j) for j in range(out_ref.shape[0])]
+    sums_body(frames, cols, table_ref, tiles_ref, inner_ref, out_ref)
     lags = read_lags(lag_ref)
+    sources = [(out_ref, j) for j in range(out_ref.shape[0])]
     for n in range(held_ref.shape[0]):
         correlate_block(frames, cols, n + 1, lags, sources, spread_ref, inverse_ref, total_ref, held_ref.at[n])
 
 
 def correlate_body(
-    frames, cols, edge_ref, low_ref, high_ref, lag_ref, early_ref, late_ref, middle_ref, inverse_ref, given_ref,
+    frames, cols, edge_ref, low_ref, high_ref, lag_ref, sums_ref, middle_ref, inverse_ref, given_ref,
     out_ref, spread_ref, held_ref, total_ref, sem,
 ):
     del given_ref
@@ -359,7 +390,7 @@
         for slot in range(2 * REACH):
             column = slot if slot < REACH else slot + cols - 2 * REACH
             spread_ref[j, pl.ds(column, frames, stride=cols), :] = tile[slot * frames : (slot + 1) * frames, :]
-    sources = [(early_ref, j) for j in range(early_ref.shape[0])] + [(late_ref, j) for j in range(late_ref.shape[0])]
+    sources = [(sums_ref, j) for j in range(tile_count)]
     lags = read_lags(lag_ref)
 
     def one_end(end, carry):
@@ -393,6 +424,17 @@
     def across(value):
         low = lax.ppermute(value, "row", ring)
         return [low] if row_count == 2 else [low, lax.ppermute(value, "row", [(b, a) for a, b in ring])]
+
+    def across_later(value):
+        windows, found = lax.axis_size("tm"), []
+        for step in (1,) if row_count == 2 else (1, -1):
+            moves = [
+                (t * row_count + r, (t + 1) % windows * row_count + (r + step) % row_count)
+                for t in range(windows)
+                for r in range(row_count)
+            ]
+            found.append(lax.ppermute(value, ("tm", "row"), moves))
+        return found
 
     def split(refs, lead=1):
         both = 1 if row_count == 2 else 2
@@ -444,6 +486,13 @@
         scratch=[VMEM((offsets + 1, radii, LANES), f32), VMEM(((offsets + 1) // 2 * radii, LANES), f32)],
     )(masks)
 
+    sums = shape((tile_count, groups, cols * (frames + 8), LANES), f32)
+
+    def inner_products(*refs):
+        inner_body(frames, cols, *refs)
+
+    partial = vmem_call(inner_products, sums, inputs=2)(table, inner_pairs)
+
     def columns(*refs):
         columns_body(frames, cols, *refs)
 
@@ -452,6 +501,7 @@
     )(held, one, two, three)
 
     sides = across(blurred)
+    far = across_later(edges)
     edges = lax.ppermute(edges, "tm", later)
 
     def windows(*refs):
@@ -468,25 +518,14 @@
     total = VMEM((tile_count, lag_count, groups, 8, LANES), f32)
     lags = lag_list.reshape(1, lag_count)
 
-    def sums_of(count):
-        flops = 2 * count * cols * frames * radii * TILE * depth
-        cost = pl.CostEstimate(flops=flops, bytes_accessed=1 << 20, transcendentals=0)
-        return shape((count, groups, cols * (frames + 8), LANES), f32), cost
+    flops = 2 * tile_count * cols * frames * radii * TILE * depth
+    cost = pl.CostEstimate(flops=flops, bytes_accessed=1 << 20, transcendentals=0)
 
     def products(*refs):
-        sums_body(frames, cols, 0, *refs)
-
-    sums, cost = sums_of(tile_count - 1)
-    early = vmem_call(products, sums, inputs=2, cost=cost)(table, tiles)
-
-    far = across(edges)
-
-    def others(*refs):
-        later_body(frames, cols, *refs)
-
-    sums, cost = sums_of(1)
-    late, spread, middle = vmem_call(
-        others,
+        products_body(frames, cols, *refs)
+
+    found, spread, middle = vmem_call(
+        products,
         [
             sums,
             shape((tile_count, 2 * frames * cols, LANES), f32),
@@ -495,7 +534,7 @@
         scratch=[total],
         inputs=7,
         cost=cost,
-    )(table, tiles, whole, earlier, lags, inverse, early)
+    )(table, tiles, partial, whole, earlier, lags, inverse)
 
     def correlate(*refs):
         correlate_body(frames, cols, *split(refs))
@@ -508,10 +547,10 @@
             total,
             pltpu.SemaphoreType.DMA((blocks,)),
         ],
-        inputs=7 + len(far),
+        inputs=6 + len(far),
         out_space=[pl.ANY, VMEM],
-        aliases={6 + len(far): 1},
-    )(edges, *far, lags, early, late, middle, inverse, spread)
+        aliases={5 + len(far): 1},
+    )(edges, *far, lags, found, middle, inverse, spread)
     return out[None]
 
 

time: 19.4 us -> 18.5 us (0.954)
  the two profiles are of different devices: /device:TPU:0 before, /device:TPU:1 now
where the time goes in v6:
time: 18.5 us; the launch traced here: 18.3 us
  starting transfers between devices  8.34 us (45%)
  Pallas kernels  7.55 us (41%)
  waiting for transfers between devices  2.34 us (13%)
    ppermute x1, waiting for transfers between devices, local(): one = lax.ppermute(flat, ('space', 'row'), pairs(count, 0, row_count))  2.32 us
    ppermute x1, starting transfers between devices, local(): one = lax.ppermute(flat, ('space', 'row'), pairs(count, 0, row_count))  2.11 us
    pallas_call x1, Pallas kernels, local(): vmem_call(products, [sums, shape((tile_count, 2 * frames * cols, LANES),...  1.88 us
    ppermute x1, starting transfers between devices, across_later(): found.append(lax.ppermute(value, ('tm', 'row'), moves))  1.85 us
    ppermute x2, starting transfers between devices, across(): low = lax.ppermute(value, 'row', ring)  1.82 us
    pallas_call x1, Pallas kernels, local(): vmem_call(correlate, [shape((radii, lag_count, cols, rows), f32), shape(s...  1.66 us
    ppermute x1, starting transfers between devices, local(): earlier = lax.ppermute(smooth, 'tm', later)  1.44 us
    pallas_call x1, Pallas kernels, local(): vmem_call(prepare_body, [shape((2 * LANES, 2 * LANES), f32), shape((frame...  1.02 us
  transfers between devices with their start and end apart: 8, of which 1 were waited for; matrix products, arithmetic and copies ran while one was open for 0% of the time, Pallas kernels for 32%

profile of v6, /device:TPU:1, one launch (start us, length us, event | category | flops | bytes accessed | tf_op | source)
XLA Modules:
  0.0 18.3 jit_solution(5991834500522421551)
XLA Ops:
  0.0 2.1 %collective-permute-start = (f32[384,128]{1,0:T(8,128)}, f32[384,128]{1,0:T(8,128)S(1)}, u32[]{:S(2)}, u32[]{:S(2)}) collective-permute-start(f32[384,128]{1,0:T(8,128)} %bitcast.6), channel_id=1, source_target_pairs={{0,4},{1,5},{4,0},{5,1},{8,9},{9,8},{12,13},{13,12},{2,6},{3,7},{6... | collective-permute-start | bytes 589832 | tf_op jit(solution)/shard_map/ppermute | solution.py:444
  2.1 1.0 %collective-permute-start.1 = (f32[384,128]{1,0:T(8,128)}, f32[384,128]{1,0:T(8,128)S(1)}, u32[]{:S(2)}, u32[]{:S(2)}) collective-permute-start(f32[384,128]{1,0:T(8,128)} %bitcast.7), channel_id=1, source_target_pairs={{0,1},{1,0},{4,8},{5,9},{8,4},{9,5},{12,13},{13,12},{2,3},{3,2},{6... | collective-permute-start | bytes 589832 | tf_op jit(solution)/shard_map/ppermute | solution.py:445
  3.1 0.0 collective-permute-start.2
  3.1 0.5 %collective-permute-start.6 = (f32[384,128]{1,0:T(8,128)}, f32[384,128]{1,0:T(8,128)S(1)}, u32[]{:S(2)}, u32[]{:S(2)}) collective-permute-start(f32[384,128]{1,0:T(8,128)} %bitcast.9), channel_id=1, source_target_pairs={{0,1},{1,0},{2,3},{3,2},{4,5},{5,4},{6,7},{7,6},{8,9},{9,8},{10,11... | collective-permute-start | bytes 589832 | tf_op jit(solution)/shard_map/ppermute | solution.py:425
  3.6 1.0 %shard_map.37 = (f32[256,256]{1,0:T(8,128)S(1)}, f32[384,128]{1,0:T(8,128)S(1)}, s32[33,8,33]{2,1,0:T(8,128)S(1)}) custom-call(s32[33,8,33]{2,1,0:T(8,128)} %bitcast.11, f32[384,128]{1,0:T(8,128)} %bitcast.10), custom_call_target="tpu_custom_call" | custom-call | tf_op jit(solution)/shard_map/pallas_call | solution.py:451
  4.6 2.3 %collective-permute-done.refs_1_ = f32[384,128]{1,0:T(8,128)S(1)} collective-permute-done((f32[384,128]{1,0:T(8,128)}, f32[384,128]{1,0:T(8,128)S(1)}, u32[]{:S(2)}, u32[]{:S(2)}) %collective-permute-start) | collective-permute-done | bytes 196640 | tf_op jit(solution)/shard_map/ppermute | solution.py:444
  6.9 0.0 collective-permute-done.1.refs_2_
  6.9 0.0 collective-permute-done.2.refs_3_
  6.9 0.2 %shard_map.38 = (f32[576,128]{1,0:T(8,128)S(1)}, f32[64,128]{1,0:T(8,128)S(1)}) custom-call(f32[384,128]{1,0:T(8,128)S(1)} %get-tuple-element.21.refs_0_, f32[384,128]{1,0:T(8,128)S(1)} %collective-permute-done.refs_1_, f32[384,128]{1,0:T(8,128)S(1)} %collective-permute-done.1.refs_2_, f32[384,128]{1,0:T(8,128)S(1)} %collective-permute-done.2.refs_3_), custom_call_target="tpu_custom_call" | custom-call | tf_op jit(solution)/shard_map/pallas_call | solution.py:499
  7.1 1.3 %collective-permute-start.5 = (f32[576,128]{1,0:T(8,128)S(1)}, f32[576,128]{1,0:T(8,128)S(1)}, u32[]{:S(2)}, u32[]{:S(2)}) collective-permute-start(f32[576,128]{1,0:T(8,128)S(1)} %get-tuple-element.25.refs_0_), channel_id=1, source_target_pairs={{0,1},{1,0},{2,3},{3,2},{4,5},{5,4},{6,7},{7,6},{8,9},{9,8},{10,11... | collective-permute-start | bytes 884744 | tf_op jit(solution)/shard_map/ppermute | solution.py:425
  8.5 0.0 collective-permute-done.6.refs_1_
  8.5 0.7 %shard_map.40 = (bf16[384,128]{1,0:T(8,128)(2,1)S(1)}, bf16[4,19,16,128]{3,2,1,0:T(8,128)(2,1)S(1)}, f32[2,2,16,128]{3,2,1,0:T(8,128)S(1)}) custom-call(f32[384,128]{1,0:T(8,128)S(1)} %get-tuple-element.21.refs_0_, f32[384,128]{1,0:T(8,128)S(1)} %collective-permute-done.6.refs_1_, f32[256,256]{1,0:T(8,128)S(1)} %get-tuple-element.26.refs_2_), custom_call_target="tpu_custom_call" | custom-call | tf_op jit(solution)/shard_map/pallas_call | solution.py:466
  9.2 1.4 %collective-permute-start.7 = (bf16[384,128]{1,0:T(8,128)(2,1)S(1)}, bf16[384,128]{1,0:T(8,128)(2,1)S(1)}, u32[]{:S(2)}, u32[]{:S(2)}) collective-permute-start(bf16[384,128]{1,0:T(8,128)(2,1)S(1)} %get-tuple-element.27.refs_3_), channel_id=1, source_target_pairs={{0,2},{2,0},{1,3},{3,1},{4,6},{6,4},{5,7},{7,5},{8,10},{10,8},{9,1... | collective-permute-start | bytes 294920 | tf_op jit(solution)/shard_map/ppermute | solution.py:481
  10.6 0.5 %shard_map.39 = (bf16[256,2176]{1,0:T(8,128)(2,1)S(1)}, f32[8,128]{1,0:T(8,128)S(1)}) custom-call(s32[33,8,33]{2,1,0:T(8,128)S(1)} %get-tuple-element.23.masks_ref), custom_call_target="tpu_custom_call" | custom-call | tf_op jit(solution)/shard_map/pallas_call | solution.py:483
  11.1 0.2 collective-permute-start.3
  11.2 1.8 %collective-permute-start.4 = (f32[64,128]{1,0:T(8,128)S(1)}, f32[64,128]{1,0:T(8,128)S(1)}, u32[]{:S(2)}, u32[]{:S(2)}) collective-permute-start(f32[64,128]{1,0:T(8,128)S(1)} %get-tuple-element.22), channel_id=1, source_target_pairs={{0,3},{1,2},{2,1},{3,0},{4,7},{5,6},{6,5},{7,4},{8,11},{9,10},{10,... | collective-permute-start | bytes 98312 | tf_op jit(solution)/shard_map/ppermute | solution.py:436
  13.1 0.8 %shard_map.42.refs_2_ = f32[4,2,576,128]{3,2,1,0:T(8,128)S(1)} custom-call(bf16[256,2176]{1,0:T(8,128)(2,1)S(1)} %get-tuple-element.24.refs_0_, bf16[4,19,16,128]{3,2,1,0:T(8,128)(2,1)S(1)} %get-tuple-element.28.refs_4_.refs_1_), custom_call_target="tpu_custom_call" | custom-call | tf_op jit(solution)/shard_map/pallas_call | solution.py:494
  13.9 0.0 collective-permute-done.5.refs_1_
  13.9 0.8 %shard_map.41 = (bf16[4,56,16,128]{3,2,1,0:T(8,128)(2,1)S(1)}, bf16[384,128]{1,0:T(8,128)(2,1)S(1)}) custom-call(f32[576,128]{1,0:T(8,128)S(1)} %get-tuple-element.25.refs_0_, f32[576,128]{1,0:T(8,128)S(1)} %collective-permute-done.5.refs_1_, f32[256,256]{1,0:T(8,128)S(1)} %get-tuple-element.26.refs_2_, bf16[384,128]{1,0:T(8,128)(2,1)S(1)} %get-tuple-element.27.refs_3_, ...), custom_call_target="tpu_custom_call" | custom-call | tf_op jit(solution)/shard_map/pallas_call | solution.py:510
  14.7 0.0 collective-permute-done.7.refs_4_
  14.8 1.9 %shard_map.43 = (f32[4,2,576,128]{3,2,1,0:T(8,128)S(1)}, f32[4,768,128]{2,1,0:T(8,128)S(1)}, f32[1,8,4,8,128]{4,3,2,1,0:T(8,128)S(1)}) custom-call(bf16[256,2176]{1,0:T(8,128)(2,1)S(1)} %get-tuple-element.24.refs_0_, bf16[4,56,16,128]{3,2,1,0:T(8,128)(2,1)S(1)} %get-tuple-element.30.refs_1_, f32[4,2,576,128]{3,2,1,0:T(8,128)S(1)} %shard_map.42.refs_2_, ...), custom_call_target="tpu_custom_call" | custom-call | flops 1711276032 | bytes 1048576 | tf_op jit(solution)/shard_map/pallas_call | solution.py:527
  16.6 0.0 collective-permute-done.3.refs_0_
  16.7 0.0 collective-permute-done.4.refs_1_
  16.7 1.7 %shard_map.44 = (f32[8,4,24,128]{3,2,1,0:T(8,128)}, f32[4,768,128]{2,1,0:T(8,128)S(1)}) custom-call(f32[64,128]{1,0:T(8,128)S(1)} %collective-permute-done.3.refs_0_, f32[64,128]{1,0:T(8,128)S(1)} %collective-permute-done.4.refs_1_, s32[1,4]{1,0:T(1,128)S(1)} %bitcast.5, ...), custom_call_target="tpu_custom_call", output_to_operand_aliasing={{1}: (6, {})} | custom-call | tf_op jit(solution)/shard_map/pallas_call | solution.py:542
  (2 shorter events, 0.0 us)
Async XLA Ops:
  0.0 6.9 %collective-permute-start = (f32[384,128]{1,0:T(8,128)}, f32[384,128]{1,0:T(8,128)S(1)}, u32[]{:S(2)}, u32[]{:S(2)}) collective-permute-start(f32[384,128]{1,0:T(8,128)} %bitcast.6), channel_id=1, source_target_pairs={{0,4},{1,5},{4,0},{5,1},{8,9},{9,8},{12,13},{13,12},{2,6},{3,7},{6... | collective-permute-start | bytes 589832 | tf_op jit(solution)/shard_map/ppermute | solution.py:444
  2.1 4.8 %collective-permute-start.1 = (f32[384,128]{1,0:T(8,128)}, f32[384,128]{1,0:T(8,128)S(1)}, u32[]{:S(2)}, u32[]{:S(2)}) collective-permute-start(f32[384,128]{1,0:T(8,128)} %bitcast.7), channel_id=1, source_target_pairs={{0,1},{1,0},{4,8},{5,9},{8,4},{9,5},{12,13},{13,12},{2,3},{3,2},{6... | collective-permute-start | bytes 589832 | tf_op jit(solution)/shard_map/ppermute | solution.py:445
  3.1 3.9 %collective-permute-start.2 = (f32[384,128]{1,0:T(8,128)}, f32[384,128]{1,0:T(8,128)S(1)}, u32[]{:S(2)}, u32[]{:S(2)}) collective-permute-start(f32[384,128]{1,0:T(8,128)} %bitcast.8), channel_id=1, source_target_pairs={{0,1},{1,0},{4,5},{5,4},{8,12},{9,13},{12,8},{13,9},{2,3},{3,2},{6... | collective-permute-start | bytes 589832 | tf_op jit(solution)/shard_map/ppermute | solution.py:446
  3.1 5.4 %collective-permute-start.6 = (f32[384,128]{1,0:T(8,128)}, f32[384,128]{1,0:T(8,128)S(1)}, u32[]{:S(2)}, u32[]{:S(2)}) collective-permute-start(f32[384,128]{1,0:T(8,128)} %bitcast.9), channel_id=1, source_target_pairs={{0,1},{1,0},{2,3},{3,2},{4,5},{5,4},{6,7},{7,6},{8,9},{9,8},{10,11... | collective-permute-start | bytes 589832 | tf_op jit(solution)/shard_map/ppermute | solution.py:425
  7.1 6.8 %collective-permute-start.5 = (f32[576,128]{1,0:T(8,128)S(1)}, f32[576,128]{1,0:T(8,128)S(1)}, u32[]{:S(2)}, u32[]{:S(2)}) collective-permute-start(f32[576,128]{1,0:T(8,128)S(1)} %get-tuple-element.25.refs_0_), channel_id=1, source_target_pairs={{0,1},{1,0},{2,3},{3,2},{4,5},{5,4},{6,7},{7,6},{8,9},{9,8},{10,11... | collective-permute-start | bytes 884744 | tf_op jit(solution)/shard_map/ppermute | solution.py:425
  9.2 5.6 %collective-permute-start.7 = (bf16[384,128]{1,0:T(8,128)(2,1)S(1)}, bf16[384,128]{1,0:T(8,128)(2,1)S(1)}, u32[]{:S(2)}, u32[]{:S(2)}) collective-permute-start(bf16[384,128]{1,0:T(8,128)(2,1)S(1)} %get-tuple-element.27.refs_3_), channel_id=1, source_target_pairs={{0,2},{2,0},{1,3},{3,1},{4,6},{6,4},{5,7},{7,5},{8,10},{10,8},{9,1... | collective-permute-start | bytes 294920 | tf_op jit(solution)/shard_map/ppermute | solution.py:481
  11.1 5.6 %collective-permute-start.3 = (f32[64,128]{1,0:T(8,128)S(1)}, f32[64,128]{1,0:T(8,128)S(1)}, u32[]{:S(2)}, u32[]{:S(2)}) collective-permute-start(f32[64,128]{1,0:T(8,128)S(1)} %get-tuple-element.22), channel_id=1, source_target_pairs={{0,2},{2,0},{1,3},{3,1},{4,6},{6,4},{5,7},{7,5},{8,10},{10,8},{9,1... | collective-permute-start | bytes 98312 | tf_op jit(solution)/shard_map/ppermute | solution.py:505
  11.2 5.4 %collective-permute-start.4 = (f32[64,128]{1,0:T(8,128)S(1)}, f32[64,128]{1,0:T(8,128)S(1)}, u32[]{:S(2)}, u32[]{:S(2)}) collective-permute-start(f32[64,128]{1,0:T(8,128)S(1)} %get-tuple-element.22), channel_id=1, source_target_pairs={{0,3},{1,2},{2,1},{3,0},{4,7},{5,6},{6,5},{7,4},{8,11},{9,10},{10,... | collective-permute-start | bytes 98312 | tf_op jit(solution)/shard_map/ppermute | solution.py:436
  13.1 1.7 %copy-start = (s32[4]{0:T(128)S(1)}, s32[4]{0:T(128)}, u32[]{:S(2)}) copy-start(s32[4]{0:T(128)} %param.5) | copy-start | bytes 52

commit v7 on v6

--- a/solution.py
+++ b/solution.py
@@ -15,6 +15,7 @@
 LANES = 128
 VMEM = pltpu.VMEM
 PHASES = 3
+END_LANES = 16
 
 
 def pairs(count, first, beside):
@@ -162,7 +163,11 @@
         smooth_ref[t * cols : (t + 1) * cols, :] = turn_ref[pl.ds(t, cols, stride=frames), :].astype(jnp.bfloat16)
 
 
-def columns_body(frames, cols, x_ref, a_ref, b_ref, c_ref, out_ref, edge_ref):
+def end_shifts(rows):
+    return [(END_LANES // 2 + END_LANES * n) % LANES for n in range(rows // 8)]
+
+
+def columns_body(frames, cols, x_ref, a_ref, b_ref, c_ref, out_ref, edge_ref, ends_ref):
     place, count = lax.axis_index("space"), lax.axis_size("space")
     phase = lax.rem(place, PHASES)
     lowest, highest = place > 0, place < count - 1
@@ -192,6 +197,11 @@
                     edge_ref[slot * frames : (slot + 1) * frames, :] = value
                 out_ref[order * frames : (order + 1) * frames, :] = value
                 order += 1
+    spot = lax.broadcasted_iota(jnp.int32, ends_ref.shape, 1)
+    ends = jnp.zeros(ends_ref.shape, jnp.float32)
+    for n, shift in enumerate(end_shifts(edge_ref.shape[0])):
+        ends = jnp.where(spot // END_LANES == n, pltpu.roll(edge_ref[8 * n : 8 * n + 8, :], shift, 1), ends)
+    ends_ref[...] = ends
 
 
 def placed(frames, cols, edges):
@@ -277,9 +287,9 @@
                     out_ref[j, g, at : at + frames, :] = found[row : row + frames, g * LANES : (g + 1) * LANES]
 
 
-def sums_body(frames, cols, table_ref, tiles_ref, inner_ref, out_ref):
+def sums_body(frames, cols, blocks, table_ref, tiles_ref, inner_ref, out_ref):
     tile_count, groups, pitch = out_ref.shape[0], out_ref.shape[1], frames + 8
-    for block in range(cols // 8):
+    for block in blocks:
         begin, end = inner_span(cols, block)
         chosen = [p for p in range(RMAX + 1) if not begin <= p < end]
         start = 8 * block
@@ -345,11 +355,14 @@
             value = jnp.where(begun, value, 0.0)
         for j in range(LANES // TILE):
             spread_ref[j, half * rows : (half + 1) * rows, :] = value[:, j * LANES : (j + 1) * LANES]
-    sums_body(frames, cols, table_ref, tiles_ref, inner_ref, out_ref)
+    last = cols // 8 - 1
+    sums_body(frames, cols, range(1, last), table_ref, tiles_ref, inner_ref, out_ref)
     lags = read_lags(lag_ref)
     sources = [(out_ref, j) for j in range(out_ref.shape[0])]
+    sums_body(frames, cols, (0,), table_ref, tiles_ref, inner_ref, out_ref)
     for n in range(held_ref.shape[0]):
         correlate_block(frames, cols, n + 1, lags, sources, spread_ref, inverse_ref, total_ref, held_ref.at[n])
+    sums_body(frames, cols, (last,), table_ref, tiles_ref, inner_ref, out_ref)
 
 
 def correlate_body(
@@ -367,7 +380,12 @@
         send(middle_ref.at[n], n + 1).start()
     tile_count = LANES // TILE
     begun = lax.axis_index("tm") > 0
-    side = beside(low_ref[...], None if high_ref is None else high_ref[...])
+    shifts = end_shifts(edge_ref.shape[0])
+
+    def apart(ends_ref):
+        return jnp.concatenate([pltpu.roll(ends_ref[...], LANES - shift, 1) for shift in shifts], axis=0)
+
+    side = beside(apart(low_ref), None if high_ref is None else apart(high_ref))
     place, count = lax.axis_index("row"), lax.axis_size("row")
     spot = lax.broadcasted_iota(jnp.int32, side.shape, 1)
     halo = spot < LANES // 2
@@ -483,7 +501,7 @@
     table, inverse = vmem_call(
         table_body,
         [shape((radii * TILE, depth), bf16), shape((radii, LANES), f32)],
-        scratch=[VMEM((offsets + 1, radii, LANES), f32), VMEM(((offsets + 1) // 2 * radii, LANES), f32)],
+        scratch=[VMEM((offsets + 1, radii, LANES), f32), VMEM(((offsets + 1) // 2 * radii + TILE, LANES), f32)],
     )(masks)
 
     sums = shape((tile_count, groups, cols * (frames + 8), LANES), f32)
@@ -496,12 +514,14 @@
     def columns(*refs):
         columns_body(frames, cols, *refs)
 
-    blurred, edges = vmem_call(
-        columns, [shape((2 * edge * frames, rows), f32), shape((2 * REACH * frames, rows), f32)], inputs=4
+    blurred, edges, ends = vmem_call(
+        columns,
+        [shape((2 * edge * frames, rows), f32), shape((2 * REACH * frames, rows), f32), shape((8, LANES), f32)],
+        inputs=4,
     )(held, one, two, three)
 
     sides = across(blurred)
-    far = across_later(edges)
+    far = across_later(ends)
     edges = lax.ppermute(edges, "tm", later)
 
     def windows(*refs):

time: 18.5 us -> 21 us (1.14)
  the two profiles are of different devices: /device:TPU:1 before, /device:TPU:0 now
where the time goes in v7:
time: 21 us; the launch traced here: 20.9 us
  starting transfers between devices  9.74 us (46%)
  Pallas kernels  7.48 us (36%)
  waiting for transfers between devices  3.55 us (17%)
    ppermute x1, starting transfers between devices, local(): one = lax.ppermute(flat, ('space', 'row'), pairs(count, 0, row_count))  5.69 us
    ppermute x1, waiting for transfers between devices, local(): one = lax.ppermute(flat, ('space', 'row'), pairs(count, 0, row_count))  3.53 us
    pallas_call x1, Pallas kernels, local(): vmem_call(products, [sums, shape((tile_count, 2 * frames * cols, LANES),...  1.76 us
    pallas_call x1, Pallas kernels, local(): vmem_call(correlate, [shape((radii, lag_count, cols, rows), f32), shape(s...  1.69 us
    ppermute x1, starting transfers between devices, local(): earlier = lax.ppermute(smooth, 'tm', later)  1.56 us
    ppermute x1, starting transfers between devices, local(): edges = lax.ppermute(edges, 'tm', later)  1.49 us
    pallas_call x1, Pallas kernels, local(): vmem_call(prepare_body, [shape((2 * LANES, 2 * LANES), f32), shape((frame...  1.02 us
    pallas_call x1, Pallas kernels, local(): vmem_call(windows, [shape((tile_count, wide, frames, LANES), bf16), shape...  0.82 us
  transfers between devices with their start and end apart: 8, of which 1 were waited for; matrix products, arithmetic and copies ran while one was open for 0% of the time, Pallas kernels for 28%

profile of v7, /device:TPU:0, one launch (start us, length us, event | category | flops | bytes accessed | tf_op | source)
XLA Modules:
  0.0 20.9 jit_solution(6578084071556218570)
XLA Ops:
  0.0 0.5 %collective-permute-start.2 = (f32[384,128]{1,0:T(8,128)}, f32[384,128]{1,0:T(8,128)S(1)}, u32[]{:S(2)}, u32[]{:S(2)}) collective-permute-start(f32[384,128]{1,0:T(8,128)} %bitcast.6), channel_id=1, source_target_pairs={{0,1},{1,0},{4,5},{5,4},{8,12},{9,13},{12,8},{13,9},{2,3},{3,2},{6... | collective-permute-start | bytes 589832 | tf_op jit(solution)/shard_map/ppermute | solution.py:464
  0.5 0.0 collective-permute-start.1
  0.5 5.7 %collective-permute-start = (f32[384,128]{1,0:T(8,128)}, f32[384,128]{1,0:T(8,128)S(1)}, u32[]{:S(2)}, u32[]{:S(2)}) collective-permute-start(f32[384,128]{1,0:T(8,128)} %bitcast.8), channel_id=1, source_target_pairs={{0,4},{1,5},{4,0},{5,1},{8,9},{9,8},{12,13},{13,12},{2,6},{3,7},{6... | collective-permute-start | bytes 589832 | tf_op jit(solution)/shard_map/ppermute | solution.py:462
  6.2 0.0 collective-permute-start.6
  6.2 1.0 %shard_map.37 = (f32[256,256]{1,0:T(8,128)S(1)}, f32[384,128]{1,0:T(8,128)S(1)}, s32[33,8,33]{2,1,0:T(8,128)S(1)}) custom-call(s32[33,8,33]{2,1,0:T(8,128)} %bitcast.11, f32[384,128]{1,0:T(8,128)} %bitcast.10), custom_call_target="tpu_custom_call" | custom-call | tf_op jit(solution)/shard_map/pallas_call | solution.py:469
  7.2 0.0 collective-permute-done.2.refs_3_
  7.2 0.0 collective-permute-done.1.refs_2_
  7.3 3.5 %collective-permute-done.refs_1_ = f32[384,128]{1,0:T(8,128)S(1)} collective-permute-done((f32[384,128]{1,0:T(8,128)}, f32[384,128]{1,0:T(8,128)S(1)}, u32[]{:S(2)}, u32[]{:S(2)}) %collective-permute-start) | collective-permute-done | bytes 196640 | tf_op jit(solution)/shard_map/ppermute | solution.py:462
  10.8 0.2 %shard_map.38 = (f32[576,128]{1,0:T(8,128)S(1)}, f32[64,128]{1,0:T(8,128)S(1)}, f32[8,128]{1,0:T(8,128)S(1)}) custom-call(f32[384,128]{1,0:T(8,128)S(1)} %get-tuple-element.22.refs_0_, f32[384,128]{1,0:T(8,128)S(1)} %collective-permute-done.refs_1_, f32[384,128]{1,0:T(8,128)S(1)} %collective-permute-done.1.refs_2_, f32[384,128]{1,0:T(8,128)S(1)} %collective-permute-done.2.refs_3_), custom_call_target="tpu_custom_call" | custom-call | tf_op jit(solution)/shard_map/pallas_call | solution.py:517
  11.0 0.1 collective-permute-start.5
  11.1 0.0 collective-permute-done.6.refs_1_
  11.1 0.7 %shard_map.40 = (bf16[384,128]{1,0:T(8,128)(2,1)S(1)}, bf16[4,19,16,128]{3,2,1,0:T(8,128)(2,1)S(1)}, f32[2,2,16,128]{3,2,1,0:T(8,128)S(1)}) custom-call(f32[384,128]{1,0:T(8,128)S(1)} %get-tuple-element.22.refs_0_, f32[384,128]{1,0:T(8,128)S(1)} %collective-permute-done.6.refs_1_, f32[256,256]{1,0:T(8,128)S(1)} %get-tuple-element.28.refs_2_), custom_call_target="tpu_custom_call" | custom-call | tf_op jit(solution)/shard_map/pallas_call | solution.py:484
  11.8 1.6 %collective-permute-start.7 = (bf16[384,128]{1,0:T(8,128)(2,1)S(1)}, bf16[384,128]{1,0:T(8,128)(2,1)S(1)}, u32[]{:S(2)}, u32[]{:S(2)}) collective-permute-start(bf16[384,128]{1,0:T(8,128)(2,1)S(1)} %get-tuple-element.29.refs_3_), channel_id=1, source_target_pairs={{0,2},{2,0},{1,3},{3,1},{4,6},{6,4},{5,7},{7,5},{8,10},{10,8},{9,1... | collective-permute-start | bytes 294920 | tf_op jit(solution)/shard_map/ppermute | solution.py:499
  13.4 0.5 %shard_map.39 = (bf16[256,2176]{1,0:T(8,128)(2,1)S(1)}, f32[8,128]{1,0:T(8,128)S(1)}) custom-call(s32[33,8,33]{2,1,0:T(8,128)S(1)} %get-tuple-element.25.masks_ref), custom_call_target="tpu_custom_call" | custom-call | tf_op jit(solution)/shard_map/pallas_call | solution.py:501
  13.8 0.4 %collective-permute-start.4 = (f32[8,128]{1,0:T(8,128)S(1)}, f32[8,128]{1,0:T(8,128)S(1)}, u32[]{:S(2)}, u32[]{:S(2)}) collective-permute-start(f32[8,128]{1,0:T(8,128)S(1)} %get-tuple-element.24), channel_id=1, source_target_pairs={{0,3},{1,2},{2,1},{3,0},{4,7},{5,6},{6,5},{7,4},{8,11},{9,10},{10,... | collective-permute-start | bytes 12296 | tf_op jit(solution)/shard_map/ppermute | solution.py:454
  14.3 1.5 %collective-permute-start.3 = (f32[64,128]{1,0:T(8,128)S(1)}, f32[64,128]{1,0:T(8,128)S(1)}, u32[]{:S(2)}, u32[]{:S(2)}) collective-permute-start(f32[64,128]{1,0:T(8,128)S(1)} %get-tuple-element.23), channel_id=1, source_target_pairs={{0,2},{2,0},{1,3},{3,1},{4,6},{6,4},{5,7},{7,5},{8,10},{10,8},{9,1... | collective-permute-start | bytes 98312 | tf_op jit(solution)/shard_map/ppermute | solution.py:525
  15.7 0.8 %shard_map.42.refs_2_ = f32[4,2,576,128]{3,2,1,0:T(8,128)S(1)} custom-call(bf16[256,2176]{1,0:T(8,128)(2,1)S(1)} %get-tuple-element.26.refs_0_, bf16[4,19,16,128]{3,2,1,0:T(8,128)(2,1)S(1)} %get-tuple-element.30.refs_4_.refs_1_), custom_call_target="tpu_custom_call" | custom-call | tf_op jit(solution)/shard_map/pallas_call | solution.py:512
  16.6 0.0 collective-permute-done.5.refs_1_
  16.6 0.8 %shard_map.41 = (bf16[4,56,16,128]{3,2,1,0:T(8,128)(2,1)S(1)}, bf16[384,128]{1,0:T(8,128)(2,1)S(1)}) custom-call(f32[576,128]{1,0:T(8,128)S(1)} %get-tuple-element.27.refs_0_, f32[576,128]{1,0:T(8,128)S(1)} %collective-permute-done.5.refs_1_, f32[256,256]{1,0:T(8,128)S(1)} %get-tuple-element.28.refs_2_, bf16[384,128]{1,0:T(8,128)(2,1)S(1)} %get-tuple-element.29.refs_3_, ...), custom_call_target="tpu_custom_call" | custom-call | tf_op jit(solution)/shard_map/pallas_call | solution.py:530
  17.4 0.0 collective-permute-done.7.refs_4_
  17.4 1.8 %shard_map.43 = (f32[4,2,576,128]{3,2,1,0:T(8,128)S(1)}, f32[4,768,128]{2,1,0:T(8,128)S(1)}, f32[1,8,4,8,128]{4,3,2,1,0:T(8,128)S(1)}) custom-call(bf16[256,2176]{1,0:T(8,128)(2,1)S(1)} %get-tuple-element.26.refs_0_, bf16[4,56,16,128]{3,2,1,0:T(8,128)(2,1)S(1)} %get-tuple-element.32.refs_1_, f32[4,2,576,128]{3,2,1,0:T(8,128)S(1)} %shard_map.42.refs_2_, ...), custom_call_target="tpu_custom_call" | custom-call | flops 1711276032 | bytes 1048576 | tf_op jit(solution)/shard_map/pallas_call | solution.py:547
  19.2 0.0 collective-permute-done.4.refs_1_
  19.2 0.0 collective-permute-done.3.refs_0_
  19.2 1.7 %shard_map.44 = (f32[8,4,24,128]{3,2,1,0:T(8,128)}, f32[4,768,128]{2,1,0:T(8,128)S(1)}) custom-call(f32[64,128]{1,0:T(8,128)S(1)} %collective-permute-done.3.refs_0_, f32[8,128]{1,0:T(8,128)S(1)} %collective-permute-done.4.refs_1_, s32[1,4]{1,0:T(1,128)S(1)} %bitcast.5, ...), custom_call_target="tpu_custom_call", output_to_operand_aliasing={{1}: (6, {})} | custom-call | tf_op jit(solution)/shard_map/pallas_call | solution.py:562
  (2 shorter events, 0.0 us)
Async XLA Ops:
  0.0 7.2 %collective-permute-start.2 = (f32[384,128]{1,0:T(8,128)}, f32[384,128]{1,0:T(8,128)S(1)}, u32[]{:S(2)}, u32[]{:S(2)}) collective-permute-start(f32[384,128]{1,0:T(8,128)} %bitcast.6), channel_id=1, source_target_pairs={{0,1},{1,0},{4,5},{5,4},{8,12},{9,13},{12,8},{13,9},{2,3},{3,2},{6... | collective-permute-start | bytes 589832 | tf_op jit(solution)/shard_map/ppermute | solution.py:464
  0.5 6.8 %collective-permute-start.1 = (f32[384,128]{1,0:T(8,128)}, f32[384,128]{1,0:T(8,128)S(1)}, u32[]{:S(2)}, u32[]{:S(2)}) collective-permute-start(f32[384,128]{1,0:T(8,128)} %bitcast.7), channel_id=1, source_target_pairs={{0,1},{1,0},{4,8},{5,9},{8,4},{9,5},{12,13},{13,12},{2,3},{3,2},{6... | collective-permute-start | bytes 589832 | tf_op jit(solution)/shard_map/ppermute | solution.py:463
  0.5 10.3 %collective-permute-start = (f32[384,128]{1,0:T(8,128)}, f32[384,128]{1,0:T(8,128)S(1)}, u32[]{:S(2)}, u32[]{:S(2)}) collective-permute-start(f32[384,128]{1,0:T(8,128)} %bitcast.8), channel_id=1, source_target_pairs={{0,4},{1,5},{4,0},{5,1},{8,9},{9,8},{12,13},{13,12},{2,6},{3,7},{6... | collective-permute-start | bytes 589832 | tf_op jit(solution)/shard_map/ppermute | solution.py:462
  6.2 4.9 %collective-permute-start.6 = (f32[384,128]{1,0:T(8,128)}, f32[384,128]{1,0:T(8,128)S(1)}, u32[]{:S(2)}, u32[]{:S(2)}) collective-permute-start(f32[384,128]{1,0:T(8,128)} %bitcast.9), channel_id=1, source_target_pairs={{0,1},{1,0},{2,3},{3,2},{4,5},{5,4},{6,7},{7,6},{8,9},{9,8},{10,11... | collective-permute-start | bytes 589832 | tf_op jit(solution)/shard_map/ppermute | solution.py:443
  11.0 5.5 %collective-permute-start.5 = (f32[576,128]{1,0:T(8,128)S(1)}, f32[576,128]{1,0:T(8,128)S(1)}, u32[]{:S(2)}, u32[]{:S(2)}) collective-permute-start(f32[576,128]{1,0:T(8,128)S(1)} %get-tuple-element.27.refs_0_), channel_id=1, source_target_pairs={{0,1},{1,0},{2,3},{3,2},{4,5},{5,4},{6,7},{7,6},{8,9},{9,8},{10,11... | collective-permute-start | bytes 884744 | tf_op jit(solution)/shard_map/ppermute | solution.py:443
  11.8 5.6 %collective-permute-start.7 = (bf16[384,128]{1,0:T(8,128)(2,1)S(1)}, bf16[384,128]{1,0:T(8,128)(2,1)S(1)}, u32[]{:S(2)}, u32[]{:S(2)}) collective-permute-start(bf16[384,128]{1,0:T(8,128)(2,1)S(1)} %get-tuple-element.29.refs_3_), channel_id=1, source_target_pairs={{0,2},{2,0},{1,3},{3,1},{4,6},{6,4},{5,7},{7,5},{8,10},{10,8},{9,1... | collective-permute-start | bytes 294920 | tf_op jit(solution)/shard_map/ppermute | solution.py:499
  13.8 5.3 %collective-permute-start.4 = (f32[8,128]{1,0:T(8,128)S(1)}, f32[8,128]{1,0:T(8,128)S(1)}, u32[]{:S(2)}, u32[]{:S(2)}) collective-permute-start(f32[8,128]{1,0:T(8,128)S(1)} %get-tuple-element.24), channel_id=1, source_target_pairs={{0,3},{1,2},{2,1},{3,0},{4,7},{5,6},{6,5},{7,4},{8,11},{9,10},{10,... | collective-permute-start | bytes 12296 | tf_op jit(solution)/shard_map/ppermute | solution.py:454
  14.3 4.9 %collective-permute-start.3 = (f32[64,128]{1,0:T(8,128)S(1)}, f32[64,128]{1,0:T(8,128)S(1)}, u32[]{:S(2)}, u32[]{:S(2)}) collective-permute-start(f32[64,128]{1,0:T(8,128)S(1)} %get-tuple-element.23), channel_id=1, source_target_pairs={{0,2},{2,0},{1,3},{3,1},{4,6},{6,4},{5,7},{7,5},{8,10},{10,8},{9,1... | collective-permute-start | bytes 98312 | tf_op jit(solution)/shard_map/ppermute | solution.py:525
  15.7 1.7 %copy-start = (s32[4]{0:T(128)S(1)}, s32[4]{0:T(128)}, u32[]{:S(2)}) copy-start(s32[4]{0:T(128)} %param.5) | copy-start | bytes 52

commit v8 on v7

--- a/solution.py
+++ b/solution.py
@@ -156,8 +156,8 @@
                 rim_ref[0 if c == 0 else 1, n] = value[n]
         if before is not None:
             for n in range(2):
-                pairs_ref[2 * n, c - 1] = jnp.where(first, before[n][0], now[n][1]).astype(jnp.bfloat16)
-                pairs_ref[2 * n + 1, c - 1] = jnp.where(first, before[n][1], now[n][0]).astype(jnp.bfloat16)
+                pairs_ref[2 * n, RMAX + REACH + c - 1] = jnp.where(first, before[n][0], now[n][1]).astype(jnp.bfloat16)
+                pairs_ref[2 * n + 1, RMAX + REACH + c - 1] = jnp.where(first, before[n][1], now[n][0]).astype(jnp.bfloat16)
         before = now
     for t in range(frames):
         smooth_ref[t * cols : (t + 1) * cols, :] = turn_ref[pl.ds(t, cols, stride=frames), :].astype(jnp.bfloat16)
@@ -252,8 +252,7 @@
                     tiles_ref[2 * n, c - 1] = low.astype(jnp.bfloat16)
                     tiles_ref[2 * n + 1, c - 1] = high.astype(jnp.bfloat16)
             before = now
-    for j in range(pairs_ref.shape[0]):
-        tiles_ref[j, edge : wide - edge - 1] = pairs_ref[j]
+    del pairs_ref
     rows = slice(RMAX * frames, (RMAX + 2 * REACH) * frames)
     edges = own_lanes(found_ref[rows, 0:LANES], found_ref[rows, LANES : 2 * LANES]).astype(jnp.bfloat16)
     whole_ref[...] = smooth_ref[...] + placed(frames, cols, edges)
@@ -274,7 +273,7 @@
     tile_count, groups, pitch = out_ref.shape[0], out_ref.shape[1], frames + 8
     for block in range(cols // 8):
         begin, end = inner_span(cols, block)
-        start = 8 * block - RMAX - REACH
+        start = 8 * block
         pieces = [
             pairs_ref[:, start + 2 * p : start + 2 * p + 8].reshape(tile_count * 8 * frames, LANES)
             for p in range(begin, end)
@@ -485,7 +484,7 @@
         own,
         [
             shape((frames * cols, rows), bf16),
-            shape((tile_count, inner - 1, frames, LANES), bf16),
+            shape((tile_count, wide, frames, LANES), bf16),
             shape((2, 2, frames, LANES), f32),
         ],
         scratch=[
@@ -532,6 +531,7 @@
         [shape((tile_count, wide, frames, LANES), bf16), shape((frames * cols, rows), bf16)],
         scratch=[VMEM((2 * edge * frames, 2 * LANES), f32)],
         inputs=5 + len(sides),
+        aliases={3 + len(sides): 0},
     )(blurred, *sides, blur, smooth, inner_pairs, rim)
 
     blocks = cols // 8

time: 21 us -> 21 us (level)
  no operation moved by 1% of the time
where the time goes in v8:
time: 21 us; the launch traced here: 20.9 us
  starting transfers between devices  9.74 us (46%)
  Pallas kernels  7.45 us (35%)
  waiting for transfers between devices  3.55 us (17%)
    ppermute x1, starting transfers between devices, local(): one = lax.ppermute(flat, ('space', 'row'), pairs(count, 0, row_count))  5.69 us
    ppermute x1, waiting for transfers between devices, local(): one = lax.ppermute(flat, ('space', 'row'), pairs(count, 0, row_count))  3.53 us
    pallas_call x1, Pallas kernels, local(): vmem_call(products, [sums, shape((tile_count, 2 * frames * cols, LANES),...  1.74 us
    pallas_call x1, Pallas kernels, local(): vmem_call(correlate, [shape((radii, lag_count, cols, rows), f32), shape(s...  1.69 us
    ppermute x1, starting transfers between devices, local(): earlier = lax.ppermute(smooth, 'tm', later)  1.56 us
    ppermute x1, starting transfers between devices, local(): edges = lax.ppermute(edges, 'tm', later)  1.49 us
    pallas_call x1, Pallas kernels, local(): vmem_call(prepare_body, [shape((2 * LANES, 2 * LANES), f32), shape((frame...  1.02 us
    pallas_call x1, Pallas kernels, local(): vmem_call(windows, [shape((tile_count, wide, frames, LANES), bf16), shape...  0.82 us
  transfers between devices with their start and end apart: 8, of which 1 were waited for; matrix products, arithmetic and copies ran while one was open for 0% of the time, Pallas kernels for 28%

profile of v8, /device:TPU:0, one launch (start us, length us, event | category | flops | bytes accessed | tf_op | source)
XLA Modules:
  0.0 20.9 jit_solution(16091799198488516785)
XLA Ops:
  0.0 0.5 %collective-permute-start.2 = (f32[384,128]{1,0:T(8,128)}, f32[384,128]{1,0:T(8,128)S(1)}, u32[]{:S(2)}, u32[]{:S(2)}) collective-permute-start(f32[384,128]{1,0:T(8,128)} %bitcast.6), channel_id=1, source_target_pairs={{0,1},{1,0},{4,5},{5,4},{8,12},{9,13},{12,8},{13,9},{2,3},{3,2},{6... | collective-permute-start | bytes 589832 | tf_op jit(solution)/shard_map/ppermute | solution.py:463
  0.5 0.0 collective-permute-start.1
  0.5 5.7 %collective-permute-start = (f32[384,128]{1,0:T(8,128)}, f32[384,128]{1,0:T(8,128)S(1)}, u32[]{:S(2)}, u32[]{:S(2)}) collective-permute-start(f32[384,128]{1,0:T(8,128)} %bitcast.8), channel_id=1, source_target_pairs={{0,4},{1,5},{4,0},{5,1},{8,9},{9,8},{12,13},{13,12},{2,6},{3,7},{6... | collective-permute-start | bytes 589832 | tf_op jit(solution)/shard_map/ppermute | solution.py:461
  6.2 0.0 collective-permute-start.6
  6.2 1.0 %shard_map.37 = (f32[256,256]{1,0:T(8,128)S(1)}, f32[384,128]{1,0:T(8,128)S(1)}, s32[33,8,33]{2,1,0:T(8,128)S(1)}) custom-call(s32[33,8,33]{2,1,0:T(8,128)} %bitcast.11, f32[384,128]{1,0:T(8,128)} %bitcast.10), custom_call_target="tpu_custom_call" | custom-call | tf_op jit(solution)/shard_map/pallas_call | solution.py:468
  7.2 0.0 collective-permute-done.2.refs_3_
  7.3 3.5 %collective-permute-done.refs_1_ = f32[384,128]{1,0:T(8,128)S(1)} collective-permute-done((f32[384,128]{1,0:T(8,128)}, f32[384,128]{1,0:T(8,128)S(1)}, u32[]{:S(2)}, u32[]{:S(2)}) %collective-permute-start) | collective-permute-done | bytes 196640 | tf_op jit(solution)/shard_map/ppermute | solution.py:461
  10.8 0.2 %shard_map.38 = (f32[576,128]{1,0:T(8,128)S(1)}, f32[64,128]{1,0:T(8,128)S(1)}, f32[8,128]{1,0:T(8,128)S(1)}) custom-call(f32[384,128]{1,0:T(8,128)S(1)} %get-tuple-element.22.refs_0_, f32[384,128]{1,0:T(8,128)S(1)} %collective-permute-done.refs_1_, f32[384,128]{1,0:T(8,128)S(1)} %collective-permute-done.1.refs_2_, f32[384,128]{1,0:T(8,128)S(1)} %collective-permute-done.2.refs_3_), custom_call_target="tpu_custom_call" | custom-call | tf_op jit(solution)/shard_map/pallas_call | solution.py:516
  11.0 0.1 collective-permute-start.5
  11.1 0.0 collective-permute-done.6.refs_1_
  11.1 0.7 %shard_map.40 = (bf16[384,128]{1,0:T(8,128)(2,1)S(1)}, bf16[4,56,16,128]{3,2,1,0:T(8,128)(2,1)S(1)}, f32[2,2,16,128]{3,2,1,0:T(8,128)S(1)}) custom-call(f32[384,128]{1,0:T(8,128)S(1)} %get-tuple-element.22.refs_0_, f32[384,128]{1,0:T(8,128)S(1)} %collective-permute-done.6.refs_1_, f32[256,256]{1,0:T(8,128)S(1)} %get-tuple-element.28.refs_2_), custom_call_target="tpu_custom_call" | custom-call | tf_op jit(solution)/shard_map/pallas_call | solution.py:483
  11.8 1.6 %collective-permute-start.7 = (bf16[384,128]{1,0:T(8,128)(2,1)S(1)}, bf16[384,128]{1,0:T(8,128)(2,1)S(1)}, u32[]{:S(2)}, u32[]{:S(2)}) collective-permute-start(bf16[384,128]{1,0:T(8,128)(2,1)S(1)} %get-tuple-element.29.refs_3_), channel_id=1, source_target_pairs={{0,2},{2,0},{1,3},{3,1},{4,6},{6,4},{5,7},{7,5},{8,10},{10,8},{9,1... | collective-permute-start | bytes 294920 | tf_op jit(solution)/shard_map/ppermute | solution.py:498
  13.4 0.5 %shard_map.39 = (bf16[256,2176]{1,0:T(8,128)(2,1)S(1)}, f32[8,128]{1,0:T(8,128)S(1)}) custom-call(s32[33,8,33]{2,1,0:T(8,128)S(1)} %get-tuple-element.25.masks_ref), custom_call_target="tpu_custom_call" | custom-call | tf_op jit(solution)/shard_map/pallas_call | solution.py:500
  13.8 0.4 %collective-permute-start.4 = (f32[8,128]{1,0:T(8,128)S(1)}, f32[8,128]{1,0:T(8,128)S(1)}, u32[]{:S(2)}, u32[]{:S(2)}) collective-permute-start(f32[8,128]{1,0:T(8,128)S(1)} %get-tuple-element.24), channel_id=1, source_target_pairs={{0,3},{1,2},{2,1},{3,0},{4,7},{5,6},{6,5},{7,4},{8,11},{9,10},{10,... | collective-permute-start | bytes 12296 | tf_op jit(solution)/shard_map/ppermute | solution.py:453
  14.3 1.5 %collective-permute-start.3 = (f32[64,128]{1,0:T(8,128)S(1)}, f32[64,128]{1,0:T(8,128)S(1)}, u32[]{:S(2)}, u32[]{:S(2)}) collective-permute-start(f32[64,128]{1,0:T(8,128)S(1)} %get-tuple-element.23), channel_id=1, source_target_pairs={{0,2},{2,0},{1,3},{3,1},{4,6},{6,4},{5,7},{7,5},{8,10},{10,8},{9,1... | collective-permute-start | bytes 98312 | tf_op jit(solution)/shard_map/ppermute | solution.py:524
  15.7 0.8 %shard_map.42.refs_2_ = f32[4,2,576,128]{3,2,1,0:T(8,128)S(1)} custom-call(bf16[256,2176]{1,0:T(8,128)(2,1)S(1)} %get-tuple-element.26.refs_0_, bf16[4,56,16,128]{3,2,1,0:T(8,128)(2,1)S(1)} %get-tuple-element.30.refs_4_.refs_1_), custom_call_target="tpu_custom_call" | custom-call | tf_op jit(solution)/shard_map/pallas_call | solution.py:511
  16.6 0.0 copy-start
  16.6 0.0 collective-permute-done.5.refs_1_
  16.6 0.8 %shard_map.41 = (bf16[4,56,16,128]{3,2,1,0:T(8,128)(2,1)S(1)}, bf16[384,128]{1,0:T(8,128)(2,1)S(1)}) custom-call(f32[576,128]{1,0:T(8,128)S(1)} %get-tuple-element.27.refs_0_, f32[576,128]{1,0:T(8,128)S(1)} %collective-permute-done.5.refs_1_, f32[256,256]{1,0:T(8,128)S(1)} %get-tuple-element.28.refs_2_, ...), custom_call_target="tpu_custom_call", output_to_operand_aliasing={{0}: (4, {})} | custom-call | tf_op jit(solution)/shard_map/pallas_call | solution.py:529
  17.4 0.0 collective-permute-done.7.refs_4_
  17.4 1.7 %shard_map.43 = (f32[4,2,576,128]{3,2,1,0:T(8,128)S(1)}, f32[4,768,128]{2,1,0:T(8,128)S(1)}, f32[1,8,4,8,128]{4,3,2,1,0:T(8,128)S(1)}) custom-call(bf16[256,2176]{1,0:T(8,128)(2,1)S(1)} %get-tuple-element.26.refs_0_, bf16[4,56,16,128]{3,2,1,0:T(8,128)(2,1)S(1)} %get-tuple-element.32.refs_1_, f32[4,2,576,128]{3,2,1,0:T(8,128)S(1)} %shard_map.42.refs_2_, ...), custom_call_target="tpu_custom_call" | custom-call | flops 1711276032 | bytes 1048576 | tf_op jit(solution)/shard_map/pallas_call | solution.py:547
  19.2 0.0 collective-permute-done.4.refs_1_
  19.2 0.0 collective-permute-done.3.refs_0_
  19.2 1.7 %shard_map.44 = (f32[8,4,24,128]{3,2,1,0:T(8,128)}, f32[4,768,128]{2,1,0:T(8,128)S(1)}) custom-call(f32[64,128]{1,0:T(8,128)S(1)} %collective-permute-done.3.refs_0_, f32[8,128]{1,0:T(8,128)S(1)} %collective-permute-done.4.refs_1_, s32[1,4]{1,0:T(1,128)S(1)} %bitcast.5, ...), custom_call_target="tpu_custom_call", output_to_operand_aliasing={{1}: (6, {})} | custom-call | tf_op jit(solution)/shard_map/pallas_call | solution.py:562
  (2 shorter events, 0.0 us)
Async XLA Ops:
  0.0 7.2 %collective-permute-start.2 = (f32[384,128]{1,0:T(8,128)}, f32[384,128]{1,0:T(8,128)S(1)}, u32[]{:S(2)}, u32[]{:S(2)}) collective-permute-start(f32[384,128]{1,0:T(8,128)} %bitcast.6), channel_id=1, source_target_pairs={{0,1},{1,0},{4,5},{5,4},{8,12},{9,13},{12,8},{13,9},{2,3},{3,2},{6... | collective-permute-start | bytes 589832 | tf_op jit(solution)/shard_map/ppermute | solution.py:463
  0.5 6.8 %collective-permute-start.1 = (f32[384,128]{1,0:T(8,128)}, f32[384,128]{1,0:T(8,128)S(1)}, u32[]{:S(2)}, u32[]{:S(2)}) collective-permute-start(f32[384,128]{1,0:T(8,128)} %bitcast.7), channel_id=1, source_target_pairs={{0,1},{1,0},{4,8},{5,9},{8,4},{9,5},{12,13},{13,12},{2,3},{3,2},{6... | collective-permute-start | bytes 589832 | tf_op jit(solution)/shard_map/ppermute | solution.py:462
  0.5 10.3 %collective-permute-start = (f32[384,128]{1,0:T(8,128)}, f32[384,128]{1,0:T(8,128)S(1)}, u32[]{:S(2)}, u32[]{:S(2)}) collective-permute-start(f32[384,128]{1,0:T(8,128)} %bitcast.8), channel_id=1, source_target_pairs={{0,4},{1,5},{4,0},{5,1},{8,9},{9,8},{12,13},{13,12},{2,6},{3,7},{6... | collective-permute-start | bytes 589832 | tf_op jit(solution)/shard_map/ppermute | solution.py:461
  6.2 4.9 %collective-permute-start.6 = (f32[384,128]{1,0:T(8,128)}, f32[384,128]{1,0:T(8,128)S(1)}, u32[]{:S(2)}, u32[]{:S(2)}) collective-permute-start(f32[384,128]{1,0:T(8,128)} %bitcast.9), channel_id=1, source_target_pairs={{0,1},{1,0},{2,3},{3,2},{4,5},{5,4},{6,7},{7,6},{8,9},{9,8},{10,11... | collective-permute-start | bytes 589832 | tf_op jit(solution)/shard_map/ppermute | solution.py:442
  11.0 5.6 %collective-permute-start.5 = (f32[576,128]{1,0:T(8,128)S(1)}, f32[576,128]{1,0:T(8,128)S(1)}, u32[]{:S(2)}, u32[]{:S(2)}) collective-permute-start(f32[576,128]{1,0:T(8,128)S(1)} %get-tuple-element.27.refs_0_), channel_id=1, source_target_pairs={{0,1},{1,0},{2,3},{3,2},{4,5},{5,4},{6,7},{7,6},{8,9},{9,8},{10,11... | collective-permute-start | bytes 884744 | tf_op jit(solution)/shard_map/ppermute | solution.py:442
  11.8 5.6 %collective-permute-start.7 = (bf16[384,128]{1,0:T(8,128)(2,1)S(1)}, bf16[384,128]{1,0:T(8,128)(2,1)S(1)}, u32[]{:S(2)}, u32[]{:S(2)}) collective-permute-start(bf16[384,128]{1,0:T(8,128)(2,1)S(1)} %get-tuple-element.29.refs_3_), channel_id=1, source_target_pairs={{0,2},{2,0},{1,3},{3,1},{4,6},{6,4},{5,7},{7,5},{8,10},{10,8},{9,1... | collective-permute-start | bytes 294920 | tf_op jit(solution)/shard_map/ppermute | solution.py:498
  13.8 5.3 %collective-permute-start.4 = (f32[8,128]{1,0:T(8,128)S(1)}, f32[8,128]{1,0:T(8,128)S(1)}, u32[]{:S(2)}, u32[]{:S(2)}) collective-permute-start(f32[8,128]{1,0:T(8,128)S(1)} %get-tuple-element.24), channel_id=1, source_target_pairs={{0,3},{1,2},{2,1},{3,0},{4,7},{5,6},{6,5},{7,4},{8,11},{9,10},{10,... | collective-permute-start | bytes 12296 | tf_op jit(solution)/shard_map/ppermute | solution.py:453
  14.3 4.9 %collective-permute-start.3 = (f32[64,128]{1,0:T(8,128)S(1)}, f32[64,128]{1,0:T(8,128)S(1)}, u32[]{:S(2)}, u32[]{:S(2)}) collective-permute-start(f32[64,128]{1,0:T(8,128)S(1)} %get-tuple-element.23), channel_id=1, source_target_pairs={{0,2},{2,0},{1,3},{3,1},{4,6},{6,4},{5,7},{7,5},{8,10},{10,8},{9,1... | collective-permute-start | bytes 98312 | tf_op jit(solution)/shard_map/ppermute | solution.py:524
  16.6 0.9 %copy-start = (s32[4]{0:T(128)S(1)}, s32[4]{0:T(128)}, u32[]{:S(2)}) copy-start(s32[4]{0:T(128)} %param.5) | copy-start | bytes 52
